TPU v7x, 256 devices: a whole 4x4x8 slice. The times are simulated.
256 devices in a mesh: tile: 64 (over z, y, core), cuts: 4 (over x).
Axes of the slice: x: 4, y: 4, z: 8, core: 2. Of those that a mesh axis runs over, the one named last changes fastest.
Arguments:
- transmission: float32 [4, 2, 16384, 1024], P('cuts', None, 'tile')
- probe: float32 [2, 256, 256], replicated, may hold values from -6 to 6
- prop_phase: float32 [256, 256], replicated, may hold values from -3.140625 to 3.140625
- row_off: int32 [64], P('tile'), may hold values from 0 to 255
- col_off: int32 [64], P('tile'), may hold values from 0 to 768
- measured: float32 [64, 256, 256], P('tile'), may hold values from 0 to 1.6
Outputs:
- obj_grad: float32 [4, 2, 16384, 1024], P('cuts', None, 'tile')
All inputs are finite; a program needn't handle non-finite values.
Results may differ from a plain program's by a relative error of at most 0.0003.
Values sent between devices are 32-bit elements; how exact they have to be, the bound alone decides.
A program may use at most 64 MiB of HBM per device.

v0:
```python
import jax
import jax.numpy as jnp
from jax import lax
from jax.sharding import PartitionSpec as P


def shifted(value, axis, by):
    devices = lax.axis_size(axis)
    pairs = [(i, i + by) for i in range(devices) if 0 <= i + by < devices]
    return lax.ppermute(value, axis, pairs)


def rotated(value, axis, by):
    devices = lax.axis_size(axis)
    pairs = [(i, (i + by) % devices) for i in range(devices)]
    return lax.ppermute(value, axis, pairs)


def dft_tables(length):
    index = lax.iota(jnp.int32, length)
    product = index[:, None] * index[None, :] % length
    angle = product.astype(jnp.float32) * (2.0 * jnp.pi / length)
    factor = 1.0 / jnp.sqrt(jnp.float32(length))
    return (jnp.cos(angle) * factor, jnp.sin(angle) * factor)


def halves(value):
    scaled = value * jnp.float32(65537.0)
    high = scaled - (scaled - value)
    low = value - high
    return high.astype(jnp.bfloat16), low.astype(jnp.bfloat16)


def stacked_tables(cosines, sines, direction):
    signed = sines * direction
    left = jnp.concatenate(
        [jnp.concatenate([cosines, -signed], axis=1), jnp.concatenate([signed, cosines], axis=1)],
        axis=0,
    )
    right = jnp.concatenate([cosines, signed], axis=1)
    left_high, left_low = halves(left)
    right_high, right_low = halves(right)
    left_split = jnp.concatenate([left_high, left_high, left_low], axis=1)
    right_split = jnp.concatenate([right_high, right_low, right_high], axis=0)
    return left_split, right_split


def split_dot(split_table, value, table_first):
    high, low = halves(value)
    if table_first:
        operand = jnp.concatenate([high, low, high], axis=0)
        return jnp.dot(split_table, operand, preferred_element_type=jnp.float32)
    operand = jnp.concatenate([high, high, low], axis=1)
    return jnp.dot(operand, split_table, preferred_element_type=jnp.float32)


def transform(stacked, tables):
    left, right = tables
    width = right.shape[1] // 2
    middle = split_dot(left, stacked, True)
    products = split_dot(right, middle, False)
    out_real = products[:width, :width] - products[width:, width:]
    out_imag = products[:width, width:] + products[width:, :width]
    return out_real, out_imag


def stack(real_part, imag_part):
    return jnp.concatenate([real_part, imag_part], axis=0)


def propagate(real_part, imag_part, forward, inverse, kernel_real, kernel_imag):
    freq_real, freq_imag = transform(stack(real_part, imag_part), forward)
    prod_real = freq_real * kernel_real - freq_imag * kernel_imag
    prod_imag = freq_real * kernel_imag + freq_imag * kernel_real
    return transform(stack(prod_real, prod_imag), inverse)


def per_device(transmission, probe, prop_phase, row_off, col_off, measured):
    rows = transmission.shape[2]
    columns = transmission.shape[3]
    width = probe.shape[1]
    sections = lax.axis_size("cuts")
    cut_index = lax.axis_index("cuts")
    cosines, sines = dft_tables(width)
    forward = stacked_tables(cosines, sines, -1.0)
    inverse = stacked_tables(cosines, sines, 1.0)
    kernel_real = jnp.cos(prop_phase)
    kernel_imag = jnp.sin(prop_phase)
    zero = jnp.zeros((), jnp.int32)
    row = row_off[0]
    column = col_off[0]
    column_above = shifted(col_off, "tile", 1)[0]

    band = shifted(transmission, "tile", -1)
    whole = jnp.concatenate([transmission, band], axis=2)
    patch = lax.dynamic_slice(whole, (zero, zero, row, column), (1, 2, width, width))[0]

    have = [patch] + [rotated(patch, "cuts", k) for k in range(1, sections)]
    have = jnp.stack(have, axis=0)
    order = (cut_index - lax.iota(jnp.int32, sections)) % sections
    layers = jnp.take(have, order, axis=0)

    wave_real = probe[0]
    wave_imag = probe[1]
    saved = []
    for layer in range(sections):
        saved.append((wave_real, wave_imag))
        layer_real = layers[layer, 0]
        layer_imag = layers[layer, 1]
        mixed_real = wave_real * layer_real - wave_imag * layer_imag
        mixed_imag = wave_real * layer_imag + wave_imag * layer_real
        wave_real, wave_imag = propagate(
            mixed_real, mixed_imag, forward, inverse, kernel_real, kernel_imag
        )
    far_real, far_imag = transform(stack(wave_real, wave_imag), forward)
    residual = far_real * far_real + far_imag * far_imag - measured[0]
    grad_real, grad_imag = transform(stack(residual * far_real, residual * far_imag), inverse)
    pieces = [None] * sections
    for layer in range(sections - 1, -1, -1):
        inner_real, inner_imag = propagate(
            grad_real, grad_imag, forward, inverse, kernel_real, -kernel_imag
        )
        wave_real, wave_imag = saved[layer]
        pieces[layer] = jnp.stack(
            [wave_real * inner_real + wave_imag * inner_imag,
             wave_real * inner_imag - wave_imag * inner_real],
            axis=0,
        )
        if layer > 0:
            layer_real = layers[layer, 0]
            layer_imag = layers[layer, 1]
            grad_real = layer_real * inner_real + layer_imag * inner_imag
            grad_imag = layer_real * inner_imag - layer_imag * inner_real
    piece = jnp.take(jnp.stack(pieces, axis=0), cut_index, axis=0)

    padded = jnp.concatenate([piece, jnp.zeros_like(piece)], axis=1)
    spill = lax.dynamic_slice(padded, (zero, rows - row, zero), (2, width, width))
    arrived = shifted(spill, "tile", 1)

    own = jnp.pad(piece, ((0, 0), (rows, rows), (columns, columns)))
    own = lax.dynamic_slice(own, (zero, rows - row, columns - column), (2, rows, columns))
    above = jnp.pad(arrived, ((0, 0), (0, rows), (columns, columns)))
    above = lax.dynamic_slice(above, (zero, zero, columns - column_above), (2, rows, columns))
    result = own + above
    return result[None]


def solution(mesh):
    placed = (P("cuts", None, "tile", None), P(), P(), P("tile"), P("tile"), P("tile", None, None))
    return jax.shard_map(
        per_device,
        mesh=mesh,
        in_specs=placed,
        out_specs=P("cuts", None, "tile", None),
        check_vma=False,
    )
```

profile of v0, /device:TPU:128, one launch (start us, length us, event | category | flops | bytes accessed | tf_op | source)
XLA Modules:
  0.0 114.1 jit_solution(11616228365702921531)
XLA Ops:
  0.0 3.9 %collective-permute-start = (f32[1,2,256,1024]{3,2,1,0:T(8,128)}, f32[1,2,256,1024]{3,2,1,0:T(8,128)}, u32[]{:S(2)}, u32[]{:S(2)}) collective-permute-start(f32[1,2,256,1024]{3,2,1,0:T(8,128)} %param.6), channel_id=1, source_target_pairs={{4,0},{8,4},{12,8},{16,12},{20,16},{24,20},{28,24},{32,28},{36,32}... | collective-permute-start | bytes 6291464 | tf_op jit(solution)/shard_map/ppermute | solution.py:10
  5.2 1.0 fusion.362
  6.2 1.1 cosine_multiply_fusion
  7.3 1.0 broadcast_multiply_fusion.1
  8.3 1.1 fusion.334
  9.5 18.3 %collective-permute-done = f32[1,2,256,1024]{3,2,1,0:T(8,128)} collective-permute-done((f32[1,2,256,1024]{3,2,1,0:T(8,128)}, f32[1,2,256,1024]{3,2,1,0:T(8,128)}, u32[]{:S(2)}, u32[]{:S(2)}) %collective-permute-start) | collective-permute-done | bytes 2097184 | tf_op jit(solution)/shard_map/ppermute | solution.py:10
  27.8 1.2 %fusion.345 = f32[1,2,256,256]{3,2,1,0:T(8,128)S(1)} fusion(s32[]{:T(128)S(6)} %select_n.96, s32[]{:T(128)S(6)} %select_n.97, f32[1,2,256,1024]{3,2,1,0:T(8,128)S(1)} %copy-done, f32[1,2,256,1024]{3,2,1,0:T(8,128)} %collective-permute-done), kind=kLoop, calls=%fused_computation.407 | loop fusion | flops 131072 | bytes 4718600 | tf_op jit(solution)/shard_map/concatenate | solution.py:95
  29.0 1.6 %collective-permute-start.1 = (f32[2,256,256]{2,1,0:T(8,128)S(1)}, f32[2,256,256]{2,1,0:T(8,128)}, u32[]{:S(2)}, u32[]{:S(2)}) collective-permute-start(f32[2,256,256]{2,1,0:T(8,128)S(1)} %bitcast.157), channel_id=1, source_target_pairs={{0,1},{1,2},{2,3},{3,0},{4,5},{5,6},{6,7},{7,4},{8,9},{9,10},{10,1... | collective-permute-start | bytes 1572872 | tf_op jit(solution)/shard_map/ppermute | solution.py:16
  30.6 2.7 %collective-permute-start.2 = (f32[2,256,256]{2,1,0:T(8,128)S(1)}, f32[2,256,256]{2,1,0:T(8,128)S(1)}, u32[]{:S(2)}, u32[]{:S(2)}) collective-permute-start(f32[2,256,256]{2,1,0:T(8,128)S(1)} %bitcast.158), channel_id=1, source_target_pairs={{0,2},{1,3},{2,0},{3,1},{4,6},{5,7},{6,4},{7,5},{8,10},{9,11},{10,... | collective-permute-start | bytes 1572872 | tf_op jit(solution)/shard_map/ppermute | solution.py:16
  33.3 1.4 %collective-permute-start.3 = (f32[2,256,256]{2,1,0:T(8,128)S(1)}, f32[2,256,256]{2,1,0:T(8,128)}, u32[]{:S(2)}, u32[]{:S(2)}) collective-permute-start(f32[2,256,256]{2,1,0:T(8,128)S(1)} %bitcast.159), channel_id=1, source_target_pairs={{0,3},{1,0},{2,1},{3,2},{4,7},{5,4},{6,5},{7,6},{8,11},{9,8},{10,9... | collective-permute-start | bytes 1572872 | tf_op jit(solution)/shard_map/ppermute | solution.py:16
  35.2 1.1 copy.126
  36.3 1.6 %fusion.3 = (bf16[512,512]{1,0:T(8,128)(2,1)}, bf16[512,512]{1,0:T(8,128)(2,1)}, bf16[512,512]{1,0:T(8,128)(2,1)}, bf16[512,512]{1,0:T(8,128)(2,1)}) fusion(f32[256,256]{1,0:T(8,128)S(1)} %get-tuple-element.157, f32[256,256]{1,0:T(8,128)S(1)} %get-tuple-element.159, f32[256,256]{1,0:T(8,128)S(1)} %get-tuple-element.160, ...), kind=kLoop, calls=%fused_computation.17 | loop fusion | flops 4718592 | bytes 3407872 | tf_op jit(solution)/shard_map/convert_element_type | solution.py:31
  37.9 0.9 fusion.403
  38.8 5.4 %collective-permute-done.1 = f32[2,256,256]{2,1,0:T(8,128)} collective-permute-done((f32[2,256,256]{2,1,0:T(8,128)S(1)}, f32[2,256,256]{2,1,0:T(8,128)}, u32[]{:S(2)}, u32[]{:S(2)}) %collective-permute-start.1) | collective-permute-done | bytes 524320 | tf_op jit(solution)/shard_map/ppermute | solution.py:16
  44.2 11.8 %collective-permute-done.2 = f32[2,256,256]{2,1,0:T(8,128)S(1)} collective-permute-done((f32[2,256,256]{2,1,0:T(8,128)S(1)}, f32[2,256,256]{2,1,0:T(8,128)S(1)}, u32[]{:S(2)}, u32[]{:S(2)}) %collective-permute-start.2) | collective-permute-done | bytes 524320 | tf_op jit(solution)/shard_map/ppermute | solution.py:16
  56.1 0.8 copy-done.7
  56.9 1.7 %pad_maximum_fusion = f32[4,2,256,256]{3,2,1,0:T(8,128)S(1)} fusion(f32[1,2,256,256]{3,2,1,0:T(8,128)} %bitcast.6, f32[1,2,256,256]{3,2,1,0:T(8,128)} %bitcast.160, f32[1,2,256,256]{3,2,1,0:T(8,128)} %bitcast.4, f32[1,2,256,256]{3,2,1,0:T(8,128)} %copy-done.1), kind=kLoop, calls=%fused_computation.7 | loop fusion | flops 1572864 | bytes 4194304 | tf_op jit(solution)/shard_map/stack | solution.py:99
  58.5 2.0 %gather_fusion = f32[4,2,256,256]{3,2,1,0:T(8,128)} fusion(f32[4,2,256,256]{3,2,1,0:T(8,128)S(1)} %pad_maximum_fusion, s32[1024]{0:T(1024)S(1)} %pad_clamp_fusion), kind=kCustom, calls=%fused_computation | custom fusion | bytes 4194320 | tf_op jit(solution)/shard_map/jit(_take)/gather | solution.py:101
  60.5 2.9 %copy.86 = f32[4,2,256,256]{2,3,1,0:T(8,128)} copy(f32[4,2,256,256]{3,2,1,0:T(8,128)} %gather_fusion) | data formatting | bytes 4194304 | tf_op jit(solution)/shard_map/jit(_take)/gather | solution.py:101
  63.4 1.9 %broadcast_select_fusion = f32[4,2,256,256]{2,3,1,0:T(8,128)S(1)} fusion(f32[4,2,256,256]{2,3,1,0:T(8,128)} %copy.86, pred[4]{0:T(512)(128)(4,1)S(1)} %compare_and_fusion), kind=kLoop, calls=%fused_computation.29 | loop fusion | flops 524288 | bytes 4194308 | tf_op jit(solution)/shard_map/jit(_take)/select_n | solution.py:101
  65.5 0.8 copy-done.5
  66.5 0.6 fusion.229
  67.5 0.6 fusion.16
  68.4 0.8 copy-done.3
  69.3 0.6 fusion.235
  70.0 0.3 copy-done.8
  70.4 0.6 fusion.28
  71.3 0.6 fusion.241
  71.9 0.6 fusion.40
  72.7 0.6 fusion.245
  73.4 0.6 fusion.52
  74.3 0.6 fusion.249
  74.9 0.6 fusion.64
  75.7 0.6 fusion.253
  76.4 0.6 fusion.76
  77.3 0.6 fusion.257
  77.9 0.6 fusion.88
  78.7 0.6 fusion.261
  79.4 0.6 fusion.100
  80.2 0.6 fusion.265
  80.8 0.6 fusion.112
  81.6 0.6 fusion.269
  82.3 0.6 fusion.124
  83.1 0.6 fusion.273
  83.7 0.8 fusion.136
  84.7 0.6 fusion.277
  85.4 0.6 fusion.148
  86.3 0.6 fusion.281
  86.9 0.6 fusion.160
  87.8 0.6 fusion.285
  88.4 0.6 fusion.172
  89.3 0.6 fusion.289
  90.0 0.6 fusion.184
  90.8 0.6 fusion.293
  91.4 0.6 fusion.196
  92.4 0.6 fusion.297
  93.0 0.6 fusion.208
  93.9 0.6 fusion.301
  94.5 0.6 fusion.220
  95.8 1.9 %collective-permute-start.4 = (f32[2,256,256]{1,2,0:T(8,128)S(1)}, f32[2,256,256]{1,2,0:T(8,128)S(1)}, u32[]{:S(2)}, u32[]{:S(2)}) collective-permute-start(f32[2,256,256]{1,2,0:T(8,128)S(1)} %pad_dynamic-slice_fusion.8), channel_id=1, source_target_pairs={{0,4},{4,8},{8,12},{12,16},{16,20},{20,24},{24,28},{28,32},{32,36}... | collective-permute-start | bytes 1572872 | tf_op jit(solution)/shard_map/ppermute | solution.py:10
  97.7 2.1 %collective-permute-start.5 = (s32[1]{0:T(128)}, s32[1]{0:T(128)}, u32[]{:S(2)}, u32[]{:S(2)}) collective-permute-start(s32[1]{0:T(128)} %param.10), channel_id=1, source_target_pairs={{0,4},{4,8},{8,12},{12,16},{16,20},{20,24},{24,28},{28,32},{32,36}... | collective-permute-start | bytes 20 | tf_op jit(solution)/shard_map/ppermute | solution.py:10
  99.8 10.0 %collective-permute-done.5 = s32[1]{0:T(128)} collective-permute-done((s32[1]{0:T(128)}, s32[1]{0:T(128)}, u32[]{:S(2)}, u32[]{:S(2)}) %collective-permute-start.5) | collective-permute-done | bytes 36 | tf_op jit(solution)/shard_map/ppermute | solution.py:10
  111.0 1.3 %fusion.1 = f32[1,2,256,1024]{2,3,1,0:T(8,128)S(1)} fusion(s32[]{:T(128)S(6)} %select_n.105, f32[2,256,256]{1,2,0:T(8,128)S(1)} %collective-permute-done.4, s32[]{:T(128)S(6)} %select_n.102, s32[]{:T(128)S(6)} %select_n.103, f32[2,256,256]{1,2,0:T(8,128)S(1)} %fusion.344), kind=kLoop, calls=%fused_computation.6 | loop fusion | flops 524288 | bytes 3145740 | tf_op jit(solution)/shard_map/broadcast_in_dim | solution.py:145
  112.3 1.8 %copy.163 = f32[1,2,256,1024]{3,2,1,0:T(8,128)} copy(f32[1,2,256,1024]{2,3,1,0:T(8,128)S(1)} %fusion.1) | data formatting | bytes 4194304 | tf_op jit(solution)/shard_map/broadcast_in_dim | solution.py:145
  (80 shorter events, 5.9 us)
Async XLA Ops:
  0.0 27.8 %collective-permute-start = (f32[1,2,256,1024]{3,2,1,0:T(8,128)}, f32[1,2,256,1024]{3,2,1,0:T(8,128)}, u32[]{:S(2)}, u32[]{:S(2)}) collective-permute-start(f32[1,2,256,1024]{3,2,1,0:T(8,128)} %param.6), channel_id=1, source_target_pairs={{4,0},{8,4},{12,8},{16,12},{20,16},{24,20},{28,24},{32,28},{36,32}... | collective-permute-start | bytes 6291464 | tf_op jit(solution)/shard_map/ppermute | solution.py:10
  5.2 4.2 %copy-start.2 = (f32[2,256,256]{2,1,0:T(8,128)S(1)}, f32[2,256,256]{2,1,0:T(8,128)}, u32[]{:S(2)}) copy-start(f32[2,256,256]{2,1,0:T(8,128)} %param.7) | copy-start | bytes 1572868
  8.3 19.5 %copy-start = (f32[1,2,256,1024]{3,2,1,0:T(8,128)S(1)}, f32[1,2,256,1024]{3,2,1,0:T(8,128)}, u32[]{:S(2)}) copy-start(f32[1,2,256,1024]{3,2,1,0:T(8,128)} %param.6) | copy-start | bytes 6291460
  9.4 25.6 %copy-start.12 = (f32[256,256]{1,0:T(8,128)S(1)}, f32[256,256]{1,0:T(8,128)}, u32[]{:S(2)}) copy-start(f32[256,256]{1,0:T(8,128)} %param.8) | copy-start | bytes 786436
  29.0 8.9 %copy-start.1 = (f32[1,2,256,256]{3,2,1,0:T(8,128)}, f32[1,2,256,256]{3,2,1,0:T(8,128)S(1)}, u32[]{:S(2)}) copy-start(f32[1,2,256,256]{3,2,1,0:T(8,128)S(1)} %fusion.345) | copy-start | bytes 1572868
  29.0 15.2 %collective-permute-start.1 = (f32[2,256,256]{2,1,0:T(8,128)S(1)}, f32[2,256,256]{2,1,0:T(8,128)}, u32[]{:S(2)}, u32[]{:S(2)}) collective-permute-start(f32[2,256,256]{2,1,0:T(8,128)S(1)} %bitcast.157), channel_id=1, source_target_pairs={{0,1},{1,2},{2,3},{3,0},{4,5},{5,6},{6,7},{7,4},{8,9},{9,10},{10,1... | collective-permute-start | bytes 1572872 | tf_op jit(solution)/shard_map/ppermute | solution.py:16
  30.6 25.5 %collective-permute-start.2 = (f32[2,256,256]{2,1,0:T(8,128)S(1)}, f32[2,256,256]{2,1,0:T(8,128)S(1)}, u32[]{:S(2)}, u32[]{:S(2)}) collective-permute-start(f32[2,256,256]{2,1,0:T(8,128)S(1)} %bitcast.158), channel_id=1, source_target_pairs={{0,2},{1,3},{2,0},{3,1},{4,6},{5,7},{6,4},{7,5},{8,10},{9,11},{10,... | collective-permute-start | bytes 1572872 | tf_op jit(solution)/shard_map/ppermute | solution.py:16
  33.3 22.8 %collective-permute-start.3 = (f32[2,256,256]{2,1,0:T(8,128)S(1)}, f32[2,256,256]{2,1,0:T(8,128)}, u32[]{:S(2)}, u32[]{:S(2)}) collective-permute-start(f32[2,256,256]{2,1,0:T(8,128)S(1)} %bitcast.159), channel_id=1, source_target_pairs={{0,3},{1,0},{2,1},{3,2},{4,7},{5,4},{6,5},{7,6},{8,11},{9,8},{10,9... | collective-permute-start | bytes 1572872 | tf_op jit(solution)/shard_map/ppermute | solution.py:16
  56.1 0.8 copy-start.7
  65.3 1.0 copy-start.5
  65.3 1.2 %copy-start.6 = (bf16[512,512]{1,0:T(8,128)(2,1)S(1)}, bf16[512,512]{1,0:T(8,128)(2,1)}, u32[]{:S(2)}) copy-start(bf16[512,512]{1,0:T(8,128)(2,1)} %get-tuple-element.154) | copy-start | bytes 1572868
  66.5 0.9 copy-start.10
  66.5 1.0 copy-start.11
  68.1 1.0 copy-start.3
  68.1 1.2 %copy-start.4 = (bf16[512,512]{1,0:T(8,128)(2,1)S(1)}, bf16[512,512]{1,0:T(8,128)(2,1)}, u32[]{:S(2)}) copy-start(bf16[512,512]{1,0:T(8,128)(2,1)} %get-tuple-element.67) | copy-start | bytes 1572868
  69.3 0.9 copy-start.8
  69.3 1.0 copy-start.9
  95.8 15.1 %collective-permute-start.4 = (f32[2,256,256]{1,2,0:T(8,128)S(1)}, f32[2,256,256]{1,2,0:T(8,128)S(1)}, u32[]{:S(2)}, u32[]{:S(2)}) collective-permute-start(f32[2,256,256]{1,2,0:T(8,128)S(1)} %pad_dynamic-slice_fusion.8), channel_id=1, source_target_pairs={{0,4},{4,8},{8,12},{12,16},{16,20},{20,24},{24,28},{28,32},{32,36}... | collective-permute-start | bytes 1572872 | tf_op jit(solution)/shard_map/ppermute | solution.py:10
  97.7 12.1 %collective-permute-start.5 = (s32[1]{0:T(128)}, s32[1]{0:T(128)}, u32[]{:S(2)}, u32[]{:S(2)}) collective-permute-start(s32[1]{0:T(128)} %param.10), channel_id=1, source_target_pairs={{0,4},{4,8},{8,12},{12,16},{16,20},{20,24},{24,28},{28,32},{32,36}... | collective-permute-start | bytes 20 | tf_op jit(solution)/shard_map/ppermute | solution.py:10
where the time goes:
time: 115 us; the launch traced here: 114 us
  waiting for transfers between devices  45.5 us (40%)
  matrix products  22.5 us (20%)
  other arithmetic  16.2 us (14%)
  starting transfers between devices  13.6 us (12%)
  local copies, waits for them, and re-layouts  12.9 us (11%)
  between operations  3.27 us (3%)
    ppermute x3, waiting for transfers between devices, shifted(): return lax.ppermute(value, axis, pairs)  28.3 us
    ppermute x3, waiting for transfers between devices, rotated(): return lax.ppermute(value, axis, pairs)  17.2 us
    dot_general x18, matrix products, split_dot(): return jnp.dot(operand, split_table, preferred_element_type=jnp.float32)  11.3 us
    dot_general x18, matrix products, split_dot(): return jnp.dot(split_table, operand, preferred_element_type=jnp.float32)  11.2 us
    ppermute x3, starting transfers between devices, shifted(): return lax.ppermute(value, axis, pairs)  7.89 us
    ppermute x3, starting transfers between devices, rotated(): return lax.ppermute(value, axis, pairs)  5.73 us
    unnamed x30, local copies, waits for them, and re-layouts  5.06 us
    gather x2, local copies, waits for them, and re-layouts, per_device(): layers = jnp.take(have, order, axis=0)  4.88 us
  transfers between devices with their start and end apart: 6, of which 4 were waited for; matrix products, arithmetic and copies ran while one was open for 7% of the time, Pallas kernels for 0%

commit v1 on v0

--- a/solution.py
+++ b/solution.py
@@ -89,24 +89,33 @@
     zero = jnp.zeros((), jnp.int32)
     row = row_off[0]
     column = col_off[0]
-    column_above = shifted(col_off, "tile", 1)[0]
+    offsets_above = shifted(jnp.stack([row, column]), "tile", 1)
+    row_above = offsets_above[0]
+    column_above = offsets_above[1]
 
-    band = shifted(transmission, "tile", -1)
-    whole = jnp.concatenate([transmission, band], axis=2)
-    patch = lax.dynamic_slice(whole, (zero, zero, row, column), (1, 2, width, width))[0]
+    strip = transmission[0]
+    lent = lax.dynamic_slice(strip, (zero, zero, column_above), (2, width, width))
+    lent = jnp.pad(lent, ((0, 0), (width, 0), (0, 0)))
+    lent = lax.dynamic_slice(lent, (zero, row_above, zero), (2, width, width))
+    borrowed = shifted(lent, "tile", -1)
+    kept = jnp.pad(strip, ((0, 0), (0, width), (0, 0)))
+    kept = lax.dynamic_slice(kept, (zero, row, column), (2, width, width))
+    window = kept + borrowed
 
-    have = [patch] + [rotated(patch, "cuts", k) for k in range(1, sections)]
-    have = jnp.stack(have, axis=0)
-    order = (cut_index - lax.iota(jnp.int32, sections)) % sections
-    layers = jnp.take(have, order, axis=0)
+    layers = []
+    for layer in range(sections):
+        total = jnp.where(cut_index == layer, window, jnp.zeros_like(window))
+        for step in range(1, sections):
+            total = total + lax.ppermute(window, "cuts", [(layer, (layer + step) % sections)])
+        layers.append(total)
 
     wave_real = probe[0]
     wave_imag = probe[1]
     saved = []
     for layer in range(sections):
         saved.append((wave_real, wave_imag))
-        layer_real = layers[layer, 0]
-        layer_imag = layers[layer, 1]
+        layer_real = layers[layer][0]
+        layer_imag = layers[layer][1]
         mixed_real = wave_real * layer_real - wave_imag * layer_imag
         mixed_imag = wave_real * layer_imag + wave_imag * layer_real
         wave_real, wave_imag = propagate(
@@ -127,8 +136,8 @@
             axis=0,
         )
         if layer > 0:
-            layer_real = layers[layer, 0]
-            layer_imag = layers[layer, 1]
+            layer_real = layers[layer][0]
+            layer_imag = layers[layer][1]
             grad_real = layer_real * inner_real + layer_imag * inner_imag
             grad_imag = layer_real * inner_imag - layer_imag * inner_real
     piece = jnp.take(jnp.stack(pieces, axis=0), cut_index, axis=0)

time: 115 us -> 129 us (1.12)
  starting transfers between devices: 13.6 us -> 24.3 us
  waiting for transfers between devices: 45.5 us -> 51.3 us
  between operations: 3.27 us -> 7.58 us
  local copies, waits for them, and re-layouts: 12.9 us -> 9.01 us
  other arithmetic: 16.2 us -> 12.4 us
    ppermute x3 -> x12, starting transfers between devices: 5.73 us -> 18.6 us  [per_device(): lax.ppermute(window, 'cuts', [(layer, (layer + step) % sections)])]
    ppermute x3 -> x12, waiting for transfers between devices: 17.2 us -> 29.8 us  [per_device(): lax.ppermute(window, 'cuts', [(layer, (layer + step) % sections)])]
    ppermute x3, waiting for transfers between devices: 28.3 us -> 21.5 us  [shifted(): return lax.ppermute(value, axis, pairs)]
    gather x2 -> x0, local copies, waits for them, and re-layouts: 4.88 us -> none  [per_device(): layers = jnp.take(have, order, axis=0)]
    add x0 -> x2, other arithmetic: none -> 3.12 us  [the longest x1 2.12 us: per_device(): total + lax.ppermute(window, 'cuts', [(layer, (layer + step) % sections)])]
    convert_element_type x20, other arithmetic: 4.37 us -> 2.09 us  [halves(): return (high.astype(jnp.bfloat16), low.astype(jnp.bfloat16))]
    ppermute x3, starting transfers between devices: 7.89 us -> 5.75 us  [shifted(): return lax.ppermute(value, axis, pairs)]
    select_n x2 -> x0, other arithmetic: 1.87 us -> none  [per_device(): layers = jnp.take(have, order, axis=0)]
  transfers between devices with their start and end apart: 6 -> 15, of which waited for: 4 -> 9; matrix products, arithmetic and copies ran while one was open for 7% -> 6% of each run, Pallas kernels for 0% -> 0%
where the time goes in v1:
time: 129 us; the launch traced here: 127 us
  waiting for transfers between devices  51.3 us (40%)
  starting transfers between devices  24.3 us (19%)
  matrix products  22.6 us (18%)
  other arithmetic  12.4 us (10%)
  local copies, waits for them, and re-layouts  9.01 us (7%)
  between operations  7.58 us (6%)
    ppermute x12, waiting for transfers between devices, per_device(): lax.ppermute(window, 'cuts', [(layer, (layer + step) % sections)])  29.8 us
    ppermute x3, waiting for transfers between devices, shifted(): return lax.ppermute(value, axis, pairs)  21.5 us
    ppermute x12, starting transfers between devices, per_device(): lax.ppermute(window, 'cuts', [(layer, (layer + step) % sections)])  18.6 us
    dot_general x18, matrix products, split_dot(): return jnp.dot(split_table, operand, preferred_element_type=jnp.float32)  11.4 us
    dot_general x18, matrix products, split_dot(): return jnp.dot(operand, split_table, preferred_element_type=jnp.float32)  11.2 us
    ppermute x3, starting transfers between devices, shifted(): return lax.ppermute(value, axis, pairs)  5.75 us
    unnamed x9, local copies, waits for them, and re-layouts  3.4 us
  transfers between devices with their start and end apart: 15, of which 9 were waited for; matrix products, arithmetic and copies ran while one was open for 6% of the time, Pallas kernels for 0%

profile of v1, /device:TPU:128, one launch (start us, length us, event | category | flops | bytes accessed | tf_op | source)
XLA Modules:
  0.0 127.2 jit_solution(14253058066643195347)
XLA Ops:
  1.4 1.9 %collective-permute-start = (s32[2]{0:T(128)S(1)}, s32[2]{0:T(128)S(1)}, u32[]{:S(2)}, u32[]{:S(2)}) collective-permute-start(s32[2]{0:T(128)S(1)} %pad_add_fusion), channel_id=1, source_target_pairs={{0,4},{4,8},{8,12},{12,16},{16,20},{20,24},{24,28},{28,32},{32,36}... | collective-permute-start | bytes 32 | tf_op jit(solution)/shard_map/ppermute | solution.py:10
  3.3 6.3 %collective-permute-done = s32[2]{0:T(128)S(1)} collective-permute-done((s32[2]{0:T(128)S(1)}, s32[2]{0:T(128)S(1)}, u32[]{:S(2)}, u32[]{:S(2)}) %collective-permute-start) | collective-permute-done | bytes 40 | tf_op jit(solution)/shard_map/ppermute | solution.py:10
  9.5 0.7 fusion.401
  12.3 1.3 %constant_dynamic-slice_fusion = f32[1,2,256,256]{3,2,1,0:T(8,128)S(1)} fusion(f32[1,2,256,1024]{3,2,1,0:T(8,128)} %param.6, s32[]{:T(128)S(6)} %select_n.92), kind=kLoop, calls=%fused_computation.541 | loop fusion | bytes 1048580 | tf_op jit(solution)/shard_map/dynamic_slice | solution.py:97
  16.0 1.9 %collective-permute-start.1 = (f32[2,256,256]{1,2,0:T(8,128)S(1)}, f32[2,256,256]{1,2,0:T(8,128)S(1)}, u32[]{:S(2)}, u32[]{:S(2)}) collective-permute-start(f32[2,256,256]{1,2,0:T(8,128)S(1)} %pad_dynamic-slice_fusion.8), channel_id=1, source_target_pairs={{4,0},{8,4},{12,8},{16,12},{20,16},{24,20},{28,24},{32,28},{36,32}... | collective-permute-start | bytes 1572872 | tf_op jit(solution)/shard_map/ppermute | solution.py:10
  17.9 1.9 %copy.8 = f32[1,2,256,1024]{2,3,1,0:T(8,128)S(1)} copy(f32[1,2,256,1024]{3,2,1,0:T(8,128)} %param.6) | data formatting | bytes 4194304 | tf_op args[0]
  19.9 4.7 %collective-permute-done.1 = f32[2,256,256]{1,2,0:T(8,128)S(1)} collective-permute-done((f32[2,256,256]{1,2,0:T(8,128)S(1)}, f32[2,256,256]{1,2,0:T(8,128)S(1)}, u32[]{:S(2)}, u32[]{:S(2)}) %collective-permute-start.1) | collective-permute-done | bytes 524320 | tf_op jit(solution)/shard_map/ppermute | solution.py:10
  24.6 1.0 fusion.345
  25.6 0.8 collective-permute-start.10
  26.4 3.4 %collective-permute-start.11 = (f32[2,256,256]{1,2,0:T(8,128)}, f32[2,256,256]{1,2,0:T(8,128)S(1)}, u32[]{:S(2)}, u32[]{:S(2)}) collective-permute-start(f32[2,256,256]{1,2,0:T(8,128)} %fusion.345), channel_id=1, source_target_pairs={{0,1},{4,5},{8,9},{12,13},{16,17},{20,21},{24,25},{28,29},{32,33},... | collective-permute-start | bytes 1572872 | tf_op jit(solution)/shard_map/ppermute | solution.py:109
  29.9 2.8 %collective-permute-start.12 = (f32[2,256,256]{1,2,0:T(8,128)}, f32[2,256,256]{1,2,0:T(8,128)S(1)}, u32[]{:S(2)}, u32[]{:S(2)}) collective-permute-start(f32[2,256,256]{1,2,0:T(8,128)} %fusion.345), channel_id=1, source_target_pairs={{0,2},{4,6},{8,10},{12,14},{16,18},{20,22},{24,26},{28,30},{32,34}... | collective-permute-start | bytes 1572872 | tf_op jit(solution)/shard_map/ppermute | solution.py:109
  32.7 2.7 %collective-permute-start.13 = (f32[2,256,256]{1,2,0:T(8,128)}, f32[2,256,256]{1,2,0:T(8,128)}, u32[]{:S(2)}, u32[]{:S(2)}) collective-permute-start(f32[2,256,256]{1,2,0:T(8,128)} %fusion.345), channel_id=1, source_target_pairs={{0,3},{4,7},{8,11},{12,15},{16,19},{20,23},{24,27},{28,31},{32,35}... | collective-permute-start | bytes 1572872 | tf_op jit(solution)/shard_map/ppermute | solution.py:109
  35.4 1.5 %collective-permute-start.2 = (f32[2,256,256]{1,2,0:T(8,128)}, f32[2,256,256]{1,2,0:T(8,128)}, u32[]{:S(2)}, u32[]{:S(2)}) collective-permute-start(f32[2,256,256]{1,2,0:T(8,128)} %fusion.345), channel_id=1, source_target_pairs={{1,2},{5,6},{9,10},{13,14},{17,18},{21,22},{25,26},{29,30},{33,34}... | collective-permute-start | bytes 1572872 | tf_op jit(solution)/shard_map/ppermute | solution.py:109
  36.9 1.5 %collective-permute-start.3 = (f32[2,256,256]{1,2,0:T(8,128)}, f32[2,256,256]{1,2,0:T(8,128)}, u32[]{:S(2)}, u32[]{:S(2)}) collective-permute-start(f32[2,256,256]{1,2,0:T(8,128)} %fusion.345), channel_id=1, source_target_pairs={{1,3},{5,7},{9,11},{13,15},{17,19},{21,23},{25,27},{29,31},{33,35}... | collective-permute-start | bytes 1572872 | tf_op jit(solution)/shard_map/ppermute | solution.py:109
  38.3 4.2 %collective-permute-done.11 = f32[2,256,256]{1,2,0:T(8,128)S(1)} collective-permute-done((f32[2,256,256]{1,2,0:T(8,128)}, f32[2,256,256]{1,2,0:T(8,128)S(1)}, u32[]{:S(2)}, u32[]{:S(2)}) %collective-permute-start.11) | collective-permute-done | bytes 524320 | tf_op jit(solution)/shard_map/ppermute | solution.py:109
  42.5 1.3 %collective-permute-start.4 = (f32[2,256,256]{1,2,0:T(8,128)}, f32[2,256,256]{1,2,0:T(8,128)}, u32[]{:S(2)}, u32[]{:S(2)}) collective-permute-start(f32[2,256,256]{1,2,0:T(8,128)} %fusion.345), channel_id=1, source_target_pairs={{1,0},{5,4},{9,8},{13,12},{17,16},{21,20},{25,24},{29,28},{33,32},... | collective-permute-start | bytes 1572872 | tf_op jit(solution)/shard_map/ppermute | solution.py:109
  44.3 1.1 copy.49
  45.4 1.1 cosine_multiply_fusion
  46.4 1.0 broadcast_multiply_fusion.1
  47.6 3.7 %collective-permute-done.12 = f32[2,256,256]{1,2,0:T(8,128)S(1)} collective-permute-done((f32[2,256,256]{1,2,0:T(8,128)}, f32[2,256,256]{1,2,0:T(8,128)S(1)}, u32[]{:S(2)}, u32[]{:S(2)}) %collective-permute-start.12) | collective-permute-done | bytes 524320 | tf_op jit(solution)/shard_map/ppermute | solution.py:109
  51.3 0.7 collective-permute-start.5
  52.0 3.0 %collective-permute-done.13 = f32[2,256,256]{1,2,0:T(8,128)} collective-permute-done((f32[2,256,256]{1,2,0:T(8,128)}, f32[2,256,256]{1,2,0:T(8,128)}, u32[]{:S(2)}, u32[]{:S(2)}) %collective-permute-start.13) | collective-permute-done | bytes 524320 | tf_op jit(solution)/shard_map/ppermute | solution.py:109
  55.0 1.3 %collective-permute-start.6 = (f32[2,256,256]{1,2,0:T(8,128)}, f32[2,256,256]{1,2,0:T(8,128)S(1)}, u32[]{:S(2)}, u32[]{:S(2)}) collective-permute-start(f32[2,256,256]{1,2,0:T(8,128)} %fusion.345), channel_id=1, source_target_pairs={{2,0},{6,4},{10,8},{14,12},{18,16},{22,20},{26,24},{30,28},{34,32}... | collective-permute-start | bytes 1572872 | tf_op jit(solution)/shard_map/ppermute | solution.py:109
  56.3 0.7 collective-permute-start.7
  57.0 1.3 %collective-permute-start.8 = (f32[2,256,256]{1,2,0:T(8,128)}, f32[2,256,256]{1,2,0:T(8,128)S(1)}, u32[]{:S(2)}, u32[]{:S(2)}) collective-permute-start(f32[2,256,256]{1,2,0:T(8,128)} %fusion.345), channel_id=1, source_target_pairs={{3,0},{7,4},{11,8},{15,12},{19,16},{23,20},{27,24},{31,28},{35,32}... | collective-permute-start | bytes 1572872 | tf_op jit(solution)/shard_map/ppermute | solution.py:109
  58.3 6.8 %collective-permute-done.4 = f32[2,256,256]{1,2,0:T(8,128)} collective-permute-done((f32[2,256,256]{1,2,0:T(8,128)}, f32[2,256,256]{1,2,0:T(8,128)}, u32[]{:S(2)}, u32[]{:S(2)}) %collective-permute-start.4) | collective-permute-done | bytes 524320 | tf_op jit(solution)/shard_map/ppermute | solution.py:109
  65.1 0.7 collective-permute-start.9
  65.8 1.0 fusion.362
  67.1 1.1 fusion.400
  68.3 9.4 %collective-permute-done.6 = f32[2,256,256]{1,2,0:T(8,128)S(1)} collective-permute-done((f32[2,256,256]{1,2,0:T(8,128)}, f32[2,256,256]{1,2,0:T(8,128)S(1)}, u32[]{:S(2)}, u32[]{:S(2)}) %collective-permute-start.6) | collective-permute-done | bytes 524320 | tf_op jit(solution)/shard_map/ppermute | solution.py:109
  77.7 2.7 %collective-permute-done.8 = f32[2,256,256]{1,2,0:T(8,128)S(1)} collective-permute-done((f32[2,256,256]{1,2,0:T(8,128)}, f32[2,256,256]{1,2,0:T(8,128)S(1)}, u32[]{:S(2)}, u32[]{:S(2)}) %collective-permute-start.8) | collective-permute-done | bytes 524320 | tf_op jit(solution)/shard_map/ppermute | solution.py:109
  80.4 2.1 %add_add_fusion.1 = (f32[2,256,256]{1,2,0:T(8,128)S(1)}, f32[2,256,256]{1,2,0:T(8,128)S(1)}, f32[2,256,256]{1,2,0:T(8,128)S(1)}, f32[2,256,256]{1,2,0:T(8,128)S(1)}) fusion(f32[2,256,256]{1,2,0:T(8,128)S(1)} %collective-permute-done.10, f32[2,256,256]{1,2,0:T(8,128)S(1)} %collective-permute-done.9, f32[2,256,256]{1,2,0:T(8,128)S(1)} %collective-permute-done.8, ...), kind=kLoop, calls=%fused_computation.428 | loop fusion | flops 2097152 | bytes 8912900 | tf_op jit(solution)/shard_map/add | solution.py:109
  82.7 0.6 fusion.229
  83.3 0.6 fusion.16
  84.1 0.6 fusion.235
  85.7 0.6 fusion.241
  86.3 0.6 fusion.40
  87.1 0.6 fusion.245
  87.8 0.6 fusion.52
  88.7 0.6 fusion.249
  90.1 0.6 fusion.253
  91.7 0.6 fusion.257
  93.2 0.6 fusion.261
  94.6 0.6 fusion.265
  95.2 0.6 fusion.112
  96.0 0.6 fusion.269
  96.7 0.6 fusion.124
  97.5 0.8 fusion.273
  99.1 0.6 fusion.277
  100.7 0.6 fusion.281
  102.2 0.6 fusion.285
  102.8 0.6 fusion.172
  103.8 0.6 fusion.289
  104.4 0.6 fusion.184
  105.3 0.6 fusion.293
  105.9 0.6 fusion.196
  106.8 0.6 fusion.297
  107.5 0.6 fusion.208
  108.3 0.6 fusion.301
  109.0 0.6 fusion.220
  110.3 1.9 %collective-permute-start.14 = (f32[2,256,256]{1,2,0:T(8,128)S(1)}, f32[2,256,256]{1,2,0:T(8,128)S(1)}, u32[]{:S(2)}, u32[]{:S(2)}) collective-permute-start(f32[2,256,256]{1,2,0:T(8,128)S(1)} %pad_dynamic-slice_fusion.7), channel_id=1, source_target_pairs={{0,4},{4,8},{8,12},{12,16},{16,20},{20,24},{24,28},{28,32},{32,36}... | collective-permute-start | bytes 1572872 | tf_op jit(solution)/shard_map/ppermute | solution.py:10
  113.6 10.5 %collective-permute-done.14 = f32[2,256,256]{1,2,0:T(8,128)S(1)} collective-permute-done((f32[2,256,256]{1,2,0:T(8,128)S(1)}, f32[2,256,256]{1,2,0:T(8,128)S(1)}, u32[]{:S(2)}, u32[]{:S(2)}) %collective-permute-start.14) | collective-permute-done | bytes 524320 | tf_op jit(solution)/shard_map/ppermute | solution.py:10
  124.1 1.3 %fusion.1 = f32[1,2,256,1024]{2,3,1,0:T(8,128)S(1)} fusion(s32[]{:T(128)S(6)} %select_n.105, f32[2,256,256]{1,2,0:T(8,128)S(1)} %collective-permute-done.14, s32[]{:T(128)S(6)} %select_n.102, s32[]{:T(128)S(6)} %select_n.103, f32[2,256,256]{1,2,0:T(8,128)S(1)} %fusion.344), kind=kLoop, calls=%fused_computation.4 | loop fusion | flops 524288 | bytes 3145740 | tf_op jit(solution)/shard_map/broadcast_in_dim | solution.py:154
  125.4 1.8 %copy.86 = f32[1,2,256,1024]{3,2,1,0:T(8,128)} copy(f32[1,2,256,1024]{2,3,1,0:T(8,128)S(1)} %fusion.1) | data formatting | bytes 4194304 | tf_op jit(solution)/shard_map/broadcast_in_dim | solution.py:154
  (76 shorter events, 10.9 us)
Async XLA Ops:
  1.4 8.2 %collective-permute-start = (s32[2]{0:T(128)S(1)}, s32[2]{0:T(128)S(1)}, u32[]{:S(2)}, u32[]{:S(2)}) collective-permute-start(s32[2]{0:T(128)S(1)} %pad_add_fusion), channel_id=1, source_target_pairs={{0,4},{4,8},{8,12},{12,16},{16,20},{20,24},{24,28},{28,32},{32,36}... | collective-permute-start | bytes 32 | tf_op jit(solution)/shard_map/ppermute | solution.py:10
  16.0 8.6 %collective-permute-start.1 = (f32[2,256,256]{1,2,0:T(8,128)S(1)}, f32[2,256,256]{1,2,0:T(8,128)S(1)}, u32[]{:S(2)}, u32[]{:S(2)}) collective-permute-start(f32[2,256,256]{1,2,0:T(8,128)S(1)} %pad_dynamic-slice_fusion.8), channel_id=1, source_target_pairs={{4,0},{8,4},{12,8},{16,12},{20,16},{24,20},{28,24},{32,28},{36,32}... | collective-permute-start | bytes 1572872 | tf_op jit(solution)/shard_map/ppermute | solution.py:10
  24.6 19.2 %copy-start = (f32[2,256,256]{2,1,0:T(8,128)S(1)}, f32[2,256,256]{2,1,0:T(8,128)}, u32[]{:S(2)}) copy-start(f32[2,256,256]{2,1,0:T(8,128)} %param.7) | copy-start | bytes 1572868
  25.6 18.5 %copy-start.1 = (f32[256,256]{1,0:T(8,128)S(1)}, f32[256,256]{1,0:T(8,128)}, u32[]{:S(2)}) copy-start(f32[256,256]{1,0:T(8,128)} %param.8) | copy-start | bytes 786436
  25.6 11.3 %collective-permute-start.10 = (f32[2,256,256]{1,2,0:T(8,128)}, f32[2,256,256]{1,2,0:T(8,128)S(1)}, u32[]{:S(2)}, u32[]{:S(2)}) collective-permute-start(f32[2,256,256]{1,2,0:T(8,128)} %fusion.345), channel_id=1, source_target_pairs={{3,2},{7,6},{11,10},{15,14},{19,18},{23,22},{27,26},{31,30},{35,34... | collective-permute-start | bytes 1572872 | tf_op jit(solution)/shard_map/ppermute | solution.py:109
  26.4 16.1 %collective-permute-start.11 = (f32[2,256,256]{1,2,0:T(8,128)}, f32[2,256,256]{1,2,0:T(8,128)S(1)}, u32[]{:S(2)}, u32[]{:S(2)}) collective-permute-start(f32[2,256,256]{1,2,0:T(8,128)} %fusion.345), channel_id=1, source_target_pairs={{0,1},{4,5},{8,9},{12,13},{16,17},{20,21},{24,25},{28,29},{32,33},... | collective-permute-start | bytes 1572872 | tf_op jit(solution)/shard_map/ppermute | solution.py:109
  29.9 21.4 %collective-permute-start.12 = (f32[2,256,256]{1,2,0:T(8,128)}, f32[2,256,256]{1,2,0:T(8,128)S(1)}, u32[]{:S(2)}, u32[]{:S(2)}) collective-permute-start(f32[2,256,256]{1,2,0:T(8,128)} %fusion.345), channel_id=1, source_target_pairs={{0,2},{4,6},{8,10},{12,14},{16,18},{20,22},{24,26},{28,30},{32,34}... | collective-permute-start | bytes 1572872 | tf_op jit(solution)/shard_map/ppermute | solution.py:109
  32.7 22.3 %collective-permute-start.13 = (f32[2,256,256]{1,2,0:T(8,128)}, f32[2,256,256]{1,2,0:T(8,128)}, u32[]{:S(2)}, u32[]{:S(2)}) collective-permute-start(f32[2,256,256]{1,2,0:T(8,128)} %fusion.345), channel_id=1, source_target_pairs={{0,3},{4,7},{8,11},{12,15},{16,19},{20,23},{24,27},{28,31},{32,35}... | collective-permute-start | bytes 1572872 | tf_op jit(solution)/shard_map/ppermute | solution.py:109
  35.4 20.9 %collective-permute-start.2 = (f32[2,256,256]{1,2,0:T(8,128)}, f32[2,256,256]{1,2,0:T(8,128)}, u32[]{:S(2)}, u32[]{:S(2)}) collective-permute-start(f32[2,256,256]{1,2,0:T(8,128)} %fusion.345), channel_id=1, source_target_pairs={{1,2},{5,6},{9,10},{13,14},{17,18},{21,22},{25,26},{29,30},{33,34}... | collective-permute-start | bytes 1572872 | tf_op jit(solution)/shard_map/ppermute | solution.py:109
  36.9 20.2 %collective-permute-start.3 = (f32[2,256,256]{1,2,0:T(8,128)}, f32[2,256,256]{1,2,0:T(8,128)}, u32[]{:S(2)}, u32[]{:S(2)}) collective-permute-start(f32[2,256,256]{1,2,0:T(8,128)} %fusion.345), channel_id=1, source_target_pairs={{1,3},{5,7},{9,11},{13,15},{17,19},{21,23},{25,27},{29,31},{33,35}... | collective-permute-start | bytes 1572872 | tf_op jit(solution)/shard_map/ppermute | solution.py:109
  42.5 22.6 %collective-permute-start.4 = (f32[2,256,256]{1,2,0:T(8,128)}, f32[2,256,256]{1,2,0:T(8,128)}, u32[]{:S(2)}, u32[]{:S(2)}) collective-permute-start(f32[2,256,256]{1,2,0:T(8,128)} %fusion.345), channel_id=1, source_target_pairs={{1,0},{5,4},{9,8},{13,12},{17,16},{21,20},{25,24},{29,28},{33,32},... | collective-permute-start | bytes 1572872 | tf_op jit(solution)/shard_map/ppermute | solution.py:109
  51.3 17.0 %collective-permute-start.5 = (f32[2,256,256]{1,2,0:T(8,128)}, f32[2,256,256]{1,2,0:T(8,128)S(1)}, u32[]{:S(2)}, u32[]{:S(2)}) collective-permute-start(f32[2,256,256]{1,2,0:T(8,128)} %fusion.345), channel_id=1, source_target_pairs={{2,3},{6,7},{10,11},{14,15},{18,19},{22,23},{26,27},{30,31},{34,35... | collective-permute-start | bytes 1572872 | tf_op jit(solution)/shard_map/ppermute | solution.py:109
  55.0 22.7 %collective-permute-start.6 = (f32[2,256,256]{1,2,0:T(8,128)}, f32[2,256,256]{1,2,0:T(8,128)S(1)}, u32[]{:S(2)}, u32[]{:S(2)}) collective-permute-start(f32[2,256,256]{1,2,0:T(8,128)} %fusion.345), channel_id=1, source_target_pairs={{2,0},{6,4},{10,8},{14,12},{18,16},{22,20},{26,24},{30,28},{34,32}... | collective-permute-start | bytes 1572872 | tf_op jit(solution)/shard_map/ppermute | solution.py:109
  56.3 21.4 %collective-permute-start.7 = (f32[2,256,256]{1,2,0:T(8,128)}, f32[2,256,256]{1,2,0:T(8,128)S(1)}, u32[]{:S(2)}, u32[]{:S(2)}) collective-permute-start(f32[2,256,256]{1,2,0:T(8,128)} %fusion.345), channel_id=1, source_target_pairs={{2,1},{6,5},{10,9},{14,13},{18,17},{22,21},{26,25},{30,29},{34,33}... | collective-permute-start | bytes 1572872 | tf_op jit(solution)/shard_map/ppermute | solution.py:109
  57.0 23.3 %collective-permute-start.8 = (f32[2,256,256]{1,2,0:T(8,128)}, f32[2,256,256]{1,2,0:T(8,128)S(1)}, u32[]{:S(2)}, u32[]{:S(2)}) collective-permute-start(f32[2,256,256]{1,2,0:T(8,128)} %fusion.345), channel_id=1, source_target_pairs={{3,0},{7,4},{11,8},{15,12},{19,16},{23,20},{27,24},{31,28},{35,32}... | collective-permute-start | bytes 1572872 | tf_op jit(solution)/shard_map/ppermute | solution.py:109
  65.1 15.2 %collective-permute-start.9 = (f32[2,256,256]{1,2,0:T(8,128)}, f32[2,256,256]{1,2,0:T(8,128)S(1)}, u32[]{:S(2)}, u32[]{:S(2)}) collective-permute-start(f32[2,256,256]{1,2,0:T(8,128)} %fusion.345), channel_id=1, source_target_pairs={{3,1},{7,5},{11,9},{15,13},{19,17},{23,21},{27,25},{31,29},{35,33}... | collective-permute-start | bytes 1572872 | tf_op jit(solution)/shard_map/ppermute | solution.py:109
  110.3 13.8 %collective-permute-start.14 = (f32[2,256,256]{1,2,0:T(8,128)S(1)}, f32[2,256,256]{1,2,0:T(8,128)S(1)}, u32[]{:S(2)}, u32[]{:S(2)}) collective-permute-start(f32[2,256,256]{1,2,0:T(8,128)S(1)} %pad_dynamic-slice_fusion.7), channel_id=1, source_target_pairs={{0,4},{4,8},{8,12},{12,16},{16,20},{20,24},{24,28},{28,32},{32,36}... | collective-permute-start | bytes 1572872 | tf_op jit(solution)/shard_map/ppermute | solution.py:10

commit v2 on v1

--- a/solution.py
+++ b/solution.py
@@ -102,12 +102,10 @@
     kept = lax.dynamic_slice(kept, (zero, row, column), (2, width, width))
     window = kept + borrowed
 
-    layers = []
-    for layer in range(sections):
-        total = jnp.where(cut_index == layer, window, jnp.zeros_like(window))
-        for step in range(1, sections):
-            total = total + lax.ppermute(window, "cuts", [(layer, (layer + step) % sections)])
-        layers.append(total)
+    have = [window] + [rotated(window, "cuts", k) for k in range(1, sections)]
+    have = jnp.stack(have, axis=0)
+    order = (cut_index - lax.iota(jnp.int32, sections)) % sections
+    layers = jnp.take(have, order, axis=0)
 
     wave_real = probe[0]
     wave_imag = probe[1]

time: 129 us -> 108 us (0.84)
  waiting for transfers between devices: 51.3 us -> 36.8 us
  starting transfers between devices: 24.3 us -> 11.8 us
  local copies, waits for them, and re-layouts: 9.01 us -> 14.3 us
  other arithmetic: 12.4 us -> 14.8 us
    ppermute x12 -> x3, starting transfers between devices: 18.6 us -> 5.13 us  [rotated(): return lax.ppermute(value, axis, pairs)]
    ppermute x12 -> x3, waiting for transfers between devices: 29.8 us -> 17.5 us  [rotated(): return lax.ppermute(value, axis, pairs)]
    gather x0 -> x2, local copies, waits for them, and re-layouts: none -> 4.1 us  [per_device(): layers = jnp.take(have, order, axis=0)]
    convert_element_type x20, other arithmetic: 2.09 us -> 4.4 us  [halves(): return (high.astype(jnp.bfloat16), low.astype(jnp.bfloat16))]
    ppermute x3, waiting for transfers between devices: 21.5 us -> 19.3 us  [shifted(): return lax.ppermute(value, axis, pairs)]
    add x1 -> x0, other arithmetic: 2.12 us -> none  [per_device(): total + lax.ppermute(window, 'cuts', [(layer, (layer + step) % sections)])]
    unnamed x9 -> x28, local copies, waits for them, and re-layouts: 3.4 us -> 5.22 us
    another operation x0 -> x1, other arithmetic: none -> 1.74 us  [per_device(): have = jnp.stack(have, axis=0)]
  transfers between devices with their start and end apart: 15 -> 6, of which waited for: 9 -> 5; matrix products, arithmetic and copies ran while one was open for 6% -> 9% of each run, Pallas kernels for 0% -> 0%
where the time goes in v2:
time: 108 us; the launch traced here: 107 us
  waiting for transfers between devices  36.8 us (34%)
  matrix products  22.5 us (21%)
  other arithmetic  14.8 us (14%)
  local copies, waits for them, and re-layouts  14.3 us (13%)
  starting transfers between devices  11.8 us (11%)
  between operations  7.25 us (7%)
    ppermute x3, waiting for transfers between devices, shifted(): return lax.ppermute(value, axis, pairs)  19.3 us
    ppermute x3, waiting for transfers between devices, rotated(): return lax.ppermute(value, axis, pairs)  17.5 us
    dot_general x18, matrix products, split_dot(): return jnp.dot(operand, split_table, preferred_element_type=jnp.float32)  11.3 us
    dot_general x18, matrix products, split_dot(): return jnp.dot(split_table, operand, preferred_element_type=jnp.float32)  11.2 us
    ppermute x3, starting transfers between devices, shifted(): return lax.ppermute(value, axis, pairs)  6.64 us
    unnamed x28, local copies, waits for them, and re-layouts  5.22 us
    ppermute x3, starting transfers between devices, rotated(): return lax.ppermute(value, axis, pairs)  5.13 us
    convert_element_type x20, other arithmetic, halves(): return (high.astype(jnp.bfloat16), low.astype(jnp.bfloat16))  4.4 us
  transfers between devices with their start and end apart: 6, of which 5 were waited for; matrix products, arithmetic and copies ran while one was open for 9% of the time, Pallas kernels for 0%

profile of v2, /device:TPU:128, one launch (start us, length us, event | category | flops | bytes accessed | tf_op | source)
XLA Modules:
  0.0 107.4 jit_solution(2370495670573374855)
XLA Ops:
  1.4 1.9 %collective-permute-start = (s32[2]{0:T(128)S(1)}, s32[2]{0:T(128)S(1)}, u32[]{:S(2)}, u32[]{:S(2)}) collective-permute-start(s32[2]{0:T(128)S(1)} %pad_add_fusion), channel_id=1, source_target_pairs={{0,4},{4,8},{8,12},{12,16},{16,20},{20,24},{24,28},{28,32},{32,36}... | collective-permute-start | bytes 32 | tf_op jit(solution)/shard_map/ppermute | solution.py:10
  3.3 1.1 cosine_multiply_fusion
  4.3 1.0 fusion.362
  5.3 4.2 %collective-permute-done = s32[2]{0:T(128)S(1)} collective-permute-done((s32[2]{0:T(128)S(1)}, s32[2]{0:T(128)S(1)}, u32[]{:S(2)}, u32[]{:S(2)}) %collective-permute-start) | collective-permute-done | bytes 40 | tf_op jit(solution)/shard_map/ppermute | solution.py:10
  9.5 0.6 fusion.404
  13.3 1.3 %dynamic-slice_bitcast_fusion = f32[2,256,256]{2,1,0:T(8,128)S(1)} fusion(f32[1,2,256,1024]{3,2,1,0:T(8,128)} %param.6, s32[]{:T(128)S(6)} %select_n.104), kind=kLoop, calls=%fused_computation.430 | loop fusion | bytes 1048580 | tf_op jit(solution)/shard_map/dynamic_slice | solution.py:97
  15.4 2.8 %collective-permute-start.1 = (f32[2,256,256]{2,1,0:T(8,128)S(1)}, f32[2,256,256]{2,1,0:T(8,128)}, u32[]{:S(2)}, u32[]{:S(2)}) collective-permute-start(f32[2,256,256]{2,1,0:T(8,128)S(1)} %pad_dynamic-slice_fusion.8), channel_id=1, source_target_pairs={{4,0},{8,4},{12,8},{16,12},{20,16},{24,20},{28,24},{32,28},{36,32}... | collective-permute-start | bytes 1572872 | tf_op jit(solution)/shard_map/ppermute | solution.py:10
  18.3 1.0 broadcast_multiply_fusion.1
  19.3 1.1 %fusion.334 = (bf16[256,512]{1,0:T(8,128)(2,1)}, bf16[256,512]{1,0:T(8,128)(2,1)}, bf16[256,512]{1,0:T(8,128)(2,1)}, bf16[256,512]{1,0:T(8,128)(2,1)}) fusion(f32[256,256]{1,0:T(8,128)S(1)} %get-tuple-element.161, f32[256,256]{1,0:T(8,128)S(1)} %get-tuple-element.159, f32[256,256]{1,0:T(8,128)S(1)} %get-tuple-element.160), kind=kLoop, calls=%fused_computation.396 | loop fusion | flops 1835008 | bytes 1835008 | tf_op jit(solution)/shard_map/convert_element_type | solution.py:31
  20.5 4.5 %collective-permute-done.1 = f32[2,256,256]{2,1,0:T(8,128)} collective-permute-done((f32[2,256,256]{2,1,0:T(8,128)S(1)}, f32[2,256,256]{2,1,0:T(8,128)}, u32[]{:S(2)}, u32[]{:S(2)}) %collective-permute-start.1) | collective-permute-done | bytes 524320 | tf_op jit(solution)/shard_map/ppermute | solution.py:10
  24.9 1.3 %fusion.345 = f32[2,256,256]{2,1,0:T(8,128)S(1)} fusion(f32[2,256,256]{2,1,0:T(8,128)} %collective-permute-done.1, s32[]{:T(128)S(6)} %select_n.102, s32[]{:T(128)S(6)} %select_n.103, f32[2,256,1024]{2,1,0:T(8,128)S(1)} %bitcast.160), kind=kLoop, calls=%fused_computation.407 | loop fusion | flops 131072 | bytes 3145736 | tf_op jit(solution)/shard_map/add | solution.py:103
  26.2 2.8 %collective-permute-start.4 = (f32[2,256,256]{2,1,0:T(8,128)S(1)}, f32[2,256,256]{2,1,0:T(8,128)S(1)}, u32[]{:S(2)}, u32[]{:S(2)}) collective-permute-start(f32[2,256,256]{2,1,0:T(8,128)S(1)} %fusion.345), channel_id=1, source_target_pairs={{0,3},{1,0},{2,1},{3,2},{4,7},{5,4},{6,5},{7,6},{8,11},{9,8},{10,9... | collective-permute-start | bytes 1572872 | tf_op jit(solution)/shard_map/ppermute | solution.py:16
  29.0 2.3 %collective-permute-start.3 = (f32[2,256,256]{2,1,0:T(8,128)S(1)}, f32[2,256,256]{2,1,0:T(8,128)}, u32[]{:S(2)}, u32[]{:S(2)}) collective-permute-start(f32[2,256,256]{2,1,0:T(8,128)S(1)} %fusion.345), channel_id=1, source_target_pairs={{0,2},{1,3},{2,0},{3,1},{4,6},{5,7},{6,4},{7,5},{8,10},{9,11},{10,... | collective-permute-start | bytes 1572872 | tf_op jit(solution)/shard_map/ppermute | solution.py:16
  31.6 1.1 %copy.90 = f32[256,256]{0,1:T(8,128)S(1)} copy(f32[256,256]{1,0:T(8,128)} %param.8) | data formatting | bytes 524288 | tf_op args[2]
  32.7 1.1 %copy.126 = f32[1,256,256]{1,2,0:T(8,128)S(1)} copy(f32[1,256,256]{2,1,0:T(8,128)} %param.11) | data formatting | bytes 524288 | tf_op args[5]
  33.8 1.6 %fusion.3 = (bf16[512,512]{1,0:T(8,128)(2,1)}, bf16[512,512]{1,0:T(8,128)(2,1)}, bf16[512,512]{1,0:T(8,128)(2,1)}, bf16[512,512]{1,0:T(8,128)(2,1)}) fusion(f32[256,256]{1,0:T(8,128)S(1)} %get-tuple-element.159, f32[256,256]{1,0:T(8,128)S(1)} %get-tuple-element.161, f32[256,256]{1,0:T(8,128)S(1)} %get-tuple-element.162, ...), kind=kLoop, calls=%fused_computation.16 | loop fusion | flops 4718592 | bytes 3407872 | tf_op jit(solution)/shard_map/convert_element_type | solution.py:31
  35.5 0.9 fusion.403
  36.4 14.0 %collective-permute-done.4 = f32[2,256,256]{2,1,0:T(8,128)S(1)} collective-permute-done((f32[2,256,256]{2,1,0:T(8,128)S(1)}, f32[2,256,256]{2,1,0:T(8,128)S(1)}, u32[]{:S(2)}, u32[]{:S(2)}) %collective-permute-start.4) | collective-permute-done | bytes 524320 | tf_op jit(solution)/shard_map/ppermute | solution.py:16
  50.4 3.5 %collective-permute-done.2 = f32[2,256,256]{2,1,0:T(8,128)} collective-permute-done((f32[2,256,256]{2,1,0:T(8,128)S(1)}, f32[2,256,256]{2,1,0:T(8,128)}, u32[]{:S(2)}, u32[]{:S(2)}) %collective-permute-start.2) | collective-permute-done | bytes 524320 | tf_op jit(solution)/shard_map/ppermute | solution.py:16
  53.9 1.7 %pad_maximum_fusion = f32[4,2,256,256]{3,2,1,0:T(8,128)S(1)} fusion(f32[1,2,256,256]{3,2,1,0:T(8,128)} %bitcast.162, f32[1,2,256,256]{3,2,1,0:T(8,128)} %bitcast.9, f32[1,2,256,256]{3,2,1,0:T(8,128)} %bitcast.8, f32[1,2,256,256]{3,2,1,0:T(8,128)} %bitcast.161), kind=kLoop, calls=%fused_computation.6 | loop fusion | flops 1572864 | bytes 4194304 | tf_op jit(solution)/shard_map/stack | solution.py:106
  55.6 2.0 %gather_fusion = f32[4,2,256,256]{3,2,1,0:T(8,128)} fusion(f32[4,2,256,256]{3,2,1,0:T(8,128)S(1)} %pad_maximum_fusion, s32[1024]{0:T(1024)S(1)} %pad_clamp_fusion), kind=kCustom, calls=%fused_computation | custom fusion | bytes 4194320 | tf_op jit(solution)/shard_map/jit(_take)/gather | solution.py:108
  57.6 2.1 %copy.86 = f32[4,2,256,256]{2,3,1,0:T(8,128)S(1)} copy(f32[4,2,256,256]{3,2,1,0:T(8,128)} %gather_fusion) | data formatting | bytes 4194304 | tf_op jit(solution)/shard_map/jit(_take)/gather | solution.py:108
  60.2 0.8 copy-done.5
  61.2 0.6 fusion.229
  62.2 0.6 fusion.16
  63.1 0.8 copy-done.3
  64.0 0.6 fusion.235
  65.1 0.6 fusion.28
  66.0 0.6 fusion.241
  66.6 0.6 fusion.40
  67.4 0.6 fusion.245
  68.1 0.6 fusion.52
  69.0 0.6 fusion.249
  69.6 0.6 fusion.64
  70.4 0.6 fusion.253
  71.1 0.6 fusion.76
  72.0 0.6 fusion.257
  72.6 0.6 fusion.88
  73.5 0.6 fusion.261
  74.1 0.6 fusion.100
  74.9 0.6 fusion.265
  75.5 0.6 fusion.112
  76.3 0.6 fusion.269
  77.0 0.6 fusion.124
  77.8 0.6 fusion.273
  78.4 0.8 fusion.136
  79.4 0.6 fusion.277
  80.1 0.6 fusion.148
  81.0 0.6 fusion.281
  81.6 0.6 fusion.160
  82.5 0.6 fusion.285
  83.1 0.6 fusion.172
  84.1 0.6 fusion.289
  84.7 0.6 fusion.184
  85.5 0.6 fusion.293
  86.2 0.6 fusion.196
  87.1 0.6 fusion.297
  87.7 0.6 fusion.208
  88.6 0.6 fusion.301
  89.2 0.6 fusion.220
  90.5 1.9 %collective-permute-start.5 = (f32[2,256,256]{1,2,0:T(8,128)S(1)}, f32[2,256,256]{1,2,0:T(8,128)S(1)}, u32[]{:S(2)}, u32[]{:S(2)}) collective-permute-start(f32[2,256,256]{1,2,0:T(8,128)S(1)} %pad_dynamic-slice_fusion.7), channel_id=1, source_target_pairs={{0,4},{4,8},{8,12},{12,16},{16,20},{20,24},{24,28},{28,32},{32,36}... | collective-permute-start | bytes 1572872 | tf_op jit(solution)/shard_map/ppermute | solution.py:10
  93.7 10.6 %collective-permute-done.5 = f32[2,256,256]{1,2,0:T(8,128)S(1)} collective-permute-done((f32[2,256,256]{1,2,0:T(8,128)S(1)}, f32[2,256,256]{1,2,0:T(8,128)S(1)}, u32[]{:S(2)}, u32[]{:S(2)}) %collective-permute-start.5) | collective-permute-done | bytes 524320 | tf_op jit(solution)/shard_map/ppermute | solution.py:10
  104.3 1.3 %fusion.1 = f32[1,2,256,1024]{2,3,1,0:T(8,128)S(1)} fusion(s32[]{:T(128)S(6)} %select_n.113, f32[2,256,256]{1,2,0:T(8,128)S(1)} %collective-permute-done.5, s32[]{:T(128)S(6)} %select_n.110, s32[]{:T(128)S(6)} %select_n.111, f32[2,256,256]{1,2,0:T(8,128)S(1)} %fusion.344), kind=kLoop, calls=%fused_computation.5 | loop fusion | flops 524288 | bytes 3145740 | tf_op jit(solution)/shard_map/broadcast_in_dim | solution.py:152
  105.6 1.8 %copy.163 = f32[1,2,256,1024]{3,2,1,0:T(8,128)} copy(f32[1,2,256,1024]{2,3,1,0:T(8,128)S(1)} %fusion.1) | data formatting | bytes 4194304 | tf_op jit(solution)/shard_map/broadcast_in_dim | solution.py:152
  (82 shorter events, 6.5 us)
Async XLA Ops:
  1.4 8.2 %collective-permute-start = (s32[2]{0:T(128)S(1)}, s32[2]{0:T(128)S(1)}, u32[]{:S(2)}, u32[]{:S(2)}) collective-permute-start(s32[2]{0:T(128)S(1)} %pad_add_fusion), channel_id=1, source_target_pairs={{0,4},{4,8},{8,12},{12,16},{16,20},{20,24},{24,28},{28,32},{32,36}... | collective-permute-start | bytes 32 | tf_op jit(solution)/shard_map/ppermute | solution.py:10
  15.3 5.1 %copy-start.2 = (f32[2,256,256]{2,1,0:T(8,128)S(1)}, f32[2,256,256]{2,1,0:T(8,128)}, u32[]{:S(2)}) copy-start(f32[2,256,256]{2,1,0:T(8,128)} %param.7) | copy-start | bytes 1572868
  15.4 9.5 %collective-permute-start.1 = (f32[2,256,256]{2,1,0:T(8,128)S(1)}, f32[2,256,256]{2,1,0:T(8,128)}, u32[]{:S(2)}, u32[]{:S(2)}) collective-permute-start(f32[2,256,256]{2,1,0:T(8,128)S(1)} %pad_dynamic-slice_fusion.8), channel_id=1, source_target_pairs={{4,0},{8,4},{12,8},{16,12},{20,16},{24,20},{28,24},{32,28},{36,32}... | collective-permute-start | bytes 1572872 | tf_op jit(solution)/shard_map/ppermute | solution.py:10
  19.3 5.7 %copy-start = (f32[1,2,256,1024]{3,2,1,0:T(8,128)S(1)}, f32[1,2,256,1024]{3,2,1,0:T(8,128)}, u32[]{:S(2)}) copy-start(f32[1,2,256,1024]{3,2,1,0:T(8,128)} %param.6) | copy-start | bytes 6291460
  26.2 9.3 %copy-start.1 = (f32[2,256,256]{2,1,0:T(8,128)}, f32[2,256,256]{2,1,0:T(8,128)S(1)}, u32[]{:S(2)}) copy-start(f32[2,256,256]{2,1,0:T(8,128)S(1)} %fusion.345) | copy-start | bytes 1572868
  26.2 24.2 %collective-permute-start.4 = (f32[2,256,256]{2,1,0:T(8,128)S(1)}, f32[2,256,256]{2,1,0:T(8,128)S(1)}, u32[]{:S(2)}, u32[]{:S(2)}) collective-permute-start(f32[2,256,256]{2,1,0:T(8,128)S(1)} %fusion.345), channel_id=1, source_target_pairs={{0,3},{1,0},{2,1},{3,2},{4,7},{5,4},{6,5},{7,6},{8,11},{9,8},{10,9... | collective-permute-start | bytes 1572872 | tf_op jit(solution)/shard_map/ppermute | solution.py:16
  29.0 24.8 %collective-permute-start.2 = (f32[2,256,256]{2,1,0:T(8,128)S(1)}, f32[2,256,256]{2,1,0:T(8,128)}, u32[]{:S(2)}, u32[]{:S(2)}) collective-permute-start(f32[2,256,256]{2,1,0:T(8,128)S(1)} %fusion.345), channel_id=1, source_target_pairs={{0,1},{1,2},{2,3},{3,0},{4,5},{5,6},{6,7},{7,4},{8,9},{9,10},{10,1... | collective-permute-start | bytes 1572872 | tf_op jit(solution)/shard_map/ppermute | solution.py:16
  29.0 24.8 %collective-permute-start.3 = (f32[2,256,256]{2,1,0:T(8,128)S(1)}, f32[2,256,256]{2,1,0:T(8,128)}, u32[]{:S(2)}, u32[]{:S(2)}) collective-permute-start(f32[2,256,256]{2,1,0:T(8,128)S(1)} %fusion.345), channel_id=1, source_target_pairs={{0,2},{1,3},{2,0},{3,1},{4,6},{5,7},{6,4},{7,5},{8,10},{9,11},{10,... | collective-permute-start | bytes 1572872 | tf_op jit(solution)/shard_map/ppermute | solution.py:16
  50.4 3.5 %copy-start.7 = (f32[2,256,256]{2,1,0:T(8,128)}, f32[2,256,256]{2,1,0:T(8,128)S(1)}, u32[]{:S(2)}) copy-start(f32[2,256,256]{2,1,0:T(8,128)S(1)} %collective-permute-done.4) | copy-start | bytes 1572868
  60.0 1.0 copy-start.5
  60.0 1.2 %copy-start.6 = (bf16[512,512]{1,0:T(8,128)(2,1)S(1)}, bf16[512,512]{1,0:T(8,128)(2,1)}, u32[]{:S(2)}) copy-start(bf16[512,512]{1,0:T(8,128)(2,1)} %get-tuple-element.154) | copy-start | bytes 1572868
  61.2 0.9 copy-start.10
  61.2 1.0 copy-start.11
  62.8 1.0 copy-start.3
  62.8 1.2 %copy-start.4 = (bf16[512,512]{1,0:T(8,128)(2,1)S(1)}, bf16[512,512]{1,0:T(8,128)(2,1)}, u32[]{:S(2)}) copy-start(bf16[512,512]{1,0:T(8,128)(2,1)} %get-tuple-element.67) | copy-start | bytes 1572868
  64.0 0.9 copy-start.8
  64.0 1.0 copy-start.9
  90.5 13.8 %collective-permute-start.5 = (f32[2,256,256]{1,2,0:T(8,128)S(1)}, f32[2,256,256]{1,2,0:T(8,128)S(1)}, u32[]{:S(2)}, u32[]{:S(2)}) collective-permute-start(f32[2,256,256]{1,2,0:T(8,128)S(1)} %pad_dynamic-slice_fusion.7), channel_id=1, source_target_pairs={{0,4},{4,8},{8,12},{12,16},{16,20},{20,24},{24,28},{28,32},{32,36}... | collective-permute-start | bytes 1572872 | tf_op jit(solution)/shard_map/ppermute | solution.py:10

commit v3 on v2

--- a/solution.py
+++ b/solution.py
@@ -102,10 +102,17 @@
     kept = lax.dynamic_slice(kept, (zero, row, column), (2, width, width))
     window = kept + borrowed
 
-    have = [window] + [rotated(window, "cuts", k) for k in range(1, sections)]
-    have = jnp.stack(have, axis=0)
-    order = (cut_index - lax.iota(jnp.int32, sections)) % sections
-    layers = jnp.take(have, order, axis=0)
+    if sections == 4:
+        from_left = rotated(window, "cuts", 1)
+        from_right = rotated(window, "cuts", -1)
+        far_real = rotated(from_right[0], "cuts", -1)
+        far_imag = rotated(from_left[1], "cuts", 1)
+        have = [window, from_left, jnp.stack([far_real, far_imag], axis=0), from_right]
+    else:
+        have = [window] + [rotated(window, "cuts", k) for k in range(1, sections)]
+    layers = [
+        lax.select_n((cut_index - layer) % sections, *have) for layer in range(sections)
+    ]
 
     wave_real = probe[0]
     wave_imag = probe[1]

time: 108 us -> 99.5 us (0.921)
  waiting for transfers between devices: 36.8 us -> 27.4 us
    ppermute x3 -> x4, waiting for transfers between devices: 17.5 us -> 7.84 us  [rotated(): return lax.ppermute(value, axis, pairs)]
    gather x2 -> x0, local copies, waits for them, and re-layouts: 4.1 us -> none  [per_device(): layers = jnp.take(have, order, axis=0)]
    select_n x2, other arithmetic: 0.26 us -> 2.21 us  [per_device(): lax.select_n((cut_index - layer) % sections, *have)]
    unnamed x28 -> x23, local copies, waits for them, and re-layouts: 5.22 us -> 7.13 us
    another operation x1 -> x0, other arithmetic: 1.74 us -> none  [per_device(): have = jnp.stack(have, axis=0)]
    ppermute x3 -> x4, starting transfers between devices: 5.13 us -> 6.63 us  [rotated(): return lax.ppermute(value, axis, pairs)]
    squeeze x0 -> x2, local copies, waits for them, and re-layouts: none -> 1.44 us  [the longest x1 0.72 us: per_device(): far_real = rotated(from_right[0], 'cuts', -1)]
  transfers between devices with their start and end apart: 6 -> 7, of which waited for: 5 -> 5; matrix products, arithmetic and copies ran while one was open for 9% -> 13% of each run, Pallas kernels for 0% -> 0%
where the time goes in v3:
time: 99.5 us; the launch traced here: 98.5 us
  waiting for transfers between devices  27.4 us (28%)
  matrix products  22.5 us (23%)
  other arithmetic  14.9 us (15%)
  local copies, waits for them, and re-layouts  14.1 us (14%)
  starting transfers between devices  12.4 us (12%)
  between operations  7.19 us (7%)
    ppermute x3, waiting for transfers between devices, shifted(): return lax.ppermute(value, axis, pairs)  19.5 us
    dot_general x18, matrix products, split_dot(): return jnp.dot(split_table, operand, preferred_element_type=jnp.float32)  11.4 us
    dot_general x18, matrix products, split_dot(): return jnp.dot(operand, split_table, preferred_element_type=jnp.float32)  11.1 us
    ppermute x4, waiting for transfers between devices, rotated(): return lax.ppermute(value, axis, pairs)  7.84 us
    unnamed x23, local copies, waits for them, and re-layouts  7.13 us
    ppermute x4, starting transfers between devices, rotated(): return lax.ppermute(value, axis, pairs)  6.63 us
    ppermute x3, starting transfers between devices, shifted(): return lax.ppermute(value, axis, pairs)  5.75 us
    convert_element_type x20, other arithmetic, halves(): return (high.astype(jnp.bfloat16), low.astype(jnp.bfloat16))  4.29 us
  transfers between devices with their start and end apart: 7, of which 5 were waited for; matrix products, arithmetic and copies ran while one was open for 13% of the time, Pallas kernels for 0%

profile of v3, /device:TPU:128, one launch (start us, length us, event | category | flops | bytes accessed | tf_op | source)
XLA Modules:
  0.0 98.5 jit_solution(17788571705244732596)
XLA Ops:
  1.4 1.9 %collective-permute-start = (s32[2]{0:T(128)S(1)}, s32[2]{0:T(128)S(1)}, u32[]{:S(2)}, u32[]{:S(2)}) collective-permute-start(s32[2]{0:T(128)S(1)} %pad_add_fusion), channel_id=1, source_target_pairs={{0,4},{4,8},{8,12},{12,16},{16,20},{20,24},{24,28},{28,32},{32,36}... | collective-permute-start | bytes 32 | tf_op jit(solution)/shard_map/ppermute | solution.py:10
  3.3 6.3 %collective-permute-done = s32[2]{0:T(128)S(1)} collective-permute-done((s32[2]{0:T(128)S(1)}, s32[2]{0:T(128)S(1)}, u32[]{:S(2)}, u32[]{:S(2)}) %collective-permute-start) | collective-permute-done | bytes 40 | tf_op jit(solution)/shard_map/ppermute | solution.py:10
  9.5 0.6 fusion.401
  12.1 1.3 %constant_dynamic-slice_fusion = f32[1,2,256,256]{3,2,1,0:T(8,128)S(1)} fusion(f32[1,2,256,1024]{3,2,1,0:T(8,128)} %param.6, s32[]{:T(128)S(6)} %select_n.196), kind=kLoop, calls=%fused_computation.544 | loop fusion | bytes 1048580 | tf_op jit(solution)/shard_map/dynamic_slice | solution.py:97
  15.8 1.9 %collective-permute-start.1 = (f32[2,256,256]{1,2,0:T(8,128)S(1)}, f32[2,256,256]{1,2,0:T(8,128)}, u32[]{:S(2)}, u32[]{:S(2)}) collective-permute-start(f32[2,256,256]{1,2,0:T(8,128)S(1)} %pad_dynamic-slice_fusion.8), channel_id=1, source_target_pairs={{4,0},{8,4},{12,8},{16,12},{20,16},{24,20},{28,24},{32,28},{36,32}... | collective-permute-start | bytes 1572872 | tf_op jit(solution)/shard_map/ppermute | solution.py:10
  17.7 1.9 %copy.8 = f32[1,2,256,1024]{2,3,1,0:T(8,128)S(1)} copy(f32[1,2,256,1024]{3,2,1,0:T(8,128)} %param.6) | data formatting | bytes 4194304 | tf_op args[0]
  19.7 1.1 %cosine_multiply_fusion = (f32[256,256]{1,0:T(8,128)S(1)}, f32[256,256]{1,0:T(8,128)S(1)}) fusion(), kind=kLoop, calls=%fused_computation.535 | loop fusion | flops 1048576 | bytes 524288 | tf_op jit(solution)/shard_map/mul | solution.py:24
  20.7 1.0 %broadcast_multiply_fusion.1 = (f32[256,256]{1,0:T(8,128)S(1)}, f32[256,256]{1,0:T(8,128)S(1)}) fusion(), kind=kLoop, calls=%fused_computation.540 | loop fusion | flops 1048576 | bytes 524288 | tf_op jit(solution)/shard_map/mul | solution.py:24
  21.7 2.7 %collective-permute-done.1 = f32[2,256,256]{1,2,0:T(8,128)} collective-permute-done((f32[2,256,256]{1,2,0:T(8,128)S(1)}, f32[2,256,256]{1,2,0:T(8,128)}, u32[]{:S(2)}, u32[]{:S(2)}) %collective-permute-start.1) | collective-permute-done | bytes 524320 | tf_op jit(solution)/shard_map/ppermute | solution.py:10
  24.4 1.2 %fusion.345 = f32[2,256,256]{1,2,0:T(8,128)S(1)} fusion(f32[2,256,256]{1,2,0:T(8,128)} %collective-permute-done.1, s32[]{:T(128)S(6)} %select_n.194, s32[]{:T(128)S(6)} %select_n.195, f32[2,256,1024]{1,2,0:T(8,128)S(1)} %bitcast.159), kind=kLoop, calls=%fused_computation.404 | loop fusion | flops 131072 | bytes 3145736 | tf_op jit(solution)/shard_map/add | solution.py:103
  25.6 1.6 %collective-permute-start.2 = (f32[2,256,256]{1,2,0:T(8,128)S(1)}, f32[2,256,256]{1,2,0:T(8,128)S(1)}, u32[]{:S(2)}, u32[]{:S(2)}) collective-permute-start(f32[2,256,256]{1,2,0:T(8,128)S(1)} %fusion.345), channel_id=1, source_target_pairs={{0,1},{1,2},{2,3},{3,0},{4,5},{5,6},{6,7},{7,4},{8,9},{9,10},{10,1... | collective-permute-start | bytes 1572872 | tf_op jit(solution)/shard_map/ppermute | solution.py:16
  27.2 1.0 fusion.362
  28.2 1.8 %collective-permute-start.3 = (f32[2,256,256]{1,2,0:T(8,128)S(1)}, f32[2,256,256]{1,2,0:T(8,128)S(1)}, u32[]{:S(2)}, u32[]{:S(2)}) collective-permute-start(f32[2,256,256]{1,2,0:T(8,128)S(1)} %fusion.345), channel_id=1, source_target_pairs={{0,3},{1,0},{2,1},{3,2},{4,7},{5,4},{6,5},{7,6},{8,11},{9,8},{10,9... | collective-permute-start | bytes 1572872 | tf_op jit(solution)/shard_map/ppermute | solution.py:16
  30.0 1.6 %fusion.3 = (bf16[512,512]{1,0:T(8,128)(2,1)}, bf16[512,512]{1,0:T(8,128)(2,1)}, bf16[512,512]{1,0:T(8,128)(2,1)}, bf16[512,512]{1,0:T(8,128)(2,1)}) fusion(f32[256,256]{1,0:T(8,128)S(1)} %get-tuple-element.162, f32[256,256]{1,0:T(8,128)S(1)} %get-tuple-element.164, f32[256,256]{1,0:T(8,128)S(1)} %get-tuple-element.165, ...), kind=kLoop, calls=%fused_computation.14 | loop fusion | flops 4718592 | bytes 3407872 | tf_op jit(solution)/shard_map/convert_element_type | solution.py:31
  31.6 7.8 %collective-permute-done.2 = f32[2,256,256]{1,2,0:T(8,128)S(1)} collective-permute-done((f32[2,256,256]{1,2,0:T(8,128)S(1)}, f32[2,256,256]{1,2,0:T(8,128)S(1)}, u32[]{:S(2)}, u32[]{:S(2)}) %collective-permute-start.2) | collective-permute-done | bytes 524320 | tf_op jit(solution)/shard_map/ppermute | solution.py:16
  39.4 0.7 slice_bitcast_fusion.8
  40.5 0.7 slice_bitcast_fusion.9
  41.2 3.0 %collective-permute-start.4 = (f32[256,256]{0,1:T(8,128)}, f32[256,256]{0,1:T(8,128)}, u32[]{:S(2)}, u32[]{:S(2)}) collective-permute-start(f32[256,256]{0,1:T(8,128)} %slice_bitcast_fusion.9), channel_id=1, source_target_pairs={{0,3},{1,0},{2,1},{3,2},{4,7},{5,4},{6,5},{7,6},{8,11},{9,8},{10,9... | collective-permute-start | bytes 786440 | tf_op jit(solution)/shard_map/ppermute | solution.py:16
  44.1 1.1 %fusion.334 = (bf16[256,512]{1,0:T(8,128)(2,1)}, bf16[256,512]{1,0:T(8,128)(2,1)}, bf16[256,512]{1,0:T(8,128)(2,1)}, bf16[256,512]{1,0:T(8,128)(2,1)}) fusion(f32[256,256]{1,0:T(8,128)S(1)} %get-tuple-element.164, f32[256,256]{1,0:T(8,128)S(1)} %get-tuple-element.162, f32[256,256]{1,0:T(8,128)S(1)} %get-tuple-element.163), kind=kLoop, calls=%fused_computation.393 | loop fusion | flops 1835008 | bytes 1835008 | tf_op jit(solution)/shard_map/convert_element_type | solution.py:31
  45.5 1.1 %copy.13 = f32[256,256]{0,1:T(8,128)S(1)} copy(f32[256,256]{1,0:T(8,128)} %param.8) | data formatting | bytes 524288 | tf_op args[2]
  46.6 1.1 %copy.49 = f32[1,256,256]{1,2,0:T(8,128)S(1)} copy(f32[1,256,256]{2,1,0:T(8,128)} %param.11) | data formatting | bytes 524288 | tf_op args[5]
  47.7 1.1 %fusion.400 = (f32[256,256]{0,1:T(8,128)S(1)}, f32[256,256]{0,1:T(8,128)S(1)}) fusion(f32[256,256]{0,1:T(8,128)S(1)} %copy.13), kind=kLoop, calls=%fused_computation.583 | loop fusion | bytes 786432 | tf_op jit(solution)/shard_map/sin | solution.py:88
  48.8 1.1 %select_select_fusion.1 = (f32[2,256,256]{1,2,0:T(8,128)S(1)}, f32[2,256,256]{1,2,0:T(8,128)S(1)}, f32[2,256,256]{1,2,0:T(8,128)S(1)}) fusion(f32[2,256,256]{1,2,0:T(8,128)S(1)} %collective-permute-done.3, f32[2,256,256]{1,2,0:T(8,128)S(1)} %fusion.345, f32[2,256,256]{1,2,0:T(8,128)S(1)} %collective-permute-done.2, pred[]{:T(512)S(6)} %select_n.219, ...), kind=kLoop, calls=%fused_computation.429 | loop fusion | flops 1310720 | bytes 3670025 | tf_op jit(solution)/shard_map/select_n | solution.py:114
  50.2 0.8 copy-done.3
  51.2 0.6 fusion.229
  52.2 0.6 fusion.16
  53.1 0.8 copy-done.1
  54.0 0.6 fusion.235
  55.1 0.6 fusion.28
  55.7 1.1 %select_select_fusion.3 = f32[2,256,256]{1,2,0:T(8,128)S(1)} fusion(f32[2,256,256]{1,2,0:T(8,128)S(1)} %collective-permute-done.3, f32[2,256,256]{1,2,0:T(8,128)S(1)} %fusion.345, f32[2,256,256]{1,2,0:T(8,128)S(1)} %collective-permute-done.2, pred[]{:T(512)S(6)} %select_n.199, pred[]{:T(512)S(6)} %select_n.192, pred[]{:T(512)S(6)} %select_n.190, ...), kind=kLoop, calls=%fused_computation.431 | loop fusion | flops 524288 | bytes 2621443 | tf_op jit(solution)/shard_map/select_n | solution.py:114
  57.1 0.6 fusion.241
  57.7 0.6 fusion.40
  58.5 0.6 fusion.245
  59.2 0.6 fusion.52
  60.1 0.6 fusion.249
  60.7 0.6 fusion.64
  61.5 0.6 fusion.253
  62.2 0.6 fusion.76
  63.1 0.6 fusion.257
  63.7 0.6 fusion.88
  64.5 0.6 fusion.261
  65.2 0.6 fusion.100
  66.0 0.6 fusion.265
  66.6 0.6 fusion.112
  67.4 0.6 fusion.269
  68.0 0.6 fusion.124
  68.8 0.8 fusion.273
  69.7 0.6 fusion.136
  70.5 0.6 fusion.277
  71.2 0.6 fusion.148
  72.1 0.6 fusion.281
  73.6 0.6 fusion.285
  74.2 0.6 fusion.172
  75.1 0.6 fusion.289
  75.8 0.6 fusion.184
  76.6 0.6 fusion.293
  77.2 0.6 fusion.196
  78.2 0.6 fusion.297
  79.7 0.6 fusion.301
  80.3 0.6 fusion.220
  81.6 1.9 %collective-permute-start.6 = (f32[2,256,256]{1,2,0:T(8,128)S(1)}, f32[2,256,256]{1,2,0:T(8,128)S(1)}, u32[]{:S(2)}, u32[]{:S(2)}) collective-permute-start(f32[2,256,256]{1,2,0:T(8,128)S(1)} %pad_dynamic-slice_fusion.7), channel_id=1, source_target_pairs={{0,4},{4,8},{8,12},{12,16},{16,20},{20,24},{24,28},{28,32},{32,36}... | collective-permute-start | bytes 1572872 | tf_op jit(solution)/shard_map/ppermute | solution.py:10
  84.8 10.6 %collective-permute-done.6 = f32[2,256,256]{1,2,0:T(8,128)S(1)} collective-permute-done((f32[2,256,256]{1,2,0:T(8,128)S(1)}, f32[2,256,256]{1,2,0:T(8,128)S(1)}, u32[]{:S(2)}, u32[]{:S(2)}) %collective-permute-start.6) | collective-permute-done | bytes 524320 | tf_op jit(solution)/shard_map/ppermute | solution.py:10
  95.4 1.3 %fusion.1 = f32[1,2,256,1024]{2,3,1,0:T(8,128)S(1)} fusion(s32[]{:T(128)S(6)} %select_n.237, f32[2,256,256]{1,2,0:T(8,128)S(1)} %collective-permute-done.6, s32[]{:T(128)S(6)} %select_n.234, s32[]{:T(128)S(6)} %select_n.235, f32[2,256,256]{1,2,0:T(8,128)S(1)} %fusion.344), kind=kLoop, calls=%fused_computation.4 | loop fusion | flops 524288 | bytes 3145740 | tf_op jit(solution)/shard_map/broadcast_in_dim | solution.py:159
  96.7 1.8 %copy.86 = f32[1,2,256,1024]{3,2,1,0:T(8,128)} copy(f32[1,2,256,1024]{2,3,1,0:T(8,128)S(1)} %fusion.1) | data formatting | bytes 4194304 | tf_op jit(solution)/shard_map/broadcast_in_dim | solution.py:159
  (77 shorter events, 8.1 us)
Async XLA Ops:
  1.4 8.2 %collective-permute-start = (s32[2]{0:T(128)S(1)}, s32[2]{0:T(128)S(1)}, u32[]{:S(2)}, u32[]{:S(2)}) collective-permute-start(s32[2]{0:T(128)S(1)} %pad_add_fusion), channel_id=1, source_target_pairs={{0,4},{4,8},{8,12},{12,16},{16,20},{20,24},{24,28},{28,32},{32,36}... | collective-permute-start | bytes 32 | tf_op jit(solution)/shard_map/ppermute | solution.py:10
  15.8 8.6 %collective-permute-start.1 = (f32[2,256,256]{1,2,0:T(8,128)S(1)}, f32[2,256,256]{1,2,0:T(8,128)}, u32[]{:S(2)}, u32[]{:S(2)}) collective-permute-start(f32[2,256,256]{1,2,0:T(8,128)S(1)} %pad_dynamic-slice_fusion.8), channel_id=1, source_target_pairs={{4,0},{8,4},{12,8},{16,12},{20,16},{24,20},{28,24},{32,28},{36,32}... | collective-permute-start | bytes 1572872 | tf_op jit(solution)/shard_map/ppermute | solution.py:10
  25.6 13.8 %collective-permute-start.2 = (f32[2,256,256]{1,2,0:T(8,128)S(1)}, f32[2,256,256]{1,2,0:T(8,128)S(1)}, u32[]{:S(2)}, u32[]{:S(2)}) collective-permute-start(f32[2,256,256]{1,2,0:T(8,128)S(1)} %fusion.345), channel_id=1, source_target_pairs={{0,1},{1,2},{2,3},{3,0},{4,5},{5,6},{6,7},{7,4},{8,9},{9,10},{10,1... | collective-permute-start | bytes 1572872 | tf_op jit(solution)/shard_map/ppermute | solution.py:16
  28.2 12.3 %collective-permute-start.3 = (f32[2,256,256]{1,2,0:T(8,128)S(1)}, f32[2,256,256]{1,2,0:T(8,128)S(1)}, u32[]{:S(2)}, u32[]{:S(2)}) collective-permute-start(f32[2,256,256]{1,2,0:T(8,128)S(1)} %fusion.345), channel_id=1, source_target_pairs={{0,3},{1,0},{2,1},{3,2},{4,7},{5,4},{6,5},{7,6},{8,11},{9,8},{10,9... | collective-permute-start | bytes 1572872 | tf_op jit(solution)/shard_map/ppermute | solution.py:16
  30.0 1.6 %copy-start = (f32[2,256,256]{2,1,0:T(8,128)S(1)}, f32[2,256,256]{2,1,0:T(8,128)}, u32[]{:S(2)}) copy-start(f32[2,256,256]{2,1,0:T(8,128)} %param.7) | copy-start | bytes 1572868
  40.1 8.7 %collective-permute-start.5 = (f32[256,256]{0,1:T(8,128)}, f32[256,256]{0,1:T(8,128)S(1)}, u32[]{:S(2)}, u32[]{:S(2)}) collective-permute-start(f32[256,256]{0,1:T(8,128)} %slice_bitcast_fusion.8), channel_id=1, source_target_pairs={{0,1},{1,2},{2,3},{3,0},{4,5},{5,6},{6,7},{7,4},{8,9},{9,10},{10,1... | collective-permute-start | bytes 786440 | tf_op jit(solution)/shard_map/ppermute | solution.py:16
  41.2 7.7 %collective-permute-start.4 = (f32[256,256]{0,1:T(8,128)}, f32[256,256]{0,1:T(8,128)}, u32[]{:S(2)}, u32[]{:S(2)}) collective-permute-start(f32[256,256]{0,1:T(8,128)} %slice_bitcast_fusion.9), channel_id=1, source_target_pairs={{0,3},{1,0},{2,1},{3,2},{4,7},{5,4},{6,5},{7,6},{8,11},{9,8},{10,9... | collective-permute-start | bytes 786440 | tf_op jit(solution)/shard_map/ppermute | solution.py:16
  50.0 1.0 %copy-start.3 = (bf16[512,512]{1,0:T(8,128)(2,1)S(1)}, bf16[512,512]{1,0:T(8,128)(2,1)}, u32[]{:S(2)}) copy-start(bf16[512,512]{1,0:T(8,128)(2,1)} %get-tuple-element.156) | copy-start | bytes 1572868
  50.0 1.2 %copy-start.4 = (bf16[512,512]{1,0:T(8,128)(2,1)S(1)}, bf16[512,512]{1,0:T(8,128)(2,1)}, u32[]{:S(2)}) copy-start(bf16[512,512]{1,0:T(8,128)(2,1)} %get-tuple-element.157) | copy-start | bytes 1572868
  51.2 0.9 copy-start.7
  51.2 1.0 %copy-start.8 = (bf16[256,512]{1,0:T(8,128)(2,1)S(1)}, bf16[256,512]{1,0:T(8,128)(2,1)}, u32[]{:S(2)}) copy-start(bf16[256,512]{1,0:T(8,128)(2,1)} %get-tuple-element.155) | copy-start | bytes 786436
  52.8 1.0 %copy-start.1 = (bf16[512,512]{1,0:T(8,128)(2,1)S(1)}, bf16[512,512]{1,0:T(8,128)(2,1)}, u32[]{:S(2)}) copy-start(bf16[512,512]{1,0:T(8,128)(2,1)} %get-tuple-element.69) | copy-start | bytes 1572868
  52.8 1.2 %copy-start.2 = (bf16[512,512]{1,0:T(8,128)(2,1)S(1)}, bf16[512,512]{1,0:T(8,128)(2,1)}, u32[]{:S(2)}) copy-start(bf16[512,512]{1,0:T(8,128)(2,1)} %get-tuple-element.70) | copy-start | bytes 1572868
  54.0 0.9 copy-start.5
  54.0 1.0 %copy-start.6 = (bf16[256,512]{1,0:T(8,128)(2,1)S(1)}, bf16[256,512]{1,0:T(8,128)(2,1)}, u32[]{:S(2)}) copy-start(bf16[256,512]{1,0:T(8,128)(2,1)} %get-tuple-element.141) | copy-start | bytes 786436
  81.6 13.8 %collective-permute-start.6 = (f32[2,256,256]{1,2,0:T(8,128)S(1)}, f32[2,256,256]{1,2,0:T(8,128)S(1)}, u32[]{:S(2)}, u32[]{:S(2)}) collective-permute-start(f32[2,256,256]{1,2,0:T(8,128)S(1)} %pad_dynamic-slice_fusion.7), channel_id=1, source_target_pairs={{0,4},{4,8},{8,12},{12,16},{16,20},{20,24},{24,28},{28,32},{32,36}... | collective-permute-start | bytes 1572872 | tf_op jit(solution)/shard_map/ppermute | solution.py:10

commit v4 on v3

--- a/solution.py
+++ b/solution.py
@@ -68,13 +68,6 @@
     return jnp.concatenate([real_part, imag_part], axis=0)
 
 
-def propagate(real_part, imag_part, forward, inverse, kernel_real, kernel_imag):
-    freq_real, freq_imag = transform(stack(real_part, imag_part), forward)
-    prod_real = freq_real * kernel_real - freq_imag * kernel_imag
-    prod_imag = freq_real * kernel_imag + freq_imag * kernel_real
-    return transform(stack(prod_real, prod_imag), inverse)
-
-
 def per_device(transmission, probe, prop_phase, row_off, col_off, measured):
     rows = transmission.shape[2]
     columns = transmission.shape[3]
@@ -123,17 +116,22 @@
         layer_imag = layers[layer][1]
         mixed_real = wave_real * layer_real - wave_imag * layer_imag
         mixed_imag = wave_real * layer_imag + wave_imag * layer_real
-        wave_real, wave_imag = propagate(
-            mixed_real, mixed_imag, forward, inverse, kernel_real, kernel_imag
-        )
-    far_real, far_imag = transform(stack(wave_real, wave_imag), forward)
+        freq_real, freq_imag = transform(stack(mixed_real, mixed_imag), forward)
+        prod_real = freq_real * kernel_real - freq_imag * kernel_imag
+        prod_imag = freq_real * kernel_imag + freq_imag * kernel_real
+        if layer < sections - 1:
+            wave_real, wave_imag = transform(stack(prod_real, prod_imag), inverse)
+    far_real, far_imag = prod_real, prod_imag
     residual = far_real * far_real + far_imag * far_imag - measured[0]
-    grad_real, grad_imag = transform(stack(residual * far_real, residual * far_imag), inverse)
+    back_real = residual * far_real
+    back_imag = residual * far_imag
     pieces = [None] * sections
     for layer in range(sections - 1, -1, -1):
-        inner_real, inner_imag = propagate(
-            grad_real, grad_imag, forward, inverse, kernel_real, -kernel_imag
-        )
+        if layer < sections - 1:
+            back_real, back_imag = transform(stack(grad_real, grad_imag), forward)
+        prod_real = back_real * kernel_real + back_imag * kernel_imag
+        prod_imag = back_imag * kernel_real - back_real * kernel_imag
+        inner_real, inner_imag = transform(stack(prod_real, prod_imag), inverse)
         wave_real, wave_imag = saved[layer]
         pieces[layer] = jnp.stack(
             [wave_real * inner_real + wave_imag * inner_imag,

time: 99.5 us -> 91.7 us (0.922)
  matrix products: 22.5 us -> 17.4 us
  other arithmetic: 14.9 us -> 12.4 us
    dot_general x18 -> x14, matrix products: 11.4 us -> 8.71 us  [split_dot(): return jnp.dot(split_table, operand, preferred_element_type=jnp.float32)]
    dot_general x18 -> x14, matrix products: 11.1 us -> 8.65 us  [split_dot(): return jnp.dot(operand, split_table, preferred_element_type=jnp.float32)]
    select_n x2, other arithmetic: 2.21 us -> 0.31 us  [per_device(): lax.select_n((cut_index - layer) % sections, *have)]
    cos x0 -> x1, local copies, waits for them, and re-layouts: none -> 1.15 us  [per_device(): kernel_real = jnp.cos(prop_phase)]
    sin x1 -> x0, local copies, waits for them, and re-layouts: 1.15 us -> none  [per_device(): kernel_imag = jnp.sin(prop_phase)]
    convert_element_type x20 -> x16, other arithmetic: 4.29 us -> 3.81 us  [halves(): return (high.astype(jnp.bfloat16), low.astype(jnp.bfloat16))]
    unnamed x23 -> x21, local copies, waits for them, and re-layouts: 7.13 us -> 7.05 us
  transfers between devices with their start and end apart: 7 -> 7, of which waited for: 5 -> 5; matrix products, arithmetic and copies ran while one was open for 13% -> 14% of each run, Pallas kernels for 0% -> 0%
where the time goes in v4:
time: 91.7 us; the launch traced here: 90.8 us
  waiting for transfers between devices  27.4 us (30%)
  matrix products  17.4 us (19%)
  local copies, waits for them, and re-layouts  14.1 us (15%)
  other arithmetic  12.4 us (14%)
  starting transfers between devices  12.4 us (14%)
  between operations  7.07 us (8%)
    ppermute x3, waiting for transfers between devices, shifted(): return lax.ppermute(value, axis, pairs)  19.6 us
    dot_general x14, matrix products, split_dot(): return jnp.dot(split_table, operand, preferred_element_type=jnp.float32)  8.71 us
    dot_general x14, matrix products, split_dot(): return jnp.dot(operand, split_table, preferred_element_type=jnp.float32)  8.65 us
    ppermute x4, waiting for transfers between devices, rotated(): return lax.ppermute(value, axis, pairs)  7.86 us
    unnamed x21, local copies, waits for them, and re-layouts  7.05 us
    ppermute x4, starting transfers between devices, rotated(): return lax.ppermute(value, axis, pairs)  6.63 us
    ppermute x3, starting transfers between devices, shifted(): return lax.ppermute(value, axis, pairs)  5.75 us
    convert_element_type x16, other arithmetic, halves(): return (high.astype(jnp.bfloat16), low.astype(jnp.bfloat16))  3.81 us
  transfers between devices with their start and end apart: 7, of which 5 were waited for; matrix products, arithmetic and copies ran while one was open for 14% of the time, Pallas kernels for 0%

profile of v4, /device:TPU:128, one launch (start us, length us, event | category | flops | bytes accessed | tf_op | source)
XLA Modules:
  0.0 90.8 jit_solution(2447465378458589346)
XLA Ops:
  1.4 1.9 %collective-permute-start = (s32[2]{0:T(128)S(1)}, s32[2]{0:T(128)S(1)}, u32[]{:S(2)}, u32[]{:S(2)}) collective-permute-start(s32[2]{0:T(128)S(1)} %pad_add_fusion), channel_id=1, source_target_pairs={{0,4},{4,8},{8,12},{12,16},{16,20},{20,24},{24,28},{28,32},{32,36}... | collective-permute-start | bytes 32 | tf_op jit(solution)/shard_map/ppermute | solution.py:10
  3.3 6.3 %collective-permute-done = s32[2]{0:T(128)S(1)} collective-permute-done((s32[2]{0:T(128)S(1)}, s32[2]{0:T(128)S(1)}, u32[]{:S(2)}, u32[]{:S(2)}) %collective-permute-start) | collective-permute-done | bytes 40 | tf_op jit(solution)/shard_map/ppermute | solution.py:10
  9.5 0.6 fusion.321
  12.0 1.3 %constant_dynamic-slice_fusion = f32[1,2,256,256]{3,2,1,0:T(8,128)S(1)} fusion(f32[1,2,256,1024]{3,2,1,0:T(8,128)} %param.6, s32[]{:T(128)S(6)} %select_n.196), kind=kLoop, calls=%fused_computation.452 | loop fusion | bytes 1048580 | tf_op jit(solution)/shard_map/dynamic_slice | solution.py:90
  13.4 0.2 copy.9
  15.5 0.2 pad_dynamic-slice_fusion.8
  15.8 1.9 %collective-permute-start.1 = (f32[2,256,256]{1,2,0:T(8,128)S(1)}, f32[2,256,256]{1,2,0:T(8,128)}, u32[]{:S(2)}, u32[]{:S(2)}) collective-permute-start(f32[2,256,256]{1,2,0:T(8,128)S(1)} %pad_dynamic-slice_fusion.8), channel_id=1, source_target_pairs={{4,0},{8,4},{12,8},{16,12},{20,16},{24,20},{28,24},{32,28},{36,32}... | collective-permute-start | bytes 1572872 | tf_op jit(solution)/shard_map/ppermute | solution.py:10
  17.7 1.9 %copy.8 = f32[1,2,256,1024]{2,3,1,0:T(8,128)S(1)} copy(f32[1,2,256,1024]{3,2,1,0:T(8,128)} %param.6) | data formatting | bytes 4194304 | tf_op args[0]
  19.6 1.1 %cosine_multiply_fusion = (f32[256,256]{1,0:T(8,128)S(1)}, f32[256,256]{1,0:T(8,128)S(1)}) fusion(), kind=kLoop, calls=%fused_computation.443 | loop fusion | flops 1048576 | bytes 524288 | tf_op jit(solution)/shard_map/mul | solution.py:24
  20.7 1.0 %broadcast_multiply_fusion.1 = (f32[256,256]{1,0:T(8,128)S(1)}, f32[256,256]{1,0:T(8,128)S(1)}) fusion(), kind=kLoop, calls=%fused_computation.448 | loop fusion | flops 1048576 | bytes 524288 | tf_op jit(solution)/shard_map/mul | solution.py:24
  21.7 2.7 %collective-permute-done.1 = f32[2,256,256]{1,2,0:T(8,128)} collective-permute-done((f32[2,256,256]{1,2,0:T(8,128)S(1)}, f32[2,256,256]{1,2,0:T(8,128)}, u32[]{:S(2)}, u32[]{:S(2)}) %collective-permute-start.1) | collective-permute-done | bytes 524320 | tf_op jit(solution)/shard_map/ppermute | solution.py:10
  24.4 1.2 %fusion.273 = f32[2,256,256]{1,2,0:T(8,128)S(1)} fusion(f32[2,256,256]{1,2,0:T(8,128)} %collective-permute-done.1, s32[]{:T(128)S(6)} %select_n.194, s32[]{:T(128)S(6)} %select_n.195, f32[2,256,1024]{1,2,0:T(8,128)S(1)} %bitcast.167), kind=kLoop, calls=%fused_computation.324 | loop fusion | flops 131072 | bytes 3145736 | tf_op jit(solution)/shard_map/add | solution.py:96
  25.6 1.6 %collective-permute-start.2 = (f32[2,256,256]{1,2,0:T(8,128)S(1)}, f32[2,256,256]{1,2,0:T(8,128)S(1)}, u32[]{:S(2)}, u32[]{:S(2)}) collective-permute-start(f32[2,256,256]{1,2,0:T(8,128)S(1)} %fusion.273), channel_id=1, source_target_pairs={{0,1},{1,2},{2,3},{3,0},{4,5},{5,6},{6,7},{7,4},{8,9},{9,10},{10,1... | collective-permute-start | bytes 1572872 | tf_op jit(solution)/shard_map/ppermute | solution.py:16
  27.2 1.0 %fusion.290 = f32[256,256]{1,0:T(8,128)S(1)} fusion(), kind=kLoop, calls=%fused_computation.451 | loop fusion | flops 1048576 | bytes 262144 | tf_op jit(solution)/shard_map/neg | solution.py:37
  28.2 1.8 %collective-permute-start.3 = (f32[2,256,256]{1,2,0:T(8,128)S(1)}, f32[2,256,256]{1,2,0:T(8,128)S(1)}, u32[]{:S(2)}, u32[]{:S(2)}) collective-permute-start(f32[2,256,256]{1,2,0:T(8,128)S(1)} %fusion.273), channel_id=1, source_target_pairs={{0,3},{1,0},{2,1},{3,2},{4,7},{5,4},{6,5},{7,6},{8,11},{9,8},{10,9... | collective-permute-start | bytes 1572872 | tf_op jit(solution)/shard_map/ppermute | solution.py:16
  30.0 1.5 %fusion.3 = (bf16[512,512]{1,0:T(8,128)(2,1)}, bf16[512,512]{1,0:T(8,128)(2,1)}, bf16[512,512]{1,0:T(8,128)(2,1)}, bf16[512,512]{1,0:T(8,128)(2,1)}) fusion(f32[256,256]{1,0:T(8,128)S(1)} %get-tuple-element.138, f32[256,256]{1,0:T(8,128)S(1)} %get-tuple-element.140, f32[256,256]{1,0:T(8,128)S(1)} %get-tuple-element.141, ...), kind=kLoop, calls=%fused_computation.14 | loop fusion | flops 4718592 | bytes 3407872 | tf_op jit(solution)/shard_map/convert_element_type | solution.py:31
  31.6 7.8 %collective-permute-done.2 = f32[2,256,256]{1,2,0:T(8,128)S(1)} collective-permute-done((f32[2,256,256]{1,2,0:T(8,128)S(1)}, f32[2,256,256]{1,2,0:T(8,128)S(1)}, u32[]{:S(2)}, u32[]{:S(2)}) %collective-permute-start.2) | collective-permute-done | bytes 524320 | tf_op jit(solution)/shard_map/ppermute | solution.py:16
  39.4 0.7 slice_bitcast_fusion.8
  40.1 0.3 collective-permute-start.5
  40.4 0.7 slice_bitcast_fusion.9
  41.1 3.0 %collective-permute-start.4 = (f32[256,256]{0,1:T(8,128)}, f32[256,256]{0,1:T(8,128)S(1)}, u32[]{:S(2)}, u32[]{:S(2)}) collective-permute-start(f32[256,256]{0,1:T(8,128)} %slice_bitcast_fusion.9), channel_id=1, source_target_pairs={{0,3},{1,0},{2,1},{3,2},{4,7},{5,4},{6,5},{7,6},{8,11},{9,8},{10,9... | collective-permute-start | bytes 786440 | tf_op jit(solution)/shard_map/ppermute | solution.py:16
  44.1 1.0 %fusion.262 = (bf16[256,512]{1,0:T(8,128)(2,1)S(1)}, bf16[256,512]{1,0:T(8,128)(2,1)}, bf16[256,512]{1,0:T(8,128)(2,1)}, bf16[256,512]{1,0:T(8,128)(2,1)}) fusion(f32[256,256]{1,0:T(8,128)S(1)} %get-tuple-element.140, f32[256,256]{1,0:T(8,128)S(1)} %get-tuple-element.138, f32[256,256]{1,0:T(8,128)S(1)} %get-tuple-element.139), kind=kLoop, calls=%fused_computation.313 | loop fusion | flops 1835008 | bytes 1835008 | tf_op jit(solution)/shard_map/convert_element_type | solution.py:31
  45.4 1.1 %copy.13 = f32[256,256]{0,1:T(8,128)S(1)} copy(f32[256,256]{1,0:T(8,128)} %param.8) | data formatting | bytes 524288 | tf_op args[2]
  46.4 1.1 %copy.41 = f32[1,256,256]{1,2,0:T(8,128)S(1)} copy(f32[1,256,256]{2,1,0:T(8,128)} %param.11) | data formatting | bytes 524288 | tf_op args[5]
  47.5 1.1 %fusion.320 = (f32[256,256]{0,1:T(8,128)S(1)}, f32[256,256]{0,1:T(8,128)S(1)}) fusion(f32[256,256]{0,1:T(8,128)S(1)} %copy.13), kind=kLoop, calls=%fused_computation.483 | loop fusion | bytes 786432 | tf_op jit(solution)/shard_map/cos | solution.py:80
  49.1 0.8 copy-done.3
  50.1 0.6 fusion.181
  50.7 0.3 copy-done.6
  51.1 0.6 fusion.16
  52.0 0.8 copy-done.1
  53.0 0.6 fusion.187
  53.6 0.3 copy-done.5
  53.9 0.6 fusion.28
  55.0 0.6 fusion.193
  55.6 0.6 fusion.40
  56.4 0.6 fusion.197
  57.1 0.6 fusion.52
  58.0 0.6 fusion.201
  58.6 0.6 fusion.64
  59.4 0.6 fusion.205
  60.1 0.6 fusion.76
  61.0 0.6 fusion.209
  61.6 0.6 fusion.88
  62.2 0.2 multiply_add_fusion.6
  62.5 0.6 fusion.213
  63.2 0.6 fusion.100
  64.1 0.6 fusion.217
  64.7 0.6 fusion.112
  65.6 0.6 fusion.221
  66.2 0.6 fusion.124
  66.9 0.3 multiply_add_fusion.3
  67.4 0.6 fusion.225
  68.0 0.6 fusion.136
  68.8 0.6 fusion.229
  69.5 0.6 fusion.148
  70.4 0.6 fusion.233
  71.0 0.6 fusion.160
  71.9 0.6 fusion.237
  72.5 0.6 fusion.172
  73.6 0.2 pad_dynamic-slice_fusion.7
  73.8 1.9 %collective-permute-start.6 = (f32[2,256,256]{1,2,0:T(8,128)S(1)}, f32[2,256,256]{1,2,0:T(8,128)S(1)}, u32[]{:S(2)}, u32[]{:S(2)}) collective-permute-start(f32[2,256,256]{1,2,0:T(8,128)S(1)} %pad_dynamic-slice_fusion.7), channel_id=1, source_target_pairs={{0,4},{4,8},{8,12},{12,16},{16,20},{20,24},{24,28},{28,32},{32,36}... | collective-permute-start | bytes 1572872 | tf_op jit(solution)/shard_map/ppermute | solution.py:10
  77.0 10.6 %collective-permute-done.6 = f32[2,256,256]{1,2,0:T(8,128)S(1)} collective-permute-done((f32[2,256,256]{1,2,0:T(8,128)S(1)}, f32[2,256,256]{1,2,0:T(8,128)S(1)}, u32[]{:S(2)}, u32[]{:S(2)}) %collective-permute-start.6) | collective-permute-done | bytes 524320 | tf_op jit(solution)/shard_map/ppermute | solution.py:10
  87.6 1.3 %fusion.1 = f32[1,2,256,1024]{2,3,1,0:T(8,128)S(1)} fusion(s32[]{:T(128)S(6)} %select_n.237, f32[2,256,256]{1,2,0:T(8,128)S(1)} %collective-permute-done.6, s32[]{:T(128)S(6)} %select_n.234, s32[]{:T(128)S(6)} %select_n.235, f32[2,256,256]{1,2,0:T(8,128)S(1)} %fusion.272), kind=kLoop, calls=%fused_computation.4 | loop fusion | flops 524288 | bytes 3145740 | tf_op jit(solution)/shard_map/broadcast_in_dim | solution.py:157
  88.9 1.8 %copy.70 = f32[1,2,256,1024]{3,2,1,0:T(8,128)} copy(f32[1,2,256,1024]{2,3,1,0:T(8,128)S(1)} %fusion.1) | data formatting | bytes 4194304 | tf_op jit(solution)/shard_map/broadcast_in_dim | solution.py:157
  (59 shorter events, 4.6 us)
Async XLA Ops:
  1.4 8.2 %collective-permute-start = (s32[2]{0:T(128)S(1)}, s32[2]{0:T(128)S(1)}, u32[]{:S(2)}, u32[]{:S(2)}) collective-permute-start(s32[2]{0:T(128)S(1)} %pad_add_fusion), channel_id=1, source_target_pairs={{0,4},{4,8},{8,12},{12,16},{16,20},{20,24},{24,28},{28,32},{32,36}... | collective-permute-start | bytes 32 | tf_op jit(solution)/shard_map/ppermute | solution.py:10
  15.8 8.6 %collective-permute-start.1 = (f32[2,256,256]{1,2,0:T(8,128)S(1)}, f32[2,256,256]{1,2,0:T(8,128)}, u32[]{:S(2)}, u32[]{:S(2)}) collective-permute-start(f32[2,256,256]{1,2,0:T(8,128)S(1)} %pad_dynamic-slice_fusion.8), channel_id=1, source_target_pairs={{4,0},{8,4},{12,8},{16,12},{20,16},{24,20},{28,24},{32,28},{36,32}... | collective-permute-start | bytes 1572872 | tf_op jit(solution)/shard_map/ppermute | solution.py:10
  25.6 13.8 %collective-permute-start.2 = (f32[2,256,256]{1,2,0:T(8,128)S(1)}, f32[2,256,256]{1,2,0:T(8,128)S(1)}, u32[]{:S(2)}, u32[]{:S(2)}) collective-permute-start(f32[2,256,256]{1,2,0:T(8,128)S(1)} %fusion.273), channel_id=1, source_target_pairs={{0,1},{1,2},{2,3},{3,0},{4,5},{5,6},{6,7},{7,4},{8,9},{9,10},{10,1... | collective-permute-start | bytes 1572872 | tf_op jit(solution)/shard_map/ppermute | solution.py:16
  28.2 12.3 %collective-permute-start.3 = (f32[2,256,256]{1,2,0:T(8,128)S(1)}, f32[2,256,256]{1,2,0:T(8,128)S(1)}, u32[]{:S(2)}, u32[]{:S(2)}) collective-permute-start(f32[2,256,256]{1,2,0:T(8,128)S(1)} %fusion.273), channel_id=1, source_target_pairs={{0,3},{1,0},{2,1},{3,2},{4,7},{5,4},{6,5},{7,6},{8,11},{9,8},{10,9... | collective-permute-start | bytes 1572872 | tf_op jit(solution)/shard_map/ppermute | solution.py:16
  30.0 1.5 %copy-start = (f32[2,256,256]{2,1,0:T(8,128)S(1)}, f32[2,256,256]{2,1,0:T(8,128)}, u32[]{:S(2)}) copy-start(f32[2,256,256]{2,1,0:T(8,128)} %param.7) | copy-start | bytes 1572868
  40.1 8.6 %collective-permute-start.5 = (f32[256,256]{0,1:T(8,128)}, f32[256,256]{0,1:T(8,128)S(1)}, u32[]{:S(2)}, u32[]{:S(2)}) collective-permute-start(f32[256,256]{0,1:T(8,128)} %slice_bitcast_fusion.8), channel_id=1, source_target_pairs={{0,1},{1,2},{2,3},{3,0},{4,5},{5,6},{6,7},{7,4},{8,9},{9,10},{10,1... | collective-permute-start | bytes 786440 | tf_op jit(solution)/shard_map/ppermute | solution.py:16
  41.1 7.6 %collective-permute-start.4 = (f32[256,256]{0,1:T(8,128)}, f32[256,256]{0,1:T(8,128)S(1)}, u32[]{:S(2)}, u32[]{:S(2)}) collective-permute-start(f32[256,256]{0,1:T(8,128)} %slice_bitcast_fusion.9), channel_id=1, source_target_pairs={{0,3},{1,0},{2,1},{3,2},{4,7},{5,4},{6,5},{7,6},{8,11},{9,8},{10,9... | collective-permute-start | bytes 786440 | tf_op jit(solution)/shard_map/ppermute | solution.py:16
  48.9 1.0 %copy-start.3 = (bf16[512,512]{1,0:T(8,128)(2,1)S(1)}, bf16[512,512]{1,0:T(8,128)(2,1)}, u32[]{:S(2)}) copy-start(bf16[512,512]{1,0:T(8,128)(2,1)} %get-tuple-element.132) | copy-start | bytes 1572868
  48.9 1.2 %copy-start.4 = (bf16[512,512]{1,0:T(8,128)(2,1)S(1)}, bf16[512,512]{1,0:T(8,128)(2,1)}, u32[]{:S(2)}) copy-start(bf16[512,512]{1,0:T(8,128)(2,1)} %get-tuple-element.133) | copy-start | bytes 1572868
  50.1 0.9 %copy-start.6 = (bf16[256,512]{1,0:T(8,128)(2,1)S(1)}, bf16[256,512]{1,0:T(8,128)(2,1)}, u32[]{:S(2)}) copy-start(bf16[256,512]{1,0:T(8,128)(2,1)} %get-tuple-element.130) | copy-start | bytes 786436
  50.1 1.0 %copy-start.7 = (bf16[256,512]{1,0:T(8,128)(2,1)S(1)}, bf16[256,512]{1,0:T(8,128)(2,1)}, u32[]{:S(2)}) copy-start(bf16[256,512]{1,0:T(8,128)(2,1)} %get-tuple-element.131) | copy-start | bytes 786436
  51.8 1.0 %copy-start.1 = (bf16[512,512]{1,0:T(8,128)(2,1)S(1)}, bf16[512,512]{1,0:T(8,128)(2,1)}, u32[]{:S(2)}) copy-start(bf16[512,512]{1,0:T(8,128)(2,1)} %get-tuple-element.61) | copy-start | bytes 1572868
  51.8 1.2 %copy-start.2 = (bf16[512,512]{1,0:T(8,128)(2,1)S(1)}, bf16[512,512]{1,0:T(8,128)(2,1)}, u32[]{:S(2)}) copy-start(bf16[512,512]{1,0:T(8,128)(2,1)} %get-tuple-element.62) | copy-start | bytes 1572868
  53.0 0.9 %copy-start.5 = (bf16[256,512]{1,0:T(8,128)(2,1)S(1)}, bf16[256,512]{1,0:T(8,128)(2,1)}, u32[]{:S(2)}) copy-start(bf16[256,512]{1,0:T(8,128)(2,1)} %get-tuple-element.117) | copy-start | bytes 786436
  73.8 13.8 %collective-permute-start.6 = (f32[2,256,256]{1,2,0:T(8,128)S(1)}, f32[2,256,256]{1,2,0:T(8,128)S(1)}, u32[]{:S(2)}, u32[]{:S(2)}) collective-permute-start(f32[2,256,256]{1,2,0:T(8,128)S(1)} %pad_dynamic-slice_fusion.7), channel_id=1, source_target_pairs={{0,4},{4,8},{8,12},{12,16},{16,20},{20,24},{24,28},{28,32},{32,36}... | collective-permute-start | bytes 1572872 | tf_op jit(solution)/shard_map/ppermute | solution.py:10

commit v5 on v4

--- a/solution.py
+++ b/solution.py
@@ -1,6 +1,8 @@
 import jax
 import jax.numpy as jnp
 from jax import lax
+from jax.experimental import pallas as pl
+from jax.experimental.pallas import tpu as pltpu
 from jax.sharding import PartitionSpec as P
 
 
@@ -66,6 +68,54 @@
 
 def stack(real_part, imag_part):
     return jnp.concatenate([real_part, imag_part], axis=0)
+
+
+def exchange_kernel(window_ref, left_ref, right_ref, far_ref, send_sem, recv_sem):
+    devices = lax.axis_size("cuts")
+    me = lax.axis_index("cuts")
+    right = lax.rem(me + 1, devices)
+    left = lax.rem(me + devices - 1, devices)
+    mesh_ids = pl.DeviceIdType.MESH
+    barrier = pltpu.get_barrier_semaphore()
+    for neighbour in (left, right):
+        pl.semaphore_signal(barrier, inc=1, device_id={"cuts": neighbour}, device_id_type=mesh_ids)
+    pl.semaphore_wait(barrier, 2)
+
+    def remote(source, target, slot, neighbour):
+        return pltpu.make_async_remote_copy(
+            src_ref=source,
+            dst_ref=target,
+            send_sem=send_sem.at[slot],
+            recv_sem=recv_sem.at[slot],
+            device_id={"cuts": neighbour},
+            device_id_type=mesh_ids,
+        )
+
+    to_right = remote(window_ref, left_ref, 0, right)
+    to_left = remote(window_ref, right_ref, 1, left)
+    to_right.start()
+    to_left.start()
+    to_right.wait()
+    to_left.wait()
+    far_real = remote(right_ref.at[0], far_ref.at[0], 2, left)
+    far_imag = remote(left_ref.at[1], far_ref.at[1], 3, right)
+    far_real.start()
+    far_imag.start()
+    far_real.wait()
+    far_imag.wait()
+
+
+def exchange(window):
+    shape = jax.ShapeDtypeStruct(window.shape, window.dtype)
+    vmem = pl.BlockSpec(memory_space=pltpu.VMEM)
+    return pl.pallas_call(
+        exchange_kernel,
+        out_shape=(shape, shape, shape),
+        in_specs=[vmem],
+        out_specs=(vmem, vmem, vmem),
+        scratch_shapes=[pltpu.SemaphoreType.DMA((4,)), pltpu.SemaphoreType.DMA((4,))],
+        compiler_params=pltpu.CompilerParams(collective_id=0, has_side_effects=True),
+    )(window)
 
 
 def per_device(transmission, probe, prop_phase, row_off, col_off, measured):
@@ -96,11 +146,8 @@
     window = kept + borrowed
 
     if sections == 4:
-        from_left = rotated(window, "cuts", 1)
-        from_right = rotated(window, "cuts", -1)
-        far_real = rotated(from_right[0], "cuts", -1)
-        far_imag = rotated(from_left[1], "cuts", 1)
-        have = [window, from_left, jnp.stack([far_real, far_imag], axis=0), from_right]
+        from_left, from_right, far = exchange(window)
+        have = [window, from_left, far, from_right]
     else:
         have = [window] + [rotated(window, "cuts", k) for k in range(1, sections)]
     layers = [

time: 91.7 us -> 92.3 us (level)
  Pallas kernels: 0 us -> 23.6 us
  waiting for transfers between devices: 27.4 us -> 15.2 us
  local copies, waits for them, and re-layouts: 14.1 us -> 5.17 us
  other arithmetic: 12.4 us -> 16.6 us
  starting transfers between devices: 12.4 us -> 8.43 us
  matrix products: 17.4 us -> 16.1 us
    pallas_call x0 -> x1, Pallas kernels: none -> 23.6 us  [exchange(): pl.pallas_call(exchange_kernel, out_shape=(shape, shape, shape), in_specs...]
    ppermute x4 -> x0, waiting for transfers between devices: 7.86 us -> none  [rotated(): return lax.ppermute(value, axis, pairs)]
    ppermute x4 -> x0, starting transfers between devices: 6.63 us -> none  [rotated(): return lax.ppermute(value, axis, pairs)]
    ppermute x3, waiting for transfers between devices: 19.6 us -> 15.2 us  [shifted(): return lax.ppermute(value, axis, pairs)]
    unnamed x21 -> x22, local copies, waits for them, and re-layouts: 7.05 us -> 3.1 us
    ppermute x3, starting transfers between devices: 5.75 us -> 8.43 us  [shifted(): return lax.ppermute(value, axis, pairs)]
    broadcast_in_dim x1 -> x0, local copies, waits for them, and re-layouts: 1.81 us -> none  [per_device(): return result[None]]
    select_n x2 -> x1, other arithmetic: 0.31 us -> 1.8 us  [per_device(): lax.select_n((cut_index - layer) % sections, *have)]
  transfers between devices with their start and end apart: 7 -> 3, of which waited for: 5 -> 3; matrix products, arithmetic and copies ran while one was open for 14% -> 9% of each run, Pallas kernels for 0% -> 0%
where the time goes in v5:
time: 92.3 us; the launch traced here: 91.8 us
  Pallas kernels  23.6 us (26%)
  other arithmetic  16.6 us (18%)
  matrix products  16.1 us (17%)
  waiting for transfers between devices  15.2 us (16%)
  starting transfers between devices  8.43 us (9%)
  between operations  6.67 us (7%)
  local copies, waits for them, and re-layouts  5.17 us (6%)
    pallas_call x1, Pallas kernels, exchange(): pl.pallas_call(exchange_kernel, out_shape=(shape, shape, shape), in_specs...  23.6 us
    ppermute x3, waiting for transfers between devices, shifted(): return lax.ppermute(value, axis, pairs)  15.2 us
    ppermute x3, starting transfers between devices, shifted(): return lax.ppermute(value, axis, pairs)  8.43 us
    dot_general x14, matrix products, split_dot(): return jnp.dot(split_table, operand, preferred_element_type=jnp.float32)  8.11 us
    dot_general x14, matrix products, split_dot(): return jnp.dot(operand, split_table, preferred_element_type=jnp.float32)  7.97 us
    convert_element_type x16, other arithmetic, halves(): return (high.astype(jnp.bfloat16), low.astype(jnp.bfloat16))  4.77 us
    unnamed x22, local copies, waits for them, and re-layouts  3.1 us
    mul x2, other arithmetic, dft_tables(): return (jnp.cos(angle) * factor, jnp.sin(angle) * factor)  2.74 us
  transfers between devices with their start and end apart: 3, of which 3 were waited for; matrix products, arithmetic and copies ran while one was open for 9% of the time, Pallas kernels for 0%

profile of v5, /device:TPU:128, one launch (start us, length us, event | category | flops | bytes accessed | tf_op | source)
XLA Modules:
  0.0 91.8 jit_solution(13579053505563553551)
XLA Ops:
  1.5 1.9 %collective-permute-start = (s32[2]{0:T(128)S(1)}, s32[2]{0:T(128)S(1)}, u32[]{:S(2)}, u32[]{:S(2)}) collective-permute-start(s32[2]{0:T(128)S(1)} %pad_add_fusion), channel_id=1, source_target_pairs={{0,4},{4,8},{8,12},{12,16},{16,20},{20,24},{24,28},{28,32},{32,36}... | collective-permute-start | bytes 32 | tf_op jit(solution)/shard_map/ppermute | solution.py:12
  3.5 1.1 %cosine_multiply_fusion = (f32[256,256]{1,0:T(8,128)S(1)}, f32[256,256]{1,0:T(8,128)S(1)}) fusion(), kind=kLoop, calls=%fused_computation.441 | loop fusion | flops 1048576 | bytes 524288 | tf_op jit(solution)/shard_map/mul | solution.py:26
  4.6 1.7 %broadcast_multiply_fusion.1 = (f32[256,256]{1,0:T(8,128)S(1)}, f32[256,256]{1,0:T(8,128)}) fusion(), kind=kLoop, calls=%fused_computation.446 | loop fusion | flops 1048576 | bytes 524288 | tf_op jit(solution)/shard_map/mul | solution.py:26
  6.3 1.1 %fusion.262 = (bf16[256,512]{1,0:T(8,128)(2,1)}, bf16[256,512]{1,0:T(8,128)(2,1)}, bf16[256,512]{1,0:T(8,128)(2,1)}, bf16[256,512]{1,0:T(8,128)(2,1)}) fusion(f32[256,256]{1,0:T(8,128)S(1)} %get-tuple-element.145, f32[256,256]{1,0:T(8,128)S(1)} %get-tuple-element.143, f32[256,256]{1,0:T(8,128)S(1)} %get-tuple-element.144), kind=kLoop, calls=%fused_computation.313 | loop fusion | flops 1835008 | bytes 1835008 | tf_op jit(solution)/shard_map/convert_element_type | solution.py:33
  7.3 2.4 %collective-permute-done = s32[2]{0:T(128)S(1)} collective-permute-done((s32[2]{0:T(128)S(1)}, s32[2]{0:T(128)S(1)}, u32[]{:S(2)}, u32[]{:S(2)}) %collective-permute-start) | collective-permute-done | bytes 40 | tf_op jit(solution)/shard_map/ppermute | solution.py:12
  9.7 0.6 fusion.320
  13.1 0.2 dynamic-slice_bitcast_fusion
  14.0 4.6 %collective-permute-start.1 = (f32[2,256,256]{2,1,0:T(8,128)S(1)}, f32[2,256,256]{2,1,0:T(8,128)S(1)}, u32[]{:S(2)}, u32[]{:S(2)}) collective-permute-start(f32[2,256,256]{2,1,0:T(8,128)S(1)} %pad_dynamic-slice_fusion.8), channel_id=1, source_target_pairs={{4,0},{8,4},{12,8},{16,12},{20,16},{24,20},{28,24},{32,28},{36,32}... | collective-permute-start | bytes 1572872 | tf_op jit(solution)/shard_map/ppermute | solution.py:12
  18.6 1.0 %fusion.290 = f32[256,256]{1,0:T(8,128)S(1)} fusion(), kind=kLoop, calls=%fused_computation.449 | loop fusion | flops 1048576 | bytes 262144 | tf_op jit(solution)/shard_map/neg | solution.py:39
  19.6 2.4 %fusion.3 = (bf16[512,512]{1,0:T(8,128)(2,1)S(1)}, bf16[512,512]{1,0:T(8,128)(2,1)}, bf16[512,512]{1,0:T(8,128)(2,1)}, bf16[512,512]{1,0:T(8,128)(2,1)}) fusion(f32[256,256]{1,0:T(8,128)S(1)} %get-tuple-element.143, f32[256,256]{1,0:T(8,128)S(1)} %get-tuple-element.145, f32[256,256]{1,0:T(8,128)} %get-tuple-element.146, ...), kind=kLoop, calls=%fused_computation.14 | loop fusion | flops 4718592 | bytes 3407872 | tf_op jit(solution)/shard_map/convert_element_type | solution.py:33
  22.0 1.1 %fusion.319 = (f32[256,256]{1,0:T(8,128)S(1)}, f32[256,256]{1,0:T(8,128)S(1)}) fusion(f32[256,256]{1,0:T(8,128)S(1)} %copy-done.5), kind=kLoop, calls=%fused_computation.479 | loop fusion | bytes 786432 | tf_op jit(solution)/shard_map/cos | solution.py:130
  23.2 2.2 %collective-permute-done.1 = f32[2,256,256]{2,1,0:T(8,128)S(1)} collective-permute-done((f32[2,256,256]{2,1,0:T(8,128)S(1)}, f32[2,256,256]{2,1,0:T(8,128)S(1)}, u32[]{:S(2)}, u32[]{:S(2)}) %collective-permute-start.1) | collective-permute-done | bytes 524320 | tf_op jit(solution)/shard_map/ppermute | solution.py:12
  25.3 1.0 %fusion.273.window_ref = f32[2,256,256]{2,1,0:T(8,128)} fusion(f32[2,256,256]{2,1,0:T(8,128)S(1)} %collective-permute-done.1, s32[]{:T(128)S(6)} %select_n.194, s32[]{:T(128)S(6)} %select_n.195, f32[2,256,1024]{2,1,0:T(8,128)S(1)} %bitcast.162), kind=kLoop, calls=%fused_computation.324 | loop fusion | flops 131072 | bytes 3145736 | tf_op jit(solution)/shard_map/add | solution.py:146
  26.3 23.6 %shard_map.64 = (f32[2,256,256]{2,1,0:T(8,128)}, f32[2,256,256]{2,1,0:T(8,128)}, f32[2,256,256]{2,1,0:T(8,128)}) custom-call(f32[2,256,256]{2,1,0:T(8,128)} %fusion.273.window_ref), custom_call_target="tpu_custom_call" | custom-call | tf_op jit(solution)/shard_map/pallas_call | solution.py:111
  49.9 1.8 %select_select_fusion.1 = (f32[2,256,256]{2,1,0:T(8,128)S(1)}, f32[2,256,256]{2,1,0:T(8,128)S(1)}, f32[2,256,256]{2,1,0:T(8,128)S(1)}, f32[2,256,256]{2,1,0:T(8,128)S(1)}) fusion(f32[2,256,256]{2,1,0:T(8,128)} %get-tuple-element.9, f32[2,256,256]{2,1,0:T(8,128)} %get-tuple-element.10, f32[2,256,256]{2,1,0:T(8,128)} %fusion.273.window_ref, ...), kind=kLoop, calls=%fused_computation.344 | loop fusion | flops 1572864 | bytes 4194316 | tf_op jit(solution)/shard_map/select_n | solution.py:154
  51.9 0.8 copy-done.3
  52.8 0.2 copy-done.4
  52.9 0.6 fusion.181
  53.5 0.4 copy-done.9
  53.9 0.6 fusion.16
  54.7 0.8 copy-done.2
  55.6 0.6 fusion.187
  56.1 0.4 copy-done.7
  56.6 0.6 fusion.28
  57.2 0.1 multiply_subtract_fusion.12
  57.4 0.6 fusion.193
  58.0 0.6 fusion.40
  58.8 0.6 fusion.197
  59.4 0.6 fusion.52
  60.0 0.1 multiply_subtract_fusion.10
  60.3 0.6 fusion.201
  60.9 0.6 fusion.64
  61.6 0.6 fusion.205
  62.2 0.6 fusion.76
  62.8 0.1 multiply_subtract_fusion.8
  63.1 0.6 fusion.209
  63.7 0.6 fusion.88
  64.3 0.4 copy-done.6
  64.6 0.2 multiply_add_fusion.6
  64.9 0.6 fusion.213
  65.5 0.6 fusion.100
  66.1 0.1 add_bitcast_fusion
  66.2 0.1 multiply_add_fusion.5
  66.4 0.6 fusion.217
  67.0 0.6 fusion.112
  67.8 0.6 fusion.221
  68.3 0.6 fusion.124
  68.9 0.1 add_bitcast_fusion.1
  69.0 0.1 multiply_add_fusion.3
  69.2 0.6 fusion.225
  69.8 0.6 fusion.136
  70.6 0.6 fusion.229
  71.2 0.6 fusion.148
  71.8 0.3 add_bitcast_fusion.2
  72.1 0.1 multiply_add_fusion.1
  72.3 0.6 fusion.233
  72.9 0.6 fusion.160
  73.7 0.6 fusion.237
  74.3 0.6 fusion.172
  74.9 0.1 fusion.280
  75.1 0.2 fusion.272
  75.4 1.9 %collective-permute-start.2 = (f32[2,256,256]{2,1,0:T(8,128)S(1)}, f32[2,256,256]{2,1,0:T(8,128)S(1)}, u32[]{:S(2)}, u32[]{:S(2)}) collective-permute-start(f32[2,256,256]{2,1,0:T(8,128)S(1)} %pad_dynamic-slice_fusion.7), channel_id=1, source_target_pairs={{0,4},{4,8},{8,12},{12,16},{16,20},{20,24},{24,28},{28,32},{32,36}... | collective-permute-start | bytes 1572872 | tf_op jit(solution)/shard_map/ppermute | solution.py:12
  78.5 10.7 %collective-permute-done.2 = f32[2,256,256]{2,1,0:T(8,128)S(1)} collective-permute-done((f32[2,256,256]{2,1,0:T(8,128)S(1)}, f32[2,256,256]{2,1,0:T(8,128)S(1)}, u32[]{:S(2)}, u32[]{:S(2)}) %collective-permute-start.2) | collective-permute-done | bytes 524320 | tf_op jit(solution)/shard_map/ppermute | solution.py:12
  89.2 2.6 %fusion.1 = f32[1,2,256,1024]{3,2,1,0:T(8,128)} fusion(s32[]{:T(128)S(6)} %select_n.237, f32[2,256,256]{2,1,0:T(8,128)S(1)} %collective-permute-done.2, s32[]{:T(128)S(6)} %select_n.234, s32[]{:T(128)S(6)} %select_n.235, f32[2,256,256]{2,1,0:T(8,128)S(1)} %fusion.272), kind=kLoop, calls=%fused_computation.4 | loop fusion | flops 524288 | bytes 3145740 | tf_op jit(solution)/shard_map/broadcast_in_dim | solution.py:204
  (47 shorter events, 2.8 us)
Async XLA Ops:
  0.0 13.1 %copy-start = (f32[1,2,256,1024]{3,2,1,0:T(8,128)S(1)}, f32[1,2,256,1024]{3,2,1,0:T(8,128)}, u32[]{:S(2)}) copy-start(f32[1,2,256,1024]{3,2,1,0:T(8,128)} %param.6) | copy-start | bytes 6291460
  1.5 8.2 %collective-permute-start = (s32[2]{0:T(128)S(1)}, s32[2]{0:T(128)S(1)}, u32[]{:S(2)}, u32[]{:S(2)}) collective-permute-start(s32[2]{0:T(128)S(1)} %pad_add_fusion), channel_id=1, source_target_pairs={{0,4},{4,8},{8,12},{12,16},{16,20},{20,24},{24,28},{28,32},{32,36}... | collective-permute-start | bytes 32 | tf_op jit(solution)/shard_map/ppermute | solution.py:12
  14.0 11.3 %collective-permute-start.1 = (f32[2,256,256]{2,1,0:T(8,128)S(1)}, f32[2,256,256]{2,1,0:T(8,128)S(1)}, u32[]{:S(2)}, u32[]{:S(2)}) collective-permute-start(f32[2,256,256]{2,1,0:T(8,128)S(1)} %pad_dynamic-slice_fusion.8), channel_id=1, source_target_pairs={{4,0},{8,4},{12,8},{16,12},{20,16},{24,20},{28,24},{32,28},{36,32}... | collective-permute-start | bytes 1572872 | tf_op jit(solution)/shard_map/ppermute | solution.py:12
  19.6 2.4 %copy-start.5 = (f32[256,256]{1,0:T(8,128)S(1)}, f32[256,256]{1,0:T(8,128)}, u32[]{:S(2)}) copy-start(f32[256,256]{1,0:T(8,128)} %param.8) | copy-start | bytes 786436
  49.9 1.8 %copy-start.1 = (f32[2,256,256]{2,1,0:T(8,128)S(1)}, f32[2,256,256]{2,1,0:T(8,128)}, u32[]{:S(2)}) copy-start(f32[2,256,256]{2,1,0:T(8,128)} %param.7) | copy-start | bytes 1572868
  51.7 1.0 %copy-start.3 = (bf16[512,512]{1,0:T(8,128)(2,1)S(1)}, bf16[512,512]{1,0:T(8,128)(2,1)}, u32[]{:S(2)}) copy-start(bf16[512,512]{1,0:T(8,128)(2,1)} %get-tuple-element.137) | copy-start | bytes 1572868
  51.7 1.2 %copy-start.4 = (bf16[512,512]{1,0:T(8,128)(2,1)S(1)}, bf16[512,512]{1,0:T(8,128)(2,1)}, u32[]{:S(2)}) copy-start(bf16[512,512]{1,0:T(8,128)(2,1)} %get-tuple-element.138) | copy-start | bytes 1572868
  52.9 0.9 %copy-start.9 = (bf16[256,512]{1,0:T(8,128)(2,1)S(1)}, bf16[256,512]{1,0:T(8,128)(2,1)}, u32[]{:S(2)}) copy-start(bf16[256,512]{1,0:T(8,128)(2,1)} %get-tuple-element.135) | copy-start | bytes 786436
  52.9 1.0 %copy-start.10 = (bf16[256,512]{1,0:T(8,128)(2,1)S(1)}, bf16[256,512]{1,0:T(8,128)(2,1)}, u32[]{:S(2)}) copy-start(bf16[256,512]{1,0:T(8,128)(2,1)} %get-tuple-element.136) | copy-start | bytes 786436
  54.5 1.0 %copy-start.2 = (bf16[512,512]{1,0:T(8,128)(2,1)S(1)}, bf16[512,512]{1,0:T(8,128)(2,1)}, u32[]{:S(2)}) copy-start(bf16[512,512]{1,0:T(8,128)(2,1)} %get-tuple-element.69) | copy-start | bytes 1572868
  55.6 0.9 %copy-start.7 = (bf16[256,512]{1,0:T(8,128)(2,1)S(1)}, bf16[256,512]{1,0:T(8,128)(2,1)}, u32[]{:S(2)}) copy-start(bf16[256,512]{1,0:T(8,128)(2,1)} %get-tuple-element.123) | copy-start | bytes 786436
  55.6 1.0 %copy-start.8 = (bf16[256,512]{1,0:T(8,128)(2,1)S(1)}, bf16[256,512]{1,0:T(8,128)(2,1)}, u32[]{:S(2)}) copy-start(bf16[256,512]{1,0:T(8,128)(2,1)} %get-tuple-element.124) | copy-start | bytes 786436
  63.7 1.0 %copy-start.6 = (f32[1,256,256]{2,1,0:T(8,128)S(1)}, f32[1,256,256]{2,1,0:T(8,128)}, u32[]{:S(2)}) copy-start(f32[1,256,256]{2,1,0:T(8,128)} %param.11) | copy-start | bytes 786436
  75.4 13.8 %collective-permute-start.2 = (f32[2,256,256]{2,1,0:T(8,128)S(1)}, f32[2,256,256]{2,1,0:T(8,128)S(1)}, u32[]{:S(2)}, u32[]{:S(2)}) collective-permute-start(f32[2,256,256]{2,1,0:T(8,128)S(1)} %pad_dynamic-slice_fusion.7), channel_id=1, source_target_pairs={{0,4},{4,8},{8,12},{12,16},{16,20},{20,24},{24,28},{28,32},{32,36}... | collective-permute-start | bytes 1572872 | tf_op jit(solution)/shard_map/ppermute | solution.py:12

commit v6 on v5

--- a/solution.py
+++ b/solution.py
@@ -91,18 +91,24 @@
             device_id_type=mesh_ids,
         )
 
-    to_right = remote(window_ref, left_ref, 0, right)
-    to_left = remote(window_ref, right_ref, 1, left)
-    to_right.start()
-    to_left.start()
-    to_right.wait()
-    to_left.wait()
+    passed_left = remote(window_ref.at[0], right_ref.at[0], 0, left)
+    passed_right = remote(window_ref.at[1], left_ref.at[1], 1, right)
+    passed_left.start()
+    passed_right.start()
+    passed_left.wait()
+    passed_right.wait()
     far_real = remote(right_ref.at[0], far_ref.at[0], 2, left)
     far_imag = remote(left_ref.at[1], far_ref.at[1], 3, right)
     far_real.start()
     far_imag.start()
+    kept_left = remote(window_ref.at[1], right_ref.at[1], 4, left)
+    kept_right = remote(window_ref.at[0], left_ref.at[0], 5, right)
+    kept_left.start()
+    kept_right.start()
     far_real.wait()
     far_imag.wait()
+    kept_left.wait()
+    kept_right.wait()
 
 
 def exchange(window):
@@ -113,7 +119,7 @@
         out_shape=(shape, shape, shape),
         in_specs=[vmem],
         out_specs=(vmem, vmem, vmem),
-        scratch_shapes=[pltpu.SemaphoreType.DMA((4,)), pltpu.SemaphoreType.DMA((4,))],
+        scratch_shapes=[pltpu.SemaphoreType.DMA((6,)), pltpu.SemaphoreType.DMA((6,))],
         compiler_params=pltpu.CompilerParams(collective_id=0, has_side_effects=True),
     )(window)
 

time: 92.3 us -> 91.4 us (level)
  no operation moved by 1% of the time
where the time goes in v6:
time: 91.4 us; the launch traced here: 90.9 us
  Pallas kernels  22.7 us (25%)
  other arithmetic  16.6 us (18%)
  matrix products  16.1 us (18%)
  waiting for transfers between devices  15.2 us (17%)
  starting transfers between devices  8.44 us (9%)
  between operations  6.67 us (7%)
  local copies, waits for them, and re-layouts  5.17 us (6%)
    pallas_call x1, Pallas kernels, exchange(): pl.pallas_call(exchange_kernel, out_shape=(shape, shape, shape), in_specs...  22.7 us
    ppermute x3, waiting for transfers between devices, shifted(): return lax.ppermute(value, axis, pairs)  15.2 us
    ppermute x3, starting transfers between devices, shifted(): return lax.ppermute(value, axis, pairs)  8.44 us
    dot_general x14, matrix products, split_dot(): return jnp.dot(split_table, operand, preferred_element_type=jnp.float32)  8.12 us
    dot_general x14, matrix products, split_dot(): return jnp.dot(operand, split_table, preferred_element_type=jnp.float32)  7.97 us
    convert_element_type x16, other arithmetic, halves(): return (high.astype(jnp.bfloat16), low.astype(jnp.bfloat16))  4.77 us
    unnamed x22, local copies, waits for them, and re-layouts  3.1 us
    mul x2, other arithmetic, dft_tables(): return (jnp.cos(angle) * factor, jnp.sin(angle) * factor)  2.74 us
  transfers between devices with their start and end apart: 3, of which 3 were waited for; matrix products, arithmetic and copies ran while one was open for 9% of the time, Pallas kernels for 0%

profile of v6, /device:TPU:128, one launch (start us, length us, event | category | flops | bytes accessed | tf_op | source)
XLA Modules:
  0.0 90.9 jit_solution(16504787640982585948)
XLA Ops:
  1.5 1.9 %collective-permute-start = (s32[2]{0:T(128)S(1)}, s32[2]{0:T(128)S(1)}, u32[]{:S(2)}, u32[]{:S(2)}) collective-permute-start(s32[2]{0:T(128)S(1)} %pad_add_fusion), channel_id=1, source_target_pairs={{0,4},{4,8},{8,12},{12,16},{16,20},{20,24},{24,28},{28,32},{32,36}... | collective-permute-start | bytes 32 | tf_op jit(solution)/shard_map/ppermute | solution.py:12
  3.5 1.1 %cosine_multiply_fusion = (f32[256,256]{1,0:T(8,128)S(1)}, f32[256,256]{1,0:T(8,128)S(1)}) fusion(), kind=kLoop, calls=%fused_computation.441 | loop fusion | flops 1048576 | bytes 524288 | tf_op jit(solution)/shard_map/mul | solution.py:26
  4.6 1.7 %broadcast_multiply_fusion.1 = (f32[256,256]{1,0:T(8,128)S(1)}, f32[256,256]{1,0:T(8,128)}) fusion(), kind=kLoop, calls=%fused_computation.446 | loop fusion | flops 1048576 | bytes 524288 | tf_op jit(solution)/shard_map/mul | solution.py:26
  6.3 1.1 %fusion.262 = (bf16[256,512]{1,0:T(8,128)(2,1)}, bf16[256,512]{1,0:T(8,128)(2,1)}, bf16[256,512]{1,0:T(8,128)(2,1)}, bf16[256,512]{1,0:T(8,128)(2,1)}) fusion(f32[256,256]{1,0:T(8,128)S(1)} %get-tuple-element.145, f32[256,256]{1,0:T(8,128)S(1)} %get-tuple-element.143, f32[256,256]{1,0:T(8,128)S(1)} %get-tuple-element.144), kind=kLoop, calls=%fused_computation.313 | loop fusion | flops 1835008 | bytes 1835008 | tf_op jit(solution)/shard_map/convert_element_type | solution.py:33
  7.3 2.4 %collective-permute-done = s32[2]{0:T(128)S(1)} collective-permute-done((s32[2]{0:T(128)S(1)}, s32[2]{0:T(128)S(1)}, u32[]{:S(2)}, u32[]{:S(2)}) %collective-permute-start) | collective-permute-done | bytes 40 | tf_op jit(solution)/shard_map/ppermute | solution.py:12
  9.7 0.6 fusion.320
  13.1 0.2 dynamic-slice_bitcast_fusion
  14.0 4.6 %collective-permute-start.1 = (f32[2,256,256]{2,1,0:T(8,128)S(1)}, f32[2,256,256]{2,1,0:T(8,128)S(1)}, u32[]{:S(2)}, u32[]{:S(2)}) collective-permute-start(f32[2,256,256]{2,1,0:T(8,128)S(1)} %pad_dynamic-slice_fusion.8), channel_id=1, source_target_pairs={{4,0},{8,4},{12,8},{16,12},{20,16},{24,20},{28,24},{32,28},{36,32}... | collective-permute-start | bytes 1572872 | tf_op jit(solution)/shard_map/ppermute | solution.py:12
  18.6 1.0 %fusion.290 = f32[256,256]{1,0:T(8,128)S(1)} fusion(), kind=kLoop, calls=%fused_computation.449 | loop fusion | flops 1048576 | bytes 262144 | tf_op jit(solution)/shard_map/neg | solution.py:39
  19.6 2.4 %fusion.3 = (bf16[512,512]{1,0:T(8,128)(2,1)S(1)}, bf16[512,512]{1,0:T(8,128)(2,1)}, bf16[512,512]{1,0:T(8,128)(2,1)}, bf16[512,512]{1,0:T(8,128)(2,1)}) fusion(f32[256,256]{1,0:T(8,128)S(1)} %get-tuple-element.143, f32[256,256]{1,0:T(8,128)S(1)} %get-tuple-element.145, f32[256,256]{1,0:T(8,128)} %get-tuple-element.146, ...), kind=kLoop, calls=%fused_computation.14 | loop fusion | flops 4718592 | bytes 3407872 | tf_op jit(solution)/shard_map/convert_element_type | solution.py:33
  22.0 1.1 %fusion.319 = (f32[256,256]{1,0:T(8,128)S(1)}, f32[256,256]{1,0:T(8,128)S(1)}) fusion(f32[256,256]{1,0:T(8,128)S(1)} %copy-done.5), kind=kLoop, calls=%fused_computation.479 | loop fusion | bytes 786432 | tf_op jit(solution)/shard_map/cos | solution.py:136
  23.2 2.2 %collective-permute-done.1 = f32[2,256,256]{2,1,0:T(8,128)S(1)} collective-permute-done((f32[2,256,256]{2,1,0:T(8,128)S(1)}, f32[2,256,256]{2,1,0:T(8,128)S(1)}, u32[]{:S(2)}, u32[]{:S(2)}) %collective-permute-start.1) | collective-permute-done | bytes 524320 | tf_op jit(solution)/shard_map/ppermute | solution.py:12
  25.3 1.0 %fusion.273.window_ref = f32[2,256,256]{2,1,0:T(8,128)} fusion(f32[2,256,256]{2,1,0:T(8,128)S(1)} %collective-permute-done.1, s32[]{:T(128)S(6)} %select_n.194, s32[]{:T(128)S(6)} %select_n.195, f32[2,256,1024]{2,1,0:T(8,128)S(1)} %bitcast.162), kind=kLoop, calls=%fused_computation.324 | loop fusion | flops 131072 | bytes 3145736 | tf_op jit(solution)/shard_map/add | solution.py:152
  26.3 22.7 %shard_map.64 = (f32[2,256,256]{2,1,0:T(8,128)}, f32[2,256,256]{2,1,0:T(8,128)}, f32[2,256,256]{2,1,0:T(8,128)}) custom-call(f32[2,256,256]{2,1,0:T(8,128)} %fusion.273.window_ref), custom_call_target="tpu_custom_call" | custom-call | tf_op jit(solution)/shard_map/pallas_call | solution.py:117
  49.0 1.8 %select_select_fusion.1 = (f32[2,256,256]{2,1,0:T(8,128)S(1)}, f32[2,256,256]{2,1,0:T(8,128)S(1)}, f32[2,256,256]{2,1,0:T(8,128)S(1)}, f32[2,256,256]{2,1,0:T(8,128)S(1)}) fusion(f32[2,256,256]{2,1,0:T(8,128)} %get-tuple-element.9, f32[2,256,256]{2,1,0:T(8,128)} %get-tuple-element.10, f32[2,256,256]{2,1,0:T(8,128)} %fusion.273.window_ref, ...), kind=kLoop, calls=%fused_computation.344 | loop fusion | flops 1572864 | bytes 4194316 | tf_op jit(solution)/shard_map/select_n | solution.py:160
  51.0 0.8 copy-done.3
  51.9 0.2 copy-done.4
  52.0 0.6 fusion.181
  52.6 0.4 copy-done.9
  53.1 0.6 fusion.16
  53.9 0.8 copy-done.2
  54.7 0.6 fusion.187
  55.3 0.4 copy-done.7
  55.7 0.6 fusion.28
  56.3 0.1 multiply_subtract_fusion.12
  56.6 0.6 fusion.193
  57.2 0.6 fusion.40
  57.9 0.6 fusion.197
  58.5 0.6 fusion.52
  59.1 0.1 multiply_subtract_fusion.10
  59.4 0.6 fusion.201
  60.0 0.6 fusion.64
  60.8 0.6 fusion.205
  61.3 0.6 fusion.76
  61.9 0.1 multiply_subtract_fusion.8
  62.2 0.6 fusion.209
  62.8 0.6 fusion.88
  63.4 0.4 copy-done.6
  63.7 0.2 multiply_add_fusion.6
  64.0 0.6 fusion.213
  64.6 0.6 fusion.100
  65.2 0.1 add_bitcast_fusion
  65.3 0.1 multiply_add_fusion.5
  65.5 0.6 fusion.217
  66.1 0.6 fusion.112
  66.9 0.6 fusion.221
  67.5 0.6 fusion.124
  68.0 0.1 add_bitcast_fusion.1
  68.2 0.1 multiply_add_fusion.3
  68.4 0.6 fusion.225
  69.0 0.6 fusion.136
  69.7 0.6 fusion.229
  70.3 0.6 fusion.148
  70.9 0.3 add_bitcast_fusion.2
  71.2 0.1 multiply_add_fusion.1
  71.4 0.6 fusion.233
  72.0 0.6 fusion.160
  72.8 0.6 fusion.237
  73.4 0.6 fusion.172
  74.0 0.1 fusion.280
  74.3 0.2 fusion.272
  74.5 1.9 %collective-permute-start.2 = (f32[2,256,256]{2,1,0:T(8,128)S(1)}, f32[2,256,256]{2,1,0:T(8,128)S(1)}, u32[]{:S(2)}, u32[]{:S(2)}) collective-permute-start(f32[2,256,256]{2,1,0:T(8,128)S(1)} %pad_dynamic-slice_fusion.7), channel_id=1, source_target_pairs={{0,4},{4,8},{8,12},{12,16},{16,20},{20,24},{24,28},{28,32},{32,36}... | collective-permute-start | bytes 1572872 | tf_op jit(solution)/shard_map/ppermute | solution.py:12
  77.6 10.7 %collective-permute-done.2 = f32[2,256,256]{2,1,0:T(8,128)S(1)} collective-permute-done((f32[2,256,256]{2,1,0:T(8,128)S(1)}, f32[2,256,256]{2,1,0:T(8,128)S(1)}, u32[]{:S(2)}, u32[]{:S(2)}) %collective-permute-start.2) | collective-permute-done | bytes 524320 | tf_op jit(solution)/shard_map/ppermute | solution.py:12
  88.4 2.6 %fusion.1 = f32[1,2,256,1024]{3,2,1,0:T(8,128)} fusion(s32[]{:T(128)S(6)} %select_n.237, f32[2,256,256]{2,1,0:T(8,128)S(1)} %collective-permute-done.2, s32[]{:T(128)S(6)} %select_n.234, s32[]{:T(128)S(6)} %select_n.235, f32[2,256,256]{2,1,0:T(8,128)S(1)} %fusion.272), kind=kLoop, calls=%fused_computation.4 | loop fusion | flops 524288 | bytes 3145740 | tf_op jit(solution)/shard_map/broadcast_in_dim | solution.py:210
  (47 shorter events, 2.8 us)
Async XLA Ops:
  0.0 13.1 %copy-start = (f32[1,2,256,1024]{3,2,1,0:T(8,128)S(1)}, f32[1,2,256,1024]{3,2,1,0:T(8,128)}, u32[]{:S(2)}) copy-start(f32[1,2,256,1024]{3,2,1,0:T(8,128)} %param.6) | copy-start | bytes 6291460
  1.5 8.2 %collective-permute-start = (s32[2]{0:T(128)S(1)}, s32[2]{0:T(128)S(1)}, u32[]{:S(2)}, u32[]{:S(2)}) collective-permute-start(s32[2]{0:T(128)S(1)} %pad_add_fusion), channel_id=1, source_target_pairs={{0,4},{4,8},{8,12},{12,16},{16,20},{20,24},{24,28},{28,32},{32,36}... | collective-permute-start | bytes 32 | tf_op jit(solution)/shard_map/ppermute | solution.py:12
  14.0 11.3 %collective-permute-start.1 = (f32[2,256,256]{2,1,0:T(8,128)S(1)}, f32[2,256,256]{2,1,0:T(8,128)S(1)}, u32[]{:S(2)}, u32[]{:S(2)}) collective-permute-start(f32[2,256,256]{2,1,0:T(8,128)S(1)} %pad_dynamic-slice_fusion.8), channel_id=1, source_target_pairs={{4,0},{8,4},{12,8},{16,12},{20,16},{24,20},{28,24},{32,28},{36,32}... | collective-permute-start | bytes 1572872 | tf_op jit(solution)/shard_map/ppermute | solution.py:12
  19.6 2.4 %copy-start.5 = (f32[256,256]{1,0:T(8,128)S(1)}, f32[256,256]{1,0:T(8,128)}, u32[]{:S(2)}) copy-start(f32[256,256]{1,0:T(8,128)} %param.8) | copy-start | bytes 786436
  49.0 1.8 %copy-start.1 = (f32[2,256,256]{2,1,0:T(8,128)S(1)}, f32[2,256,256]{2,1,0:T(8,128)}, u32[]{:S(2)}) copy-start(f32[2,256,256]{2,1,0:T(8,128)} %param.7) | copy-start | bytes 1572868
  50.8 1.0 %copy-start.3 = (bf16[512,512]{1,0:T(8,128)(2,1)S(1)}, bf16[512,512]{1,0:T(8,128)(2,1)}, u32[]{:S(2)}) copy-start(bf16[512,512]{1,0:T(8,128)(2,1)} %get-tuple-element.137) | copy-start | bytes 1572868
  50.8 1.2 %copy-start.4 = (bf16[512,512]{1,0:T(8,128)(2,1)S(1)}, bf16[512,512]{1,0:T(8,128)(2,1)}, u32[]{:S(2)}) copy-start(bf16[512,512]{1,0:T(8,128)(2,1)} %get-tuple-element.138) | copy-start | bytes 1572868
  52.0 0.9 %copy-start.9 = (bf16[256,512]{1,0:T(8,128)(2,1)S(1)}, bf16[256,512]{1,0:T(8,128)(2,1)}, u32[]{:S(2)}) copy-start(bf16[256,512]{1,0:T(8,128)(2,1)} %get-tuple-element.135) | copy-start | bytes 786436
  52.0 1.0 %copy-start.10 = (bf16[256,512]{1,0:T(8,128)(2,1)S(1)}, bf16[256,512]{1,0:T(8,128)(2,1)}, u32[]{:S(2)}) copy-start(bf16[256,512]{1,0:T(8,128)(2,1)} %get-tuple-element.136) | copy-start | bytes 786436
  53.6 1.0 %copy-start.2 = (bf16[512,512]{1,0:T(8,128)(2,1)S(1)}, bf16[512,512]{1,0:T(8,128)(2,1)}, u32[]{:S(2)}) copy-start(bf16[512,512]{1,0:T(8,128)(2,1)} %get-tuple-element.69) | copy-start | bytes 1572868
  54.7 0.9 %copy-start.7 = (bf16[256,512]{1,0:T(8,128)(2,1)S(1)}, bf16[256,512]{1,0:T(8,128)(2,1)}, u32[]{:S(2)}) copy-start(bf16[256,512]{1,0:T(8,128)(2,1)} %get-tuple-element.123) | copy-start | bytes 786436
  54.7 1.0 %copy-start.8 = (bf16[256,512]{1,0:T(8,128)(2,1)S(1)}, bf16[256,512]{1,0:T(8,128)(2,1)}, u32[]{:S(2)}) copy-start(bf16[256,512]{1,0:T(8,128)(2,1)} %get-tuple-element.124) | copy-start | bytes 786436
  62.8 1.0 %copy-start.6 = (f32[1,256,256]{2,1,0:T(8,128)S(1)}, f32[1,256,256]{2,1,0:T(8,128)}, u32[]{:S(2)}) copy-start(f32[1,256,256]{2,1,0:T(8,128)} %param.11) | copy-start | bytes 786436
  74.5 13.8 %collective-permute-start.2 = (f32[2,256,256]{2,1,0:T(8,128)S(1)}, f32[2,256,256]{2,1,0:T(8,128)S(1)}, u32[]{:S(2)}, u32[]{:S(2)}) collective-permute-start(f32[2,256,256]{2,1,0:T(8,128)S(1)} %pad_dynamic-slice_fusion.7), channel_id=1, source_target_pairs={{0,4},{4,8},{8,12},{12,16},{16,20},{20,24},{24,28},{28,32},{32,36}... | collective-permute-start | bytes 1572872 | tf_op jit(solution)/shard_map/ppermute | solution.py:12

commit v7 on v6

--- a/solution.py
+++ b/solution.py
@@ -42,28 +42,7 @@
     right = jnp.concatenate([cosines, signed], axis=1)
     left_high, left_low = halves(left)
     right_high, right_low = halves(right)
-    left_split = jnp.concatenate([left_high, left_high, left_low], axis=1)
-    right_split = jnp.concatenate([right_high, right_low, right_high], axis=0)
-    return left_split, right_split
-
-
-def split_dot(split_table, value, table_first):
-    high, low = halves(value)
-    if table_first:
-        operand = jnp.concatenate([high, low, high], axis=0)
-        return jnp.dot(split_table, operand, preferred_element_type=jnp.float32)
-    operand = jnp.concatenate([high, high, low], axis=1)
-    return jnp.dot(operand, split_table, preferred_element_type=jnp.float32)
-
-
-def transform(stacked, tables):
-    left, right = tables
-    width = right.shape[1] // 2
-    middle = split_dot(left, stacked, True)
-    products = split_dot(right, middle, False)
-    out_real = products[:width, :width] - products[width:, width:]
-    out_imag = products[:width, width:] + products[width:, :width]
-    return out_real, out_imag
+    return left_high, left_low, right_high, right_low
 
 
 def stack(real_part, imag_part):
@@ -124,6 +103,84 @@
     )(window)
 
 
+def kernel_transform(stacked, left_high, left_low, right_high, right_low):
+    width = right_high.shape[0]
+    high, low = halves(stacked)
+    middle = (
+        jnp.dot(left_high, high, preferred_element_type=jnp.float32)
+        + jnp.dot(left_high, low, preferred_element_type=jnp.float32)
+        + jnp.dot(left_low, high, preferred_element_type=jnp.float32)
+    )
+    high, low = halves(middle)
+    products = (
+        jnp.dot(high, right_high, preferred_element_type=jnp.float32)
+        + jnp.dot(low, right_high, preferred_element_type=jnp.float32)
+        + jnp.dot(high, right_low, preferred_element_type=jnp.float32)
+    )
+    out_real = products[:width, :width] - products[width:, width:]
+    out_imag = products[:width, width:] + products[width:, :width]
+    return out_real, out_imag
+
+
+def chain_kernel(probe_ref, layers_ref, kernel_real_ref, kernel_imag_ref, measured_ref,
+                 forward_lh, forward_ll, forward_rh, forward_rl,
+                 inverse_lh, inverse_ll, inverse_rh, inverse_rl, out_ref):
+    sections = layers_ref.shape[0]
+    kernel_real = kernel_real_ref[...]
+    kernel_imag = kernel_imag_ref[...]
+
+    def forward(value):
+        return kernel_transform(value, forward_lh[...], forward_ll[...], forward_rh[...], forward_rl[...])
+
+    def inverse(value):
+        return kernel_transform(value, inverse_lh[...], inverse_ll[...], inverse_rh[...], inverse_rl[...])
+
+    wave_real = probe_ref[0]
+    wave_imag = probe_ref[1]
+    saved = []
+    for layer in range(sections):
+        saved.append((wave_real, wave_imag))
+        layer_real = layers_ref[layer, 0]
+        layer_imag = layers_ref[layer, 1]
+        mixed_real = wave_real * layer_real - wave_imag * layer_imag
+        mixed_imag = wave_real * layer_imag + wave_imag * layer_real
+        freq_real, freq_imag = forward(stack(mixed_real, mixed_imag))
+        prod_real = freq_real * kernel_real - freq_imag * kernel_imag
+        prod_imag = freq_real * kernel_imag + freq_imag * kernel_real
+        if layer < sections - 1:
+            wave_real, wave_imag = inverse(stack(prod_real, prod_imag))
+    far_real, far_imag = prod_real, prod_imag
+    residual = far_real * far_real + far_imag * far_imag - measured_ref[...]
+    back_real = residual * far_real
+    back_imag = residual * far_imag
+    for layer in range(sections - 1, -1, -1):
+        if layer < sections - 1:
+            back_real, back_imag = forward(stack(grad_real, grad_imag))
+        prod_real = back_real * kernel_real + back_imag * kernel_imag
+        prod_imag = back_imag * kernel_real - back_real * kernel_imag
+        inner_real, inner_imag = inverse(stack(prod_real, prod_imag))
+        wave_real, wave_imag = saved[layer]
+        out_ref[layer, 0] = wave_real * inner_real + wave_imag * inner_imag
+        out_ref[layer, 1] = wave_real * inner_imag - wave_imag * inner_real
+        if layer > 0:
+            layer_real = layers_ref[layer, 0]
+            layer_imag = layers_ref[layer, 1]
+            grad_real = layer_real * inner_real + layer_imag * inner_imag
+            grad_imag = layer_real * inner_imag - layer_imag * inner_real
+
+
+def run_chain(probe, layers, kernel_real, kernel_imag, measured, forward, inverse):
+    vmem = pl.BlockSpec(memory_space=pltpu.VMEM)
+    operands = (probe, layers, kernel_real, kernel_imag, measured) + forward + inverse
+    return pl.pallas_call(
+        chain_kernel,
+        out_shape=jax.ShapeDtypeStruct(layers.shape, jnp.float32),
+        in_specs=[vmem] * len(operands),
+        out_specs=vmem,
+        compiler_params=pltpu.CompilerParams(vmem_limit_bytes=48 * 1024 * 1024),
+    )(*operands)
+
+
 def per_device(transmission, probe, prop_phase, row_off, col_off, measured):
     rows = transmission.shape[2]
     columns = transmission.shape[3]
@@ -160,43 +217,10 @@
         lax.select_n((cut_index - layer) % sections, *have) for layer in range(sections)
     ]
 
-    wave_real = probe[0]
-    wave_imag = probe[1]
-    saved = []
-    for layer in range(sections):
-        saved.append((wave_real, wave_imag))
-        layer_real = layers[layer][0]
-        layer_imag = layers[layer][1]
-        mixed_real = wave_real * layer_real - wave_imag * layer_imag
-        mixed_imag = wave_real * layer_imag + wave_imag * layer_real
-        freq_real, freq_imag = transform(stack(mixed_real, mixed_imag), forward)
-        prod_real = freq_real * kernel_real - freq_imag * kernel_imag
-        prod_imag = freq_real * kernel_imag + freq_imag * kernel_real
-        if layer < sections - 1:
-            wave_real, wave_imag = transform(stack(prod_real, prod_imag), inverse)
-    far_real, far_imag = prod_real, prod_imag
-    residual = far_real * far_real + far_imag * far_imag - measured[0]
-    back_real = residual * far_real
-    back_imag = residual * far_imag
-    pieces = [None] * sections
-    for layer in range(sections - 1, -1, -1):
-        if layer < sections - 1:
-            back_real, back_imag = transform(stack(grad_real, grad_imag), forward)
-        prod_real = back_real * kernel_real + back_imag * kernel_imag
-        prod_imag = back_imag * kernel_real - back_real * kernel_imag
-        inner_real, inner_imag = transform(stack(prod_real, prod_imag), inverse)
-        wave_real, wave_imag = saved[layer]
-        pieces[layer] = jnp.stack(
-            [wave_real * inner_real + wave_imag * inner_imag,
-             wave_real * inner_imag - wave_imag * inner_real],
-            axis=0,
-        )
-        if layer > 0:
-            layer_real = layers[layer][0]
-            layer_imag = layers[layer][1]
-            grad_real = layer_real * inner_real + layer_imag * inner_imag
-            grad_imag = layer_real * inner_imag - layer_imag * inner_real
-    piece = jnp.take(jnp.stack(pieces, axis=0), cut_index, axis=0)
+    pieces = run_chain(
+        probe, jnp.stack(layers, axis=0), kernel_real, kernel_imag, measured[0], forward, inverse
+    )
+    piece = jnp.take(pieces, cut_index, axis=0)
 
     padded = jnp.concatenate([piece, jnp.zeros_like(piece)], axis=1)
     spill = lax.dynamic_slice(padded, (zero, rows - row, zero), (2, width, width))

time: 91.4 us -> 99.3 us (1.086)
  Pallas kernels: 22.7 us -> 50.7 us
  matrix products: 16.1 us -> 0 us
  other arithmetic: 16.6 us -> 13.4 us
  local copies, waits for them, and re-layouts: 5.17 us -> 3.79 us
  waiting for transfers between devices: 15.2 us -> 16.3 us
    pallas_call x0 -> x1, Pallas kernels: none -> 28 us  [run_chain(): pl.pallas_call(chain_kernel, out_shape=jax.ShapeDtypeStruct(layers.shape,...]
    dot_general x28 -> x0, matrix products: 16.1 us -> none  [the longest x14 8.12 us: split_dot(): return jnp.dot(split_table, operand, preferred_element_type=jnp.float32)]
    convert_element_type x16 -> x2, other arithmetic: 4.77 us -> 1.69 us  [halves(): return (high.astype(jnp.bfloat16), low.astype(jnp.bfloat16))]
    unnamed x22 -> x14, local copies, waits for them, and re-layouts: 3.1 us -> 0.04 us
    another operation x8 -> x2, other arithmetic: 0.79 us -> 3.26 us  [per_device(): jnp.stack(layers, axis=0)]
    sin x0 -> x1, local copies, waits for them, and re-layouts: none -> 1.6 us  [per_device(): kernel_imag = jnp.sin(prop_phase)]
    dynamic_slice x1, local copies, waits for them, and re-layouts: 0.21 us -> 1.34 us  [per_device(): lax.dynamic_slice(strip, (zero, zero, column_above), (2, width, width))]
    cos x1 -> x0, local copies, waits for them, and re-layouts: 1.13 us -> none  [per_device(): kernel_real = jnp.cos(prop_phase)]
  transfers between devices with their start and end apart: 3 -> 3, of which waited for: 3 -> 3; matrix products, arithmetic and copies ran while one was open for 9% -> 7% of each run, Pallas kernels for 0% -> 0%
where the time goes in v7:
time: 99.3 us; the launch traced here: 98.7 us
  Pallas kernels  50.7 us (51%)
  waiting for transfers between devices  16.3 us (16%)
  other arithmetic  13.4 us (13%)
  starting transfers between devices  7.68 us (8%)
  between operations  6.86 us (7%)
  local copies, waits for them, and re-layouts  3.79 us (4%)
    pallas_call x1, Pallas kernels, run_chain(): pl.pallas_call(chain_kernel, out_shape=jax.ShapeDtypeStruct(layers.shape,...  28 us
    pallas_call x1, Pallas kernels, exchange(): pl.pallas_call(exchange_kernel, out_shape=(shape, shape, shape), in_specs...  22.7 us
    ppermute x3, waiting for transfers between devices, shifted(): return lax.ppermute(value, axis, pairs)  16.3 us
    ppermute x3, starting transfers between devices, shifted(): return lax.ppermute(value, axis, pairs)  7.68 us
    another operation x2, other arithmetic, per_device(): jnp.stack(layers, axis=0)  3.26 us
    mul x2, other arithmetic, dft_tables(): return (jnp.cos(angle) * factor, jnp.sin(angle) * factor)  2.74 us
    broadcast_in_dim x1, other arithmetic, per_device(): return result[None]  2.56 us
  transfers between devices with their start and end apart: 3, of which 3 were waited for; matrix products, arithmetic and copies ran while one was open for 7% of the time, Pallas kernels for 0%

profile of v7, /device:TPU:128, one launch (start us, length us, event | category | flops | bytes accessed | tf_op | source)
XLA Modules:
  0.0 98.7 jit_solution(18086968455495560070)
XLA Ops:
  1.3 0.1 pad_add_fusion
  1.4 1.9 %collective-permute-start = (s32[2]{0:T(128)S(1)}, s32[2]{0:T(128)S(1)}, u32[]{:S(2)}, u32[]{:S(2)}) collective-permute-start(s32[2]{0:T(128)S(1)} %pad_add_fusion), channel_id=1, source_target_pairs={{0,4},{4,8},{8,12},{12,16},{16,20},{20,24},{24,28},{28,32},{32,36}... | collective-permute-start | bytes 32 | tf_op jit(solution)/shard_map/ppermute | solution.py:12
  3.4 1.1 %cosine_multiply_fusion = (f32[256,256]{1,0:T(8,128)S(1)}, f32[256,256]{1,0:T(8,128)S(1)}) fusion(), kind=kLoop, calls=%fused_computation.45 | loop fusion | flops 1048576 | bytes 524288 | tf_op jit(solution)/shard_map/mul | solution.py:26
  4.4 0.0 copy-start.4
  4.4 1.7 %broadcast_multiply_fusion.1 = (f32[256,256]{1,0:T(8,128)S(1)}, f32[256,256]{1,0:T(8,128)}) fusion(), kind=kLoop, calls=%fused_computation.50 | loop fusion | flops 1048576 | bytes 524288 | tf_op jit(solution)/shard_map/mul | solution.py:26
  6.1 0.0 copy-start.5
  6.1 0.1 fusion.14
  6.3 3.3 %collective-permute-done = s32[2]{0:T(128)S(1)} collective-permute-done((s32[2]{0:T(128)S(1)}, s32[2]{0:T(128)S(1)}, u32[]{:S(2)}, u32[]{:S(2)}) %collective-permute-start) | collective-permute-done | bytes 40 | tf_op jit(solution)/shard_map/ppermute | solution.py:12
  9.5 0.7 fusion.27
  13.5 1.3 %dynamic-slice_bitcast_fusion = f32[2,256,256]{2,1,0:T(8,128)S(1)} fusion(f32[1,2,256,1024]{3,2,1,0:T(8,128)} %param.6, s32[]{:T(128)S(6)} %select_n.195), kind=kLoop, calls=%fused_computation.38 | loop fusion | bytes 1048580 | tf_op jit(solution)/shard_map/dynamic_slice | solution.py:203
  15.5 0.1 pad_dynamic-slice_fusion.4
  15.6 0.0 copy-done.4
  15.6 0.0 copy-start.6
  15.6 3.8 %collective-permute-start.1 = (f32[2,256,256]{2,1,0:T(8,128)S(1)}, f32[2,256,256]{2,1,0:T(8,128)S(1)}, u32[]{:S(2)}, u32[]{:S(2)}) collective-permute-start(f32[2,256,256]{2,1,0:T(8,128)S(1)} %pad_dynamic-slice_fusion.4), channel_id=1, source_target_pairs={{4,0},{8,4},{12,8},{16,12},{20,16},{24,20},{28,24},{32,28},{36,32}... | collective-permute-start | bytes 1572872 | tf_op jit(solution)/shard_map/ppermute | solution.py:12
  19.4 1.0 fusion.25
  20.4 0.0 copy-done.5
  20.4 0.0 copy-start.3
  20.4 1.6 %fusion.8 = (bf16[512,512]{1,0:T(8,128)(2,1)S(1)}, bf16[512,512]{1,0:T(8,128)(2,1)S(1)}, bf16[512,512]{1,0:T(8,128)(2,1)S(1)}, bf16[512,512]{1,0:T(8,128)(2,1)S(1)}) fusion(f32[256,256]{1,0:T(8,128)S(1)} %get-tuple-element.42, f32[256,256]{1,0:T(8,128)} %copy-done.5, f32[256,256]{1,0:T(8,128)} %get-tuple-element.45, f32[256,256]{1,0:T(8,128)} %copy-done.4, ...), kind=kLoop, calls=%fused_computation.18 | loop fusion | flops 4718592 | bytes 3407872 | tf_op jit(solution)/shard_map/convert_element_type | solution.py:33
  22.0 0.0 copy-done.6
  22.0 1.6 %fusion.26 = (f32[256,256]{1,0:T(8,128)S(1)}, f32[256,256]{1,0:T(8,128)}) fusion(f32[256,256]{1,0:T(8,128)S(1)} %copy-done.6), kind=kLoop, calls=%fused_computation.55 | loop fusion | bytes 786432 | tf_op jit(solution)/shard_map/sin | solution.py:194
  23.6 2.5 %collective-permute-done.1 = f32[2,256,256]{2,1,0:T(8,128)S(1)} collective-permute-done((f32[2,256,256]{2,1,0:T(8,128)S(1)}, f32[2,256,256]{2,1,0:T(8,128)S(1)}, u32[]{:S(2)}, u32[]{:S(2)}) %collective-permute-start.1) | collective-permute-done | bytes 524320 | tf_op jit(solution)/shard_map/ppermute | solution.py:12
  26.1 0.0 copy-done.3
  26.1 1.0 %fusion.16.window_ref = f32[2,256,256]{2,1,0:T(8,128)} fusion(f32[2,256,256]{2,1,0:T(8,128)S(1)} %collective-permute-done.1, s32[]{:T(128)S(6)} %select_n.193, s32[]{:T(128)S(6)} %select_n.194, f32[2,256,1024]{2,1,0:T(8,128)S(1)} %bitcast.32), kind=kLoop, calls=%fused_computation.32 | loop fusion | flops 131072 | bytes 3145736 | tf_op jit(solution)/shard_map/add | solution.py:209
  27.1 22.7 %shard_map.64 = (f32[2,256,256]{2,1,0:T(8,128)}, f32[2,256,256]{2,1,0:T(8,128)}, f32[2,256,256]{2,1,0:T(8,128)}) custom-call(f32[2,256,256]{2,1,0:T(8,128)} %fusion.16.window_ref), custom_call_target="tpu_custom_call" | custom-call | tf_op jit(solution)/shard_map/pallas_call | solution.py:96
  49.9 1.8 %select_bitcast_fusion.4 = (f32[1,2,256,256]{3,2,1,0:T(8,128)S(1)}, f32[1,2,256,256]{3,2,1,0:T(8,128)S(1)}, f32[1,2,256,256]{3,2,1,0:T(8,128)S(1)}, f32[1,2,256,256]{3,2,1,0:T(8,128)S(1)}) fusion(f32[2,256,256]{2,1,0:T(8,128)} %get-tuple-element.9, f32[2,256,256]{2,1,0:T(8,128)} %get-tuple-element.10, f32[2,256,256]{2,1,0:T(8,128)} %fusion.16.window_ref, ...), kind=kLoop, calls=%fused_computation.37 | loop fusion | flops 1572864 | bytes 4194316 | tf_op jit(solution)/shard_map/stack | solution.py:221
  51.6 0.0 copy-start
  51.7 0.0 copy-start.1
  51.7 0.0 copy-start.2
  51.7 1.5 %pad_maximum_fusion.layers_ref = f32[4,2,256,256]{3,2,1,0:T(8,128)} fusion(f32[1,2,256,256]{3,2,1,0:T(8,128)S(1)} %get-tuple-element.23, f32[1,2,256,256]{3,2,1,0:T(8,128)S(1)} %get-tuple-element.24, f32[1,2,256,256]{3,2,1,0:T(8,128)S(1)} %get-tuple-element.25, f32[1,2,256,256]{3,2,1,0:T(8,128)S(1)} %get-tuple-element.22), kind=kLoop, calls=%fused_computation.5 | loop fusion | flops 1572864 | bytes 4194304 | tf_op jit(solution)/shard_map/stack | solution.py:221
  53.2 0.0 copy-done
  53.2 0.0 copy-done.1
  53.2 0.0 copy-done.2
  53.2 28.0 %shard_map.65 = f32[4,2,256,256]{3,2,1,0:T(8,128)} custom-call(f32[2,256,256]{2,1,0:T(8,128)S(1)} %copy-done.1, f32[4,2,256,256]{3,2,1,0:T(8,128)} %pad_maximum_fusion.layers_ref, f32[256,256]{1,0:T(8,128)S(1)} %copy-done, f32[256,256]{1,0:T(8,128)S(1)} %get-tuple-element.38.kernel_imag_ref, f32[256,256]{1,0:T(8,128)S(1)} %bitcast.31, ...), custom_call_target="tpu_custom_call" | custom-call | tf_op jit(solution)/shard_map/pallas_call | solution.py:175
  81.2 1.1 %select_bitcast_fusion = f32[2,256,256]{2,1,0:T(8,128)S(1)} fusion(f32[4,2,256,256]{3,2,1,0:T(8,128)} %shard_map.65, s32[]{:T(128)S(6)} %select_n.187, pred[]{:T(512)S(6)} %and.55), kind=kLoop, calls=%fused_computation.33 | loop fusion | flops 131072 | bytes 1048581 | tf_op jit(solution)/shard_map/jit(_take)/select_n | solution.py:223
  82.2 0.1 pad_dynamic-slice_fusion.3
  82.3 1.9 %collective-permute-start.2 = (f32[2,256,256]{2,1,0:T(8,128)S(1)}, f32[2,256,256]{2,1,0:T(8,128)S(1)}, u32[]{:S(2)}, u32[]{:S(2)}) collective-permute-start(f32[2,256,256]{2,1,0:T(8,128)S(1)} %pad_dynamic-slice_fusion.3), channel_id=1, source_target_pairs={{0,4},{4,8},{8,12},{12,16},{16,20},{20,24},{24,28},{28,32},{32,36}... | collective-permute-start | bytes 1572872 | tf_op jit(solution)/shard_map/ppermute | solution.py:12
  85.6 10.5 %collective-permute-done.2 = f32[2,256,256]{2,1,0:T(8,128)S(1)} collective-permute-done((f32[2,256,256]{2,1,0:T(8,128)S(1)}, f32[2,256,256]{2,1,0:T(8,128)S(1)}, u32[]{:S(2)}, u32[]{:S(2)}) %collective-permute-start.2) | collective-permute-done | bytes 524320 | tf_op jit(solution)/shard_map/ppermute | solution.py:12
  96.1 2.6 %fusion.1 = f32[1,2,256,1024]{3,2,1,0:T(8,128)} fusion(s32[]{:T(128)S(6)} %select_n.237, f32[2,256,256]{2,1,0:T(8,128)S(1)} %collective-permute-done.2, s32[]{:T(128)S(6)} %select_n.234, s32[]{:T(128)S(6)} %select_n.235, f32[2,256,256]{2,1,0:T(8,128)S(1)} %select_bitcast_fusion), kind=kLoop, calls=%fused_computation.4 | loop fusion | flops 524288 | bytes 3145740 | tf_op jit(solution)/shard_map/broadcast_in_dim | solution.py:234
Async XLA Ops:
  1.4 8.2 %collective-permute-start = (s32[2]{0:T(128)S(1)}, s32[2]{0:T(128)S(1)}, u32[]{:S(2)}, u32[]{:S(2)}) collective-permute-start(s32[2]{0:T(128)S(1)} %pad_add_fusion), channel_id=1, source_target_pairs={{0,4},{4,8},{8,12},{12,16},{16,20},{20,24},{24,28},{28,32},{32,36}... | collective-permute-start | bytes 32 | tf_op jit(solution)/shard_map/ppermute | solution.py:12
  4.4 11.1 %copy-start.4 = (f32[256,256]{1,0:T(8,128)}, f32[256,256]{1,0:T(8,128)S(1)}, u32[]{:S(2)}) copy-start(f32[256,256]{1,0:T(8,128)S(1)} %get-tuple-element.43) | copy-start | bytes 786436
  6.1 14.3 %copy-start.5 = (f32[256,256]{1,0:T(8,128)}, f32[256,256]{1,0:T(8,128)S(1)}, u32[]{:S(2)}) copy-start(f32[256,256]{1,0:T(8,128)S(1)} %get-tuple-element.44) | copy-start | bytes 786436
  15.6 6.4 %copy-start.6 = (f32[256,256]{1,0:T(8,128)S(1)}, f32[256,256]{1,0:T(8,128)}, u32[]{:S(2)}) copy-start(f32[256,256]{1,0:T(8,128)} %param.8) | copy-start | bytes 786436
  15.6 10.5 %collective-permute-start.1 = (f32[2,256,256]{2,1,0:T(8,128)S(1)}, f32[2,256,256]{2,1,0:T(8,128)S(1)}, u32[]{:S(2)}, u32[]{:S(2)}) collective-permute-start(f32[2,256,256]{2,1,0:T(8,128)S(1)} %pad_dynamic-slice_fusion.4), channel_id=1, source_target_pairs={{4,0},{8,4},{12,8},{16,12},{20,16},{24,20},{28,24},{32,28},{36,32}... | collective-permute-start | bytes 1572872 | tf_op jit(solution)/shard_map/ppermute | solution.py:12
  20.4 5.7 %copy-start.3 = (f32[1,2,256,1024]{3,2,1,0:T(8,128)S(1)}, f32[1,2,256,1024]{3,2,1,0:T(8,128)}, u32[]{:S(2)}) copy-start(f32[1,2,256,1024]{3,2,1,0:T(8,128)} %param.6) | copy-start | bytes 6291460
  51.6 1.5 %copy-start = (f32[256,256]{1,0:T(8,128)S(1)}, f32[256,256]{1,0:T(8,128)}, u32[]{:S(2)}) copy-start(f32[256,256]{1,0:T(8,128)} %get-tuple-element.39.kernel_real_ref) | copy-start | bytes 786436
  51.7 1.5 %copy-start.1 = (f32[2,256,256]{2,1,0:T(8,128)S(1)}, f32[2,256,256]{2,1,0:T(8,128)}, u32[]{:S(2)}) copy-start(f32[2,256,256]{2,1,0:T(8,128)} %probe_ref.1) | copy-start | bytes 1572868
  51.7 1.5 %copy-start.2 = (f32[1,256,256]{2,1,0:T(8,128)S(1)}, f32[1,256,256]{2,1,0:T(8,128)}, u32[]{:S(2)}) copy-start(f32[1,256,256]{2,1,0:T(8,128)} %param.11) | copy-start | bytes 786436
  82.3 13.8 %collective-permute-start.2 = (f32[2,256,256]{2,1,0:T(8,128)S(1)}, f32[2,256,256]{2,1,0:T(8,128)S(1)}, u32[]{:S(2)}, u32[]{:S(2)}) collective-permute-start(f32[2,256,256]{2,1,0:T(8,128)S(1)} %pad_dynamic-slice_fusion.3), channel_id=1, source_target_pairs={{0,4},{4,8},{8,12},{12,16},{16,20},{20,24},{24,28},{28,32},{32,36}... | collective-permute-start | bytes 1572872 | tf_op jit(solution)/shard_map/ppermute | solution.py:12

commit v8 on v6

--- a/solution.py
+++ b/solution.py
@@ -204,9 +204,8 @@
 
     own = jnp.pad(piece, ((0, 0), (rows, rows), (columns, columns)))
     own = lax.dynamic_slice(own, (zero, rows - row, columns - column), (2, rows, columns))
-    above = jnp.pad(arrived, ((0, 0), (0, rows), (columns, columns)))
-    above = lax.dynamic_slice(above, (zero, zero, columns - column_above), (2, rows, columns))
-    result = own + above
+    current = lax.dynamic_slice(own, (zero, zero, column_above), (2, width, width))
+    result = lax.dynamic_update_slice(own, current + arrived, (zero, zero, column_above))
     return result[None]
 
 

time: 91.4 us -> 93.3 us (1.021)
  local copies, waits for them, and re-layouts: 5.17 us -> 10.9 us
  other arithmetic: 16.6 us -> 14.3 us
    dynamic_update_slice x0 -> x1, local copies, waits for them, and re-layouts: none -> 3.74 us  [per_device(): lax.dynamic_update_slice(own, current + arrived, (zero, zero, column_above))]
    broadcast_in_dim x1, other arithmetic: 2.57 us -> 0.27 us  [per_device(): return result[None]]
    broadcast_in_dim x0 -> x1, local copies, waits for them, and re-layouts: none -> 2.01 us  [per_device(): return result[None]]
  transfers between devices with their start and end apart: 3 -> 3, of which waited for: 3 -> 3; matrix products, arithmetic and copies ran while one was open for 9% -> 11% of each run, Pallas kernels for 0% -> 0%
where the time goes in v8:
time: 93.3 us; the launch traced here: 92.7 us
  Pallas kernels  22.7 us (24%)
  matrix products  16.1 us (17%)
  waiting for transfers between devices  14.4 us (15%)
  other arithmetic  14.3 us (15%)
  local copies, waits for them, and re-layouts  10.9 us (12%)
  starting transfers between devices  8.43 us (9%)
  between operations  5.86 us (6%)
    pallas_call x1, Pallas kernels, exchange(): pl.pallas_call(exchange_kernel, out_shape=(shape, shape, shape), in_specs...  22.7 us
    ppermute x3, waiting for transfers between devices, shifted(): return lax.ppermute(value, axis, pairs)  14.4 us
    ppermute x3, starting transfers between devices, shifted(): return lax.ppermute(value, axis, pairs)  8.43 us
    dot_general x14, matrix products, split_dot(): return jnp.dot(split_table, operand, preferred_element_type=jnp.float32)  8.11 us
    dot_general x14, matrix products, split_dot(): return jnp.dot(operand, split_table, preferred_element_type=jnp.float32)  7.97 us
    convert_element_type x16, other arithmetic, halves(): return (high.astype(jnp.bfloat16), low.astype(jnp.bfloat16))  4.77 us
    dynamic_update_slice x1, local copies, waits for them, and re-layouts, per_device(): lax.dynamic_update_slice(own, current + arrived, (zero, zero, column_above))  3.74 us
    unnamed x22, local copies, waits for them, and re-layouts  3.1 us
  transfers between devices with their start and end apart: 3, of which 3 were waited for; matrix products, arithmetic and copies ran while one was open for 11% of the time, Pallas kernels for 0%

profile of v8, /device:TPU:128, one launch (start us, length us, event | category | flops | bytes accessed | tf_op | source)
XLA Modules:
  0.0 92.7 jit_solution(3452200434193197169)
XLA Ops:
  1.5 1.9 %collective-permute-start = (s32[2]{0:T(128)S(1)}, s32[2]{0:T(128)S(1)}, u32[]{:S(2)}, u32[]{:S(2)}) collective-permute-start(s32[2]{0:T(128)S(1)} %pad_add_fusion), channel_id=1, source_target_pairs={{0,4},{4,8},{8,12},{12,16},{16,20},{20,24},{24,28},{28,32},{32,36}... | collective-permute-start | bytes 32 | tf_op jit(solution)/shard_map/ppermute | solution.py:12
  3.5 1.1 %cosine_multiply_fusion = (f32[256,256]{1,0:T(8,128)S(1)}, f32[256,256]{1,0:T(8,128)S(1)}) fusion(), kind=kLoop, calls=%fused_computation.442 | loop fusion | flops 1048576 | bytes 524288 | tf_op jit(solution)/shard_map/mul | solution.py:26
  4.6 1.7 %broadcast_multiply_fusion.1 = (f32[256,256]{1,0:T(8,128)S(1)}, f32[256,256]{1,0:T(8,128)}) fusion(), kind=kLoop, calls=%fused_computation.447 | loop fusion | flops 1048576 | bytes 524288 | tf_op jit(solution)/shard_map/mul | solution.py:26
  6.3 1.1 %fusion.262 = (bf16[256,512]{1,0:T(8,128)(2,1)}, bf16[256,512]{1,0:T(8,128)(2,1)}, bf16[256,512]{1,0:T(8,128)(2,1)}, bf16[256,512]{1,0:T(8,128)(2,1)}) fusion(f32[256,256]{1,0:T(8,128)S(1)} %get-tuple-element.145, f32[256,256]{1,0:T(8,128)S(1)} %get-tuple-element.143, f32[256,256]{1,0:T(8,128)S(1)} %get-tuple-element.144), kind=kLoop, calls=%fused_computation.313 | loop fusion | flops 1835008 | bytes 1835008 | tf_op jit(solution)/shard_map/convert_element_type | solution.py:33
  7.3 2.4 %collective-permute-done = s32[2]{0:T(128)S(1)} collective-permute-done((s32[2]{0:T(128)S(1)}, s32[2]{0:T(128)S(1)}, u32[]{:S(2)}, u32[]{:S(2)}) %collective-permute-start) | collective-permute-done | bytes 40 | tf_op jit(solution)/shard_map/ppermute | solution.py:12
  9.7 0.6 fusion.321
  13.4 0.2 dynamic-slice_bitcast_fusion
  14.3 4.6 %collective-permute-start.1 = (f32[2,256,256]{2,1,0:T(8,128)S(1)}, f32[2,256,256]{2,1,0:T(8,128)S(1)}, u32[]{:S(2)}, u32[]{:S(2)}) collective-permute-start(f32[2,256,256]{2,1,0:T(8,128)S(1)} %pad_dynamic-slice_fusion.8), channel_id=1, source_target_pairs={{4,0},{8,4},{12,8},{16,12},{20,16},{24,20},{28,24},{32,28},{36,32}... | collective-permute-start | bytes 1572872 | tf_op jit(solution)/shard_map/ppermute | solution.py:12
  19.0 1.0 %fusion.291 = f32[256,256]{1,0:T(8,128)S(1)} fusion(), kind=kLoop, calls=%fused_computation.450 | loop fusion | flops 1048576 | bytes 262144 | tf_op jit(solution)/shard_map/neg | solution.py:39
  19.9 2.4 %fusion.2 = (bf16[512,512]{1,0:T(8,128)(2,1)S(1)}, bf16[512,512]{1,0:T(8,128)(2,1)}, bf16[512,512]{1,0:T(8,128)(2,1)}, bf16[512,512]{1,0:T(8,128)(2,1)}) fusion(f32[256,256]{1,0:T(8,128)S(1)} %get-tuple-element.143, f32[256,256]{1,0:T(8,128)S(1)} %get-tuple-element.145, f32[256,256]{1,0:T(8,128)} %get-tuple-element.146, ...), kind=kLoop, calls=%fused_computation.13 | loop fusion | flops 4718592 | bytes 3407872 | tf_op jit(solution)/shard_map/convert_element_type | solution.py:33
  22.3 1.1 %fusion.320 = (f32[256,256]{1,0:T(8,128)S(1)}, f32[256,256]{1,0:T(8,128)S(1)}) fusion(f32[256,256]{1,0:T(8,128)S(1)} %copy-done.5), kind=kLoop, calls=%fused_computation.480 | loop fusion | bytes 786432 | tf_op jit(solution)/shard_map/cos | solution.py:136
  23.5 2.2 %collective-permute-done.1 = f32[2,256,256]{2,1,0:T(8,128)S(1)} collective-permute-done((f32[2,256,256]{2,1,0:T(8,128)S(1)}, f32[2,256,256]{2,1,0:T(8,128)S(1)}, u32[]{:S(2)}, u32[]{:S(2)}) %collective-permute-start.1) | collective-permute-done | bytes 524320 | tf_op jit(solution)/shard_map/ppermute | solution.py:12
  25.6 1.0 %fusion.273.window_ref = f32[2,256,256]{2,1,0:T(8,128)} fusion(f32[2,256,256]{2,1,0:T(8,128)S(1)} %collective-permute-done.1, s32[]{:T(128)S(6)} %select_n.199, s32[]{:T(128)S(6)} %select_n.200, f32[2,256,1024]{2,1,0:T(8,128)S(1)} %bitcast.164), kind=kLoop, calls=%fused_computation.324 | loop fusion | flops 131072 | bytes 3145736 | tf_op jit(solution)/shard_map/add | solution.py:152
  26.6 22.7 %shard_map.64 = (f32[2,256,256]{2,1,0:T(8,128)}, f32[2,256,256]{2,1,0:T(8,128)}, f32[2,256,256]{2,1,0:T(8,128)}) custom-call(f32[2,256,256]{2,1,0:T(8,128)} %fusion.273.window_ref), custom_call_target="tpu_custom_call" | custom-call | tf_op jit(solution)/shard_map/pallas_call | solution.py:117
  49.4 1.8 %select_select_fusion.1 = (f32[2,256,256]{2,1,0:T(8,128)S(1)}, f32[2,256,256]{2,1,0:T(8,128)S(1)}, f32[2,256,256]{2,1,0:T(8,128)S(1)}, f32[2,256,256]{2,1,0:T(8,128)S(1)}) fusion(f32[2,256,256]{2,1,0:T(8,128)} %get-tuple-element.9, f32[2,256,256]{2,1,0:T(8,128)} %get-tuple-element.10, f32[2,256,256]{2,1,0:T(8,128)} %fusion.273.window_ref, ...), kind=kLoop, calls=%fused_computation.344 | loop fusion | flops 1572864 | bytes 4194316 | tf_op jit(solution)/shard_map/select_n | solution.py:160
  51.4 0.8 copy-done.3
  52.2 0.2 copy-done.4
  52.4 0.6 fusion.180
  53.0 0.4 copy-done.9
  53.4 0.6 fusion.15
  54.2 0.8 copy-done.2
  55.0 0.6 fusion.186
  55.6 0.4 copy-done.7
  56.0 0.6 fusion.27
  56.6 0.1 multiply_subtract_fusion.12
  56.9 0.6 fusion.192
  57.5 0.6 fusion.39
  58.3 0.6 fusion.196
  58.9 0.6 fusion.51
  59.4 0.1 multiply_subtract_fusion.10
  59.7 0.6 fusion.200
  60.3 0.6 fusion.63
  61.1 0.6 fusion.204
  61.7 0.6 fusion.75
  62.3 0.1 multiply_subtract_fusion.8
  62.5 0.6 fusion.208
  63.1 0.6 fusion.87
  63.7 0.4 copy-done.6
  64.1 0.2 multiply_add_fusion.6
  64.4 0.6 fusion.212
  64.9 0.6 fusion.99
  65.5 0.1 add_bitcast_fusion
  65.6 0.1 multiply_add_fusion.5
  65.8 0.6 fusion.216
  66.4 0.6 fusion.111
  67.2 0.6 fusion.220
  67.8 0.6 fusion.123
  68.5 0.1 multiply_add_fusion.3
  68.7 0.6 fusion.224
  69.3 0.6 fusion.135
  70.1 0.6 fusion.228
  70.7 0.6 fusion.147
  71.2 0.3 add_bitcast_fusion.2
  71.8 0.6 fusion.232
  72.4 0.6 fusion.159
  73.1 0.6 fusion.236
  73.7 0.6 fusion.171
  74.3 0.1 fusion.281
  74.6 0.2 fusion.272
  74.9 1.9 %collective-permute-start.2 = (f32[2,256,256]{2,1,0:T(8,128)S(1)}, f32[2,256,256]{2,1,0:T(8,128)S(1)}, u32[]{:S(2)}, u32[]{:S(2)}) collective-permute-start(f32[2,256,256]{2,1,0:T(8,128)S(1)} %pad_dynamic-slice_fusion.7), channel_id=1, source_target_pairs={{0,4},{4,8},{8,12},{12,16},{16,20},{20,24},{24,28},{28,32},{32,36}... | collective-permute-start | bytes 1572872 | tf_op jit(solution)/shard_map/ppermute | solution.py:12
  76.8 2.0 %fusion = f32[1,2,256,1024]{3,2,1,0:T(8,128)} fusion(s32[]{:T(128)S(6)} %select_n.239, s32[]{:T(128)S(6)} %select_n.240, f32[2,256,256]{2,1,0:T(8,128)S(1)} %fusion.272), kind=kLoop, calls=%fused_computation.3 | loop fusion | bytes 2621448 | tf_op jit(solution)/shard_map/broadcast_in_dim | solution.py:209
  78.8 9.9 %collective-permute-done.2 = f32[2,256,256]{2,1,0:T(8,128)S(1)} collective-permute-done((f32[2,256,256]{2,1,0:T(8,128)S(1)}, f32[2,256,256]{2,1,0:T(8,128)S(1)}, u32[]{:S(2)}, u32[]{:S(2)}) %collective-permute-start.2) | collective-permute-done | bytes 524320 | tf_op jit(solution)/shard_map/ppermute | solution.py:12
  88.7 0.3 fusion.274
  89.0 3.7 %dynamic_update_slice.4 = f32[1,2,256,1024]{3,2,1,0:T(8,128)} dynamic-update-slice(f32[1,2,256,1024]{3,2,1,0:T(8,128)} %fusion, f32[1,2,256,256]{3,2,1,0:T(8,128)S(1)} %fusion.274, s32[]{:T(128)} %constant.89.clone.1, s32[]{:T(128)} %constant.89.clone.1, s32[]{:T(128)} %constant.89.clone.1, s32[]{:T(128)S(6)} %select_n.201) | dynamic-update-slice | bytes 1048580 | tf_op jit(solution)/shard_map/dynamic_update_slice | solution.py:208
  (49 shorter events, 3.0 us)
Async XLA Ops:
  0.0 13.4 %copy-start = (f32[1,2,256,1024]{3,2,1,0:T(8,128)S(1)}, f32[1,2,256,1024]{3,2,1,0:T(8,128)}, u32[]{:S(2)}) copy-start(f32[1,2,256,1024]{3,2,1,0:T(8,128)} %param.6) | copy-start | bytes 6291460
  1.5 8.2 %collective-permute-start = (s32[2]{0:T(128)S(1)}, s32[2]{0:T(128)S(1)}, u32[]{:S(2)}, u32[]{:S(2)}) collective-permute-start(s32[2]{0:T(128)S(1)} %pad_add_fusion), channel_id=1, source_target_pairs={{0,4},{4,8},{8,12},{12,16},{16,20},{20,24},{24,28},{28,32},{32,36}... | collective-permute-start | bytes 32 | tf_op jit(solution)/shard_map/ppermute | solution.py:12
  14.3 11.3 %collective-permute-start.1 = (f32[2,256,256]{2,1,0:T(8,128)S(1)}, f32[2,256,256]{2,1,0:T(8,128)S(1)}, u32[]{:S(2)}, u32[]{:S(2)}) collective-permute-start(f32[2,256,256]{2,1,0:T(8,128)S(1)} %pad_dynamic-slice_fusion.8), channel_id=1, source_target_pairs={{4,0},{8,4},{12,8},{16,12},{20,16},{24,20},{28,24},{32,28},{36,32}... | collective-permute-start | bytes 1572872 | tf_op jit(solution)/shard_map/ppermute | solution.py:12
  19.9 2.4 %copy-start.5 = (f32[256,256]{1,0:T(8,128)S(1)}, f32[256,256]{1,0:T(8,128)}, u32[]{:S(2)}) copy-start(f32[256,256]{1,0:T(8,128)} %param.8) | copy-start | bytes 786436
  49.3 1.8 %copy-start.1 = (f32[2,256,256]{2,1,0:T(8,128)S(1)}, f32[2,256,256]{2,1,0:T(8,128)}, u32[]{:S(2)}) copy-start(f32[2,256,256]{2,1,0:T(8,128)} %param.7) | copy-start | bytes 1572868
  51.2 1.0 %copy-start.3 = (bf16[512,512]{1,0:T(8,128)(2,1)S(1)}, bf16[512,512]{1,0:T(8,128)(2,1)}, u32[]{:S(2)}) copy-start(bf16[512,512]{1,0:T(8,128)(2,1)} %get-tuple-element.137) | copy-start | bytes 1572868
  51.2 1.2 %copy-start.4 = (bf16[512,512]{1,0:T(8,128)(2,1)S(1)}, bf16[512,512]{1,0:T(8,128)(2,1)}, u32[]{:S(2)}) copy-start(bf16[512,512]{1,0:T(8,128)(2,1)} %get-tuple-element.138) | copy-start | bytes 1572868
  52.4 0.9 %copy-start.9 = (bf16[256,512]{1,0:T(8,128)(2,1)S(1)}, bf16[256,512]{1,0:T(8,128)(2,1)}, u32[]{:S(2)}) copy-start(bf16[256,512]{1,0:T(8,128)(2,1)} %get-tuple-element.135) | copy-start | bytes 786436
  52.4 1.0 %copy-start.10 = (bf16[256,512]{1,0:T(8,128)(2,1)S(1)}, bf16[256,512]{1,0:T(8,128)(2,1)}, u32[]{:S(2)}) copy-start(bf16[256,512]{1,0:T(8,128)(2,1)} %get-tuple-element.136) | copy-start | bytes 786436
  54.0 1.0 %copy-start.2 = (bf16[512,512]{1,0:T(8,128)(2,1)S(1)}, bf16[512,512]{1,0:T(8,128)(2,1)}, u32[]{:S(2)}) copy-start(bf16[512,512]{1,0:T(8,128)(2,1)} %get-tuple-element.69) | copy-start | bytes 1572868
  55.0 0.9 %copy-start.7 = (bf16[256,512]{1,0:T(8,128)(2,1)S(1)}, bf16[256,512]{1,0:T(8,128)(2,1)}, u32[]{:S(2)}) copy-start(bf16[256,512]{1,0:T(8,128)(2,1)} %get-tuple-element.123) | copy-start | bytes 786436
  55.0 1.0 %copy-start.8 = (bf16[256,512]{1,0:T(8,128)(2,1)S(1)}, bf16[256,512]{1,0:T(8,128)(2,1)}, u32[]{:S(2)}) copy-start(bf16[256,512]{1,0:T(8,128)(2,1)} %get-tuple-element.124) | copy-start | bytes 786436
  63.1 1.0 %copy-start.6 = (f32[1,256,256]{2,1,0:T(8,128)S(1)}, f32[1,256,256]{2,1,0:T(8,128)}, u32[]{:S(2)}) copy-start(f32[1,256,256]{2,1,0:T(8,128)} %param.11) | copy-start | bytes 786436
  74.9 13.8 %collective-permute-start.2 = (f32[2,256,256]{2,1,0:T(8,128)S(1)}, f32[2,256,256]{2,1,0:T(8,128)S(1)}, u32[]{:S(2)}, u32[]{:S(2)}) collective-permute-start(f32[2,256,256]{2,1,0:T(8,128)S(1)} %pad_dynamic-slice_fusion.7), channel_id=1, source_target_pairs={{0,4},{4,8},{8,12},{12,16},{16,20},{20,24},{24,28},{28,32},{32,36}... | collective-permute-start | bytes 1572872 | tf_op jit(solution)/shard_map/ppermute | solution.py:12

commit v9 on v6

--- a/solution.py
+++ b/solution.py
@@ -70,7 +70,7 @@
     return jnp.concatenate([real_part, imag_part], axis=0)
 
 
-def exchange_kernel(window_ref, left_ref, right_ref, far_ref, send_sem, recv_sem):
+def exchange_kernel(window_ref, layers_ref, send_sem, recv_sem):
     devices = lax.axis_size("cuts")
     me = lax.axis_index("cuts")
     right = lax.rem(me + 1, devices)
@@ -91,18 +91,19 @@
             device_id_type=mesh_ids,
         )
 
-    passed_left = remote(window_ref.at[0], right_ref.at[0], 0, left)
-    passed_right = remote(window_ref.at[1], left_ref.at[1], 1, right)
+    passed_left = remote(window_ref.at[0], layers_ref.at[me, 0], 0, left)
+    passed_right = remote(window_ref.at[1], layers_ref.at[me, 1], 1, right)
     passed_left.start()
     passed_right.start()
+    layers_ref[me] = window_ref[...]
     passed_left.wait()
     passed_right.wait()
-    far_real = remote(right_ref.at[0], far_ref.at[0], 2, left)
-    far_imag = remote(left_ref.at[1], far_ref.at[1], 3, right)
+    far_real = remote(layers_ref.at[right, 0], layers_ref.at[right, 0], 2, left)
+    far_imag = remote(layers_ref.at[left, 1], layers_ref.at[left, 1], 3, right)
     far_real.start()
     far_imag.start()
-    kept_left = remote(window_ref.at[1], right_ref.at[1], 4, left)
-    kept_right = remote(window_ref.at[0], left_ref.at[0], 5, right)
+    kept_left = remote(window_ref.at[1], layers_ref.at[me, 1], 4, left)
+    kept_right = remote(window_ref.at[0], layers_ref.at[me, 0], 5, right)
     kept_left.start()
     kept_right.start()
     far_real.wait()
@@ -111,14 +112,14 @@
     kept_right.wait()
 
 
-def exchange(window):
-    shape = jax.ShapeDtypeStruct(window.shape, window.dtype)
+def exchange(window, sections):
+    shape = jax.ShapeDtypeStruct((sections,) + window.shape, window.dtype)
     vmem = pl.BlockSpec(memory_space=pltpu.VMEM)
     return pl.pallas_call(
         exchange_kernel,
-        out_shape=(shape, shape, shape),
+        out_shape=shape,
         in_specs=[vmem],
-        out_specs=(vmem, vmem, vmem),
+        out_specs=vmem,
         scratch_shapes=[pltpu.SemaphoreType.DMA((6,)), pltpu.SemaphoreType.DMA((6,))],
         compiler_params=pltpu.CompilerParams(collective_id=0, has_side_effects=True),
     )(window)
@@ -152,13 +153,13 @@
     window = kept + borrowed
 
     if sections == 4:
-        from_left, from_right, far = exchange(window)
-        have = [window, from_left, far, from_right]
+        stacked_layers = exchange(window, sections)
+        layers = [stacked_layers[layer] for layer in range(sections)]
     else:
         have = [window] + [rotated(window, "cuts", k) for k in range(1, sections)]
-    layers = [
-        lax.select_n((cut_index - layer) % sections, *have) for layer in range(sections)
-    ]
+        layers = [
+            lax.select_n((cut_index - layer) % sections, *have) for layer in range(sections)
+        ]
 
     wave_real = probe[0]
     wave_imag = probe[1]

time: 91.4 us -> 91.4 us (level)
    select_n x1 -> x0, other arithmetic: 1.8 us -> none  [per_device(): lax.select_n((cut_index - layer) % sections, *have)]
    sub x4, other arithmetic: 0.39 us -> 1.5 us  [per_device(): mixed_real = wave_real * layer_real - wave_imag * layer_imag]
    unnamed x22 -> x24, local copies, waits for them, and re-layouts: 3.1 us -> 3.17 us
where the time goes in v9:
time: 91.4 us; the launch traced here: 90.9 us
  Pallas kernels  22.9 us (25%)
  matrix products  16.1 us (18%)
  other arithmetic  16 us (18%)
  waiting for transfers between devices  15.2 us (17%)
  starting transfers between devices  8.4 us (9%)
  between operations  7.09 us (8%)
  local copies, waits for them, and re-layouts  5.26 us (6%)
    pallas_call x1, Pallas kernels, exchange(): pl.pallas_call(exchange_kernel, out_shape=shape, in_specs=[vmem], out_spe...  22.9 us
    ppermute x3, waiting for transfers between devices, shifted(): return lax.ppermute(value, axis, pairs)  15.2 us
    ppermute x3, starting transfers between devices, shifted(): return lax.ppermute(value, axis, pairs)  8.4 us
    dot_general x14, matrix products, split_dot(): return jnp.dot(split_table, operand, preferred_element_type=jnp.float32)  8.12 us
    dot_general x14, matrix products, split_dot(): return jnp.dot(operand, split_table, preferred_element_type=jnp.float32)  7.97 us
    convert_element_type x16, other arithmetic, halves(): return (high.astype(jnp.bfloat16), low.astype(jnp.bfloat16))  5.01 us
    unnamed x24, local copies, waits for them, and re-layouts  3.17 us
    mul x2, other arithmetic, dft_tables(): return (jnp.cos(angle) * factor, jnp.sin(angle) * factor)  2.74 us
  transfers between devices with their start and end apart: 3, of which 3 were waited for; matrix products, arithmetic and copies ran while one was open for 9% of the time, Pallas kernels for 0%

profile of v9, /device:TPU:128, one launch (start us, length us, event | category | flops | bytes accessed | tf_op | source)
XLA Modules:
  0.0 90.9 jit_solution(18367039093303126631)
XLA Ops:
  1.5 1.9 %collective-permute-start = (s32[2]{0:T(128)S(1)}, s32[2]{0:T(128)S(1)}, u32[]{:S(2)}, u32[]{:S(2)}) collective-permute-start(s32[2]{0:T(128)S(1)} %pad_add_fusion), channel_id=1, source_target_pairs={{0,4},{4,8},{8,12},{12,16},{16,20},{20,24},{24,28},{28,32},{32,36}... | collective-permute-start | bytes 32 | tf_op jit(solution)/shard_map/ppermute | solution.py:12
  3.4 1.1 %cosine_multiply_fusion = (f32[256,256]{1,0:T(8,128)S(1)}, f32[256,256]{1,0:T(8,128)S(1)}) fusion(), kind=kLoop, calls=%fused_computation.453 | loop fusion | flops 1048576 | bytes 524288 | tf_op jit(solution)/shard_map/mul | solution.py:26
  4.5 1.7 %broadcast_multiply_fusion.1 = (f32[256,256]{1,0:T(8,128)S(1)}, f32[256,256]{1,0:T(8,128)}) fusion(), kind=kLoop, calls=%fused_computation.458 | loop fusion | flops 1048576 | bytes 524288 | tf_op jit(solution)/shard_map/mul | solution.py:26
  6.2 1.1 %fusion.262 = (bf16[256,512]{1,0:T(8,128)(2,1)}, bf16[256,512]{1,0:T(8,128)(2,1)}, bf16[256,512]{1,0:T(8,128)(2,1)}, bf16[256,512]{1,0:T(8,128)(2,1)}) fusion(f32[256,256]{1,0:T(8,128)S(1)} %get-tuple-element.135, f32[256,256]{1,0:T(8,128)S(1)} %get-tuple-element.133, f32[256,256]{1,0:T(8,128)S(1)} %get-tuple-element.134), kind=kLoop, calls=%fused_computation.313 | loop fusion | flops 1835008 | bytes 1835008 | tf_op jit(solution)/shard_map/convert_element_type | solution.py:33
  7.3 2.4 %collective-permute-done = s32[2]{0:T(128)S(1)} collective-permute-done((s32[2]{0:T(128)S(1)}, s32[2]{0:T(128)S(1)}, u32[]{:S(2)}, u32[]{:S(2)}) %collective-permute-start) | collective-permute-done | bytes 40 | tf_op jit(solution)/shard_map/ppermute | solution.py:12
  9.7 0.6 fusion.332
  13.5 0.2 dynamic-slice_bitcast_fusion
  14.4 4.6 %collective-permute-start.1 = (f32[2,256,256]{2,1,0:T(8,128)S(1)}, f32[2,256,256]{2,1,0:T(8,128)S(1)}, u32[]{:S(2)}, u32[]{:S(2)}) collective-permute-start(f32[2,256,256]{2,1,0:T(8,128)S(1)} %pad_dynamic-slice_fusion.8), channel_id=1, source_target_pairs={{4,0},{8,4},{12,8},{16,12},{20,16},{24,20},{28,24},{32,28},{36,32}... | collective-permute-start | bytes 1572872 | tf_op jit(solution)/shard_map/ppermute | solution.py:12
  19.0 1.0 %fusion.302 = f32[256,256]{1,0:T(8,128)S(1)} fusion(), kind=kLoop, calls=%fused_computation.461 | loop fusion | flops 1048576 | bytes 262144 | tf_op jit(solution)/shard_map/neg | solution.py:39
  20.0 2.4 %fusion.3 = (bf16[512,512]{1,0:T(8,128)(2,1)S(1)}, bf16[512,512]{1,0:T(8,128)(2,1)}, bf16[512,512]{1,0:T(8,128)(2,1)}, bf16[512,512]{1,0:T(8,128)(2,1)}) fusion(f32[256,256]{1,0:T(8,128)S(1)} %get-tuple-element.133, f32[256,256]{1,0:T(8,128)S(1)} %get-tuple-element.135, f32[256,256]{1,0:T(8,128)} %get-tuple-element.136, ...), kind=kLoop, calls=%fused_computation.14 | loop fusion | flops 4718592 | bytes 3407872 | tf_op jit(solution)/shard_map/convert_element_type | solution.py:33
  22.4 1.1 %fusion.331 = (f32[256,256]{1,0:T(8,128)S(1)}, f32[256,256]{1,0:T(8,128)S(1)}) fusion(f32[256,256]{1,0:T(8,128)S(1)} %copy-done.6), kind=kLoop, calls=%fused_computation.491 | loop fusion | bytes 786432 | tf_op jit(solution)/shard_map/cos | solution.py:137
  23.5 2.2 %collective-permute-done.1 = f32[2,256,256]{2,1,0:T(8,128)S(1)} collective-permute-done((f32[2,256,256]{2,1,0:T(8,128)S(1)}, f32[2,256,256]{2,1,0:T(8,128)S(1)}, u32[]{:S(2)}, u32[]{:S(2)}) %collective-permute-start.1) | collective-permute-done | bytes 524320 | tf_op jit(solution)/shard_map/ppermute | solution.py:12
  25.7 1.0 %fusion.273.window_ref = f32[2,256,256]{2,1,0:T(8,128)} fusion(f32[2,256,256]{2,1,0:T(8,128)S(1)} %collective-permute-done.1, s32[]{:T(128)S(6)} %select_n.63, s32[]{:T(128)S(6)} %select_n.64, f32[2,256,1024]{2,1,0:T(8,128)S(1)} %bitcast.174), kind=kLoop, calls=%fused_computation.324 | loop fusion | flops 131072 | bytes 3145736 | tf_op jit(solution)/shard_map/add | solution.py:153
  26.7 22.9 %shard_map.64 = f32[4,2,256,256]{3,2,1,0:T(8,128)} custom-call(f32[2,256,256]{2,1,0:T(8,128)} %fusion.273.window_ref), custom_call_target="tpu_custom_call" | custom-call | tf_op jit(solution)/shard_map/pallas_call | solution.py:118
  49.7 1.2 %fusion.289 = (f32[256,256]{1,0:T(8,128)S(1)}, f32[256,256]{1,0:T(8,128)S(1)}) fusion(f32[4,2,256,256]{3,2,1,0:T(8,128)} %shard_map.64, f32[2,256,256]{2,1,0:T(8,128)S(1)} %copy-done.2), kind=kLoop, calls=%fused_computation.405 | loop fusion | flops 393216 | bytes 1572864 | tf_op jit(solution)/shard_map/sub | solution.py:171
  51.0 0.6 fusion.181
  51.6 0.4 copy-done.10
  52.0 0.6 fusion.16
  52.6 0.1 multiply_subtract_fusion.7
  52.8 0.8 copy-done.3
  53.7 0.6 fusion.187
  54.2 0.4 copy-done.8
  54.7 0.6 fusion.28
  55.3 1.0 %copy-done = f32[4,2,256,256]{3,2,1,0:T(8,128)S(1)} copy-done((f32[4,2,256,256]{3,2,1,0:T(8,128)S(1)}, f32[4,2,256,256]{3,2,1,0:T(8,128)}, u32[]{:S(2)}) %copy-start) | copy-done | bytes 2097176
  56.6 0.6 fusion.193
  57.1 0.6 fusion.40
  57.9 0.6 fusion.197
  58.5 0.6 fusion.52
  59.1 0.1 fusion.281
  59.4 0.6 fusion.201
  60.0 0.6 fusion.64
  60.7 0.6 fusion.205
  61.3 0.6 fusion.76
  61.9 0.1 fusion.277
  62.2 0.6 fusion.209
  62.8 0.6 fusion.88
  63.4 0.4 copy-done.7
  63.7 0.2 multiply_add_fusion.3
  64.0 0.6 fusion.213
  64.6 0.6 fusion.100
  65.2 0.1 add_bitcast_fusion
  65.3 0.1 fusion.279
  65.5 0.6 fusion.217
  66.1 0.6 fusion.112
  66.9 0.6 fusion.221
  67.5 0.6 fusion.124
  68.0 0.1 add_bitcast_fusion.1
  68.1 0.1 fusion.283
  68.4 0.6 fusion.225
  68.9 0.6 fusion.136
  69.7 0.6 fusion.229
  70.3 0.6 fusion.148
  70.9 0.1 add_bitcast_fusion.2
  71.0 0.1 fusion.287
  71.1 0.3 fusion.241
  71.4 0.6 fusion.233
  72.0 0.6 fusion.160
  72.8 0.6 fusion.237
  73.4 0.6 fusion.172
  74.0 0.1 fusion.292
  74.3 0.2 fusion.272
  74.5 1.9 %collective-permute-start.2 = (f32[2,256,256]{2,1,0:T(8,128)S(1)}, f32[2,256,256]{2,1,0:T(8,128)S(1)}, u32[]{:S(2)}, u32[]{:S(2)}) collective-permute-start(f32[2,256,256]{2,1,0:T(8,128)S(1)} %pad_dynamic-slice_fusion.7), channel_id=1, source_target_pairs={{0,4},{4,8},{8,12},{12,16},{16,20},{20,24},{24,28},{28,32},{32,36}... | collective-permute-start | bytes 1572872 | tf_op jit(solution)/shard_map/ppermute | solution.py:12
  77.7 10.6 %collective-permute-done.2 = f32[2,256,256]{2,1,0:T(8,128)S(1)} collective-permute-done((f32[2,256,256]{2,1,0:T(8,128)S(1)}, f32[2,256,256]{2,1,0:T(8,128)S(1)}, u32[]{:S(2)}, u32[]{:S(2)}) %collective-permute-start.2) | collective-permute-done | bytes 524320 | tf_op jit(solution)/shard_map/ppermute | solution.py:12
  88.3 2.6 %fusion.1 = f32[1,2,256,1024]{3,2,1,0:T(8,128)} fusion(s32[]{:T(128)S(6)} %select_n.71, f32[2,256,256]{2,1,0:T(8,128)S(1)} %collective-permute-done.2, s32[]{:T(128)S(6)} %select_n.68, s32[]{:T(128)S(6)} %select_n.69, f32[2,256,256]{2,1,0:T(8,128)S(1)} %fusion.272), kind=kLoop, calls=%fused_computation.4 | loop fusion | flops 524288 | bytes 3145740 | tf_op jit(solution)/shard_map/broadcast_in_dim | solution.py:211
  (48 shorter events, 2.7 us)
Async XLA Ops:
  0.0 13.5 %copy-start.1 = (f32[1,2,256,1024]{3,2,1,0:T(8,128)S(1)}, f32[1,2,256,1024]{3,2,1,0:T(8,128)}, u32[]{:S(2)}) copy-start(f32[1,2,256,1024]{3,2,1,0:T(8,128)} %param.6) | copy-start | bytes 6291460
  1.5 8.2 %collective-permute-start = (s32[2]{0:T(128)S(1)}, s32[2]{0:T(128)S(1)}, u32[]{:S(2)}, u32[]{:S(2)}) collective-permute-start(s32[2]{0:T(128)S(1)} %pad_add_fusion), channel_id=1, source_target_pairs={{0,4},{4,8},{8,12},{12,16},{16,20},{20,24},{24,28},{28,32},{32,36}... | collective-permute-start | bytes 32 | tf_op jit(solution)/shard_map/ppermute | solution.py:12
  14.4 11.3 %collective-permute-start.1 = (f32[2,256,256]{2,1,0:T(8,128)S(1)}, f32[2,256,256]{2,1,0:T(8,128)S(1)}, u32[]{:S(2)}, u32[]{:S(2)}) collective-permute-start(f32[2,256,256]{2,1,0:T(8,128)S(1)} %pad_dynamic-slice_fusion.8), channel_id=1, source_target_pairs={{4,0},{8,4},{12,8},{16,12},{20,16},{24,20},{28,24},{32,28},{36,32}... | collective-permute-start | bytes 1572872 | tf_op jit(solution)/shard_map/ppermute | solution.py:12
  20.0 2.4 %copy-start.6 = (f32[256,256]{1,0:T(8,128)S(1)}, f32[256,256]{1,0:T(8,128)}, u32[]{:S(2)}) copy-start(f32[256,256]{1,0:T(8,128)} %param.8) | copy-start | bytes 786436
  26.7 23.0 %copy-start.2 = (f32[2,256,256]{2,1,0:T(8,128)S(1)}, f32[2,256,256]{2,1,0:T(8,128)}, u32[]{:S(2)}) copy-start(f32[2,256,256]{2,1,0:T(8,128)} %param.7) | copy-start | bytes 1572868
  49.6 1.3 %copy-start.4 = (bf16[512,512]{1,0:T(8,128)(2,1)S(1)}, bf16[512,512]{1,0:T(8,128)(2,1)}, u32[]{:S(2)}) copy-start(bf16[512,512]{1,0:T(8,128)(2,1)} %get-tuple-element.127) | copy-start | bytes 1572868
  49.7 1.3 %copy-start.5 = (bf16[512,512]{1,0:T(8,128)(2,1)S(1)}, bf16[512,512]{1,0:T(8,128)(2,1)}, u32[]{:S(2)}) copy-start(bf16[512,512]{1,0:T(8,128)(2,1)} %get-tuple-element.128) | copy-start | bytes 1572868
  51.0 0.9 %copy-start.10 = (bf16[256,512]{1,0:T(8,128)(2,1)S(1)}, bf16[256,512]{1,0:T(8,128)(2,1)}, u32[]{:S(2)}) copy-start(bf16[256,512]{1,0:T(8,128)(2,1)} %get-tuple-element.125) | copy-start | bytes 786436
  51.0 1.0 %copy-start.11 = (bf16[256,512]{1,0:T(8,128)(2,1)S(1)}, bf16[256,512]{1,0:T(8,128)(2,1)}, u32[]{:S(2)}) copy-start(bf16[256,512]{1,0:T(8,128)(2,1)} %get-tuple-element.126) | copy-start | bytes 786436
  52.6 1.0 %copy-start.3 = (bf16[512,512]{1,0:T(8,128)(2,1)S(1)}, bf16[512,512]{1,0:T(8,128)(2,1)}, u32[]{:S(2)}) copy-start(bf16[512,512]{1,0:T(8,128)(2,1)} %get-tuple-element.59) | copy-start | bytes 1572868
  53.7 0.9 %copy-start.8 = (bf16[256,512]{1,0:T(8,128)(2,1)S(1)}, bf16[256,512]{1,0:T(8,128)(2,1)}, u32[]{:S(2)}) copy-start(bf16[256,512]{1,0:T(8,128)(2,1)} %get-tuple-element.113) | copy-start | bytes 786436
  53.7 1.0 %copy-start.9 = (bf16[256,512]{1,0:T(8,128)(2,1)S(1)}, bf16[256,512]{1,0:T(8,128)(2,1)}, u32[]{:S(2)}) copy-start(bf16[256,512]{1,0:T(8,128)(2,1)} %get-tuple-element.114) | copy-start | bytes 786436
  54.7 1.6 %copy-start = (f32[4,2,256,256]{3,2,1,0:T(8,128)S(1)}, f32[4,2,256,256]{3,2,1,0:T(8,128)}, u32[]{:S(2)}) copy-start(f32[4,2,256,256]{3,2,1,0:T(8,128)} %shard_map.64) | copy-start | bytes 6291460
  62.8 1.0 %copy-start.7 = (f32[1,256,256]{2,1,0:T(8,128)S(1)}, f32[1,256,256]{2,1,0:T(8,128)}, u32[]{:S(2)}) copy-start(f32[1,256,256]{2,1,0:T(8,128)} %param.11) | copy-start | bytes 786436
  74.5 13.8 %collective-permute-start.2 = (f32[2,256,256]{2,1,0:T(8,128)S(1)}, f32[2,256,256]{2,1,0:T(8,128)S(1)}, u32[]{:S(2)}, u32[]{:S(2)}) collective-permute-start(f32[2,256,256]{2,1,0:T(8,128)S(1)} %pad_dynamic-slice_fusion.7), channel_id=1, source_target_pairs={{0,4},{4,8},{8,12},{12,16},{16,20},{20,24},{24,28},{28,32},{32,36}... | collective-permute-start | bytes 1572872 | tf_op jit(solution)/shard_map/ppermute | solution.py:12

commit v10 on v9

--- a/solution.py
+++ b/solution.py
@@ -81,35 +81,49 @@
         pl.semaphore_signal(barrier, inc=1, device_id={"cuts": neighbour}, device_id_type=mesh_ids)
     pl.semaphore_wait(barrier, 2)
 
+    rows = window_ref.shape[1]
+    half = rows // 2
+
     def remote(source, target, slot, neighbour):
-        return pltpu.make_async_remote_copy(
-            src_ref=source,
-            dst_ref=target,
-            send_sem=send_sem.at[slot],
-            recv_sem=recv_sem.at[slot],
-            device_id={"cuts": neighbour},
-            device_id_type=mesh_ids,
-        )
+        return [
+            pltpu.make_async_remote_copy(
+                src_ref=source.at[pl.ds(part * half, half)],
+                dst_ref=target.at[pl.ds(part * half, half)],
+                send_sem=send_sem.at[2 * slot + part],
+                recv_sem=recv_sem.at[2 * slot + part],
+                device_id={"cuts": neighbour},
+                device_id_type=mesh_ids,
+            )
+            for part in range(2)
+        ]
+
+    def start(copies):
+        for copy in copies:
+            copy.start()
+
+    def wait(copies):
+        for copy in copies:
+            copy.wait()
 
     passed_left = remote(window_ref.at[0], layers_ref.at[me, 0], 0, left)
     passed_right = remote(window_ref.at[1], layers_ref.at[me, 1], 1, right)
-    passed_left.start()
-    passed_right.start()
+    start(passed_left)
+    start(passed_right)
     layers_ref[me] = window_ref[...]
-    passed_left.wait()
-    passed_right.wait()
+    wait(passed_left)
+    wait(passed_right)
     far_real = remote(layers_ref.at[right, 0], layers_ref.at[right, 0], 2, left)
     far_imag = remote(layers_ref.at[left, 1], layers_ref.at[left, 1], 3, right)
-    far_real.start()
-    far_imag.start()
+    start(far_real)
+    start(far_imag)
     kept_left = remote(window_ref.at[1], layers_ref.at[me, 1], 4, left)
     kept_right = remote(window_ref.at[0], layers_ref.at[me, 0], 5, right)
-    kept_left.start()
-    kept_right.start()
-    far_real.wait()
-    far_imag.wait()
-    kept_left.wait()
-    kept_right.wait()
+    start(kept_left)
+    start(kept_right)
+    wait(far_real)
+    wait(far_imag)
+    wait(kept_left)
+    wait(kept_right)
 
 
 def exchange(window, sections):
@@ -120,7 +134,7 @@
         out_shape=shape,
         in_specs=[vmem],
         out_specs=vmem,
-        scratch_shapes=[pltpu.SemaphoreType.DMA((6,)), pltpu.SemaphoreType.DMA((6,))],
+        scratch_shapes=[pltpu.SemaphoreType.DMA((12,)), pltpu.SemaphoreType.DMA((12,))],
         compiler_params=pltpu.CompilerParams(collective_id=0, has_side_effects=True),
     )(window)
 

time: 91.4 us -> 91.5 us (level)
  no operation moved by 1% of the time
where the time goes in v10:
time: 91.5 us; the launch traced here: 91 us
  Pallas kernels  23.1 us (25%)
  matrix products  16.1 us (18%)
  other arithmetic  16 us (17%)
  waiting for transfers between devices  15.2 us (17%)
  starting transfers between devices  8.4 us (9%)
  between operations  7.09 us (8%)
  local copies, waits for them, and re-layouts  5.26 us (6%)
    pallas_call x1, Pallas kernels, exchange(): pl.pallas_call(exchange_kernel, out_shape=shape, in_specs=[vmem], out_spe...  23.1 us
    ppermute x3, waiting for transfers between devices, shifted(): return lax.ppermute(value, axis, pairs)  15.2 us
    ppermute x3, starting transfers between devices, shifted(): return lax.ppermute(value, axis, pairs)  8.4 us
    dot_general x14, matrix products, split_dot(): return jnp.dot(split_table, operand, preferred_element_type=jnp.float32)  8.11 us
    dot_general x14, matrix products, split_dot(): return jnp.dot(operand, split_table, preferred_element_type=jnp.float32)  7.97 us
    convert_element_type x16, other arithmetic, halves(): return (high.astype(jnp.bfloat16), low.astype(jnp.bfloat16))  4.79 us
    unnamed x24, local copies, waits for them, and re-layouts  3.17 us
    mul x2, other arithmetic, dft_tables(): return (jnp.cos(angle) * factor, jnp.sin(angle) * factor)  2.74 us
  transfers between devices with their start and end apart: 3, of which 3 were waited for; matrix products, arithmetic and copies ran while one was open for 9% of the time, Pallas kernels for 0%

profile of v10, /device:TPU:128, one launch (start us, length us, event | category | flops | bytes accessed | tf_op | source)
XLA Modules:
  0.0 91.0 jit_solution(13343471798421031549)
XLA Ops:
  1.5 1.9 %collective-permute-start = (s32[2]{0:T(128)S(1)}, s32[2]{0:T(128)S(1)}, u32[]{:S(2)}, u32[]{:S(2)}) collective-permute-start(s32[2]{0:T(128)S(1)} %pad_add_fusion), channel_id=1, source_target_pairs={{0,4},{4,8},{8,12},{12,16},{16,20},{20,24},{24,28},{28,32},{32,36}... | collective-permute-start | bytes 32 | tf_op jit(solution)/shard_map/ppermute | solution.py:12
  3.4 1.1 %cosine_multiply_fusion = (f32[256,256]{1,0:T(8,128)S(1)}, f32[256,256]{1,0:T(8,128)S(1)}) fusion(), kind=kLoop, calls=%fused_computation.453 | loop fusion | flops 1048576 | bytes 524288 | tf_op jit(solution)/shard_map/mul | solution.py:26
  4.5 1.7 %broadcast_multiply_fusion.1 = (f32[256,256]{1,0:T(8,128)S(1)}, f32[256,256]{1,0:T(8,128)}) fusion(), kind=kLoop, calls=%fused_computation.458 | loop fusion | flops 1048576 | bytes 524288 | tf_op jit(solution)/shard_map/mul | solution.py:26
  6.2 1.1 %fusion.262 = (bf16[256,512]{1,0:T(8,128)(2,1)}, bf16[256,512]{1,0:T(8,128)(2,1)}, bf16[256,512]{1,0:T(8,128)(2,1)}, bf16[256,512]{1,0:T(8,128)(2,1)}) fusion(f32[256,256]{1,0:T(8,128)S(1)} %get-tuple-element.135, f32[256,256]{1,0:T(8,128)S(1)} %get-tuple-element.133, f32[256,256]{1,0:T(8,128)S(1)} %get-tuple-element.134), kind=kLoop, calls=%fused_computation.313 | loop fusion | flops 1835008 | bytes 1835008 | tf_op jit(solution)/shard_map/convert_element_type | solution.py:33
  7.3 2.4 %collective-permute-done = s32[2]{0:T(128)S(1)} collective-permute-done((s32[2]{0:T(128)S(1)}, s32[2]{0:T(128)S(1)}, u32[]{:S(2)}, u32[]{:S(2)}) %collective-permute-start) | collective-permute-done | bytes 40 | tf_op jit(solution)/shard_map/ppermute | solution.py:12
  9.7 0.6 fusion.332
  13.5 0.2 dynamic-slice_bitcast_fusion
  14.4 4.6 %collective-permute-start.1 = (f32[2,256,256]{2,1,0:T(8,128)S(1)}, f32[2,256,256]{2,1,0:T(8,128)S(1)}, u32[]{:S(2)}, u32[]{:S(2)}) collective-permute-start(f32[2,256,256]{2,1,0:T(8,128)S(1)} %pad_dynamic-slice_fusion.8), channel_id=1, source_target_pairs={{4,0},{8,4},{12,8},{16,12},{20,16},{24,20},{28,24},{32,28},{36,32}... | collective-permute-start | bytes 1572872 | tf_op jit(solution)/shard_map/ppermute | solution.py:12
  19.0 1.0 %fusion.302 = f32[256,256]{1,0:T(8,128)S(1)} fusion(), kind=kLoop, calls=%fused_computation.461 | loop fusion | flops 1048576 | bytes 262144 | tf_op jit(solution)/shard_map/neg | solution.py:39
  20.0 2.4 %fusion.3 = (bf16[512,512]{1,0:T(8,128)(2,1)S(1)}, bf16[512,512]{1,0:T(8,128)(2,1)}, bf16[512,512]{1,0:T(8,128)(2,1)}, bf16[512,512]{1,0:T(8,128)(2,1)}) fusion(f32[256,256]{1,0:T(8,128)S(1)} %get-tuple-element.133, f32[256,256]{1,0:T(8,128)S(1)} %get-tuple-element.135, f32[256,256]{1,0:T(8,128)} %get-tuple-element.136, ...), kind=kLoop, calls=%fused_computation.14 | loop fusion | flops 4718592 | bytes 3407872 | tf_op jit(solution)/shard_map/convert_element_type | solution.py:33
  22.4 1.1 %fusion.331 = (f32[256,256]{1,0:T(8,128)S(1)}, f32[256,256]{1,0:T(8,128)S(1)}) fusion(f32[256,256]{1,0:T(8,128)S(1)} %copy-done.6), kind=kLoop, calls=%fused_computation.491 | loop fusion | bytes 786432 | tf_op jit(solution)/shard_map/cos | solution.py:151
  23.5 2.2 %collective-permute-done.1 = f32[2,256,256]{2,1,0:T(8,128)S(1)} collective-permute-done((f32[2,256,256]{2,1,0:T(8,128)S(1)}, f32[2,256,256]{2,1,0:T(8,128)S(1)}, u32[]{:S(2)}, u32[]{:S(2)}) %collective-permute-start.1) | collective-permute-done | bytes 524320 | tf_op jit(solution)/shard_map/ppermute | solution.py:12
  25.7 1.0 %fusion.273.window_ref = f32[2,256,256]{2,1,0:T(8,128)} fusion(f32[2,256,256]{2,1,0:T(8,128)S(1)} %collective-permute-done.1, s32[]{:T(128)S(6)} %select_n.63, s32[]{:T(128)S(6)} %select_n.64, f32[2,256,1024]{2,1,0:T(8,128)S(1)} %bitcast.174), kind=kLoop, calls=%fused_computation.324 | loop fusion | flops 131072 | bytes 3145736 | tf_op jit(solution)/shard_map/add | solution.py:167
  26.7 23.1 %shard_map.64 = f32[4,2,256,256]{3,2,1,0:T(8,128)} custom-call(f32[2,256,256]{2,1,0:T(8,128)} %fusion.273.window_ref), custom_call_target="tpu_custom_call" | custom-call | tf_op jit(solution)/shard_map/pallas_call | solution.py:132
  49.8 1.2 %fusion.289 = (f32[256,256]{1,0:T(8,128)S(1)}, f32[256,256]{1,0:T(8,128)S(1)}) fusion(f32[4,2,256,256]{3,2,1,0:T(8,128)} %shard_map.64, f32[2,256,256]{2,1,0:T(8,128)S(1)} %copy-done.2), kind=kLoop, calls=%fused_computation.405 | loop fusion | flops 393216 | bytes 1572864 | tf_op jit(solution)/shard_map/sub | solution.py:185
  51.1 0.6 fusion.181
  51.7 0.4 copy-done.10
  52.1 0.6 fusion.16
  52.7 0.1 multiply_subtract_fusion.7
  52.9 0.8 copy-done.3
  53.8 0.6 fusion.187
  54.4 0.4 copy-done.8
  54.8 0.6 fusion.28
  55.4 1.0 %copy-done = f32[4,2,256,256]{3,2,1,0:T(8,128)S(1)} copy-done((f32[4,2,256,256]{3,2,1,0:T(8,128)S(1)}, f32[4,2,256,256]{3,2,1,0:T(8,128)}, u32[]{:S(2)}) %copy-start) | copy-done | bytes 2097176
  56.4 0.1 fusion.285
  56.7 0.6 fusion.193
  57.3 0.6 fusion.40
  58.0 0.6 fusion.197
  58.6 0.6 fusion.52
  59.2 0.1 fusion.281
  59.5 0.6 fusion.201
  60.1 0.6 fusion.64
  60.9 0.6 fusion.205
  61.4 0.6 fusion.76
  62.0 0.1 fusion.277
  62.3 0.6 fusion.209
  62.9 0.6 fusion.88
  63.5 0.4 copy-done.7
  63.8 0.2 multiply_add_fusion.3
  64.1 0.6 fusion.213
  64.7 0.6 fusion.100
  65.3 0.1 add_bitcast_fusion
  65.4 0.1 fusion.279
  65.6 0.6 fusion.217
  66.2 0.6 fusion.112
  67.0 0.6 fusion.221
  67.6 0.6 fusion.124
  68.1 0.1 add_bitcast_fusion.1
  68.3 0.1 fusion.283
  68.5 0.6 fusion.225
  69.1 0.6 fusion.136
  69.8 0.6 fusion.229
  70.4 0.6 fusion.148
  71.0 0.1 add_bitcast_fusion.2
  71.1 0.3 fusion.287
  71.5 0.6 fusion.233
  72.1 0.6 fusion.160
  72.9 0.6 fusion.237
  73.5 0.6 fusion.172
  74.1 0.1 fusion.292
  74.4 0.2 fusion.272
  74.6 1.9 %collective-permute-start.2 = (f32[2,256,256]{2,1,0:T(8,128)S(1)}, f32[2,256,256]{2,1,0:T(8,128)S(1)}, u32[]{:S(2)}, u32[]{:S(2)}) collective-permute-start(f32[2,256,256]{2,1,0:T(8,128)S(1)} %pad_dynamic-slice_fusion.7), channel_id=1, source_target_pairs={{0,4},{4,8},{8,12},{12,16},{16,20},{20,24},{24,28},{28,32},{32,36}... | collective-permute-start | bytes 1572872 | tf_op jit(solution)/shard_map/ppermute | solution.py:12
  77.8 10.6 %collective-permute-done.2 = f32[2,256,256]{2,1,0:T(8,128)S(1)} collective-permute-done((f32[2,256,256]{2,1,0:T(8,128)S(1)}, f32[2,256,256]{2,1,0:T(8,128)S(1)}, u32[]{:S(2)}, u32[]{:S(2)}) %collective-permute-start.2) | collective-permute-done | bytes 524320 | tf_op jit(solution)/shard_map/ppermute | solution.py:12
  88.5 2.6 %fusion.1 = f32[1,2,256,1024]{3,2,1,0:T(8,128)} fusion(s32[]{:T(128)S(6)} %select_n.71, f32[2,256,256]{2,1,0:T(8,128)S(1)} %collective-permute-done.2, s32[]{:T(128)S(6)} %select_n.68, s32[]{:T(128)S(6)} %select_n.69, f32[2,256,256]{2,1,0:T(8,128)S(1)} %fusion.272), kind=kLoop, calls=%fused_computation.4 | loop fusion | flops 524288 | bytes 3145740 | tf_op jit(solution)/shard_map/broadcast_in_dim | solution.py:225
  (48 shorter events, 2.6 us)
Async XLA Ops:
  0.0 13.5 %copy-start.1 = (f32[1,2,256,1024]{3,2,1,0:T(8,128)S(1)}, f32[1,2,256,1024]{3,2,1,0:T(8,128)}, u32[]{:S(2)}) copy-start(f32[1,2,256,1024]{3,2,1,0:T(8,128)} %param.6) | copy-start | bytes 6291460
  1.5 8.2 %collective-permute-start = (s32[2]{0:T(128)S(1)}, s32[2]{0:T(128)S(1)}, u32[]{:S(2)}, u32[]{:S(2)}) collective-permute-start(s32[2]{0:T(128)S(1)} %pad_add_fusion), channel_id=1, source_target_pairs={{0,4},{4,8},{8,12},{12,16},{16,20},{20,24},{24,28},{28,32},{32,36}... | collective-permute-start | bytes 32 | tf_op jit(solution)/shard_map/ppermute | solution.py:12
  14.4 11.3 %collective-permute-start.1 = (f32[2,256,256]{2,1,0:T(8,128)S(1)}, f32[2,256,256]{2,1,0:T(8,128)S(1)}, u32[]{:S(2)}, u32[]{:S(2)}) collective-permute-start(f32[2,256,256]{2,1,0:T(8,128)S(1)} %pad_dynamic-slice_fusion.8), channel_id=1, source_target_pairs={{4,0},{8,4},{12,8},{16,12},{20,16},{24,20},{28,24},{32,28},{36,32}... | collective-permute-start | bytes 1572872 | tf_op jit(solution)/shard_map/ppermute | solution.py:12
  20.0 2.4 %copy-start.6 = (f32[256,256]{1,0:T(8,128)S(1)}, f32[256,256]{1,0:T(8,128)}, u32[]{:S(2)}) copy-start(f32[256,256]{1,0:T(8,128)} %param.8) | copy-start | bytes 786436
  26.7 23.1 %copy-start.2 = (f32[2,256,256]{2,1,0:T(8,128)S(1)}, f32[2,256,256]{2,1,0:T(8,128)}, u32[]{:S(2)}) copy-start(f32[2,256,256]{2,1,0:T(8,128)} %param.7) | copy-start | bytes 1572868
  49.8 1.3 %copy-start.4 = (bf16[512,512]{1,0:T(8,128)(2,1)S(1)}, bf16[512,512]{1,0:T(8,128)(2,1)}, u32[]{:S(2)}) copy-start(bf16[512,512]{1,0:T(8,128)(2,1)} %get-tuple-element.127) | copy-start | bytes 1572868
  49.8 1.3 %copy-start.5 = (bf16[512,512]{1,0:T(8,128)(2,1)S(1)}, bf16[512,512]{1,0:T(8,128)(2,1)}, u32[]{:S(2)}) copy-start(bf16[512,512]{1,0:T(8,128)(2,1)} %get-tuple-element.128) | copy-start | bytes 1572868
  51.1 0.9 %copy-start.10 = (bf16[256,512]{1,0:T(8,128)(2,1)S(1)}, bf16[256,512]{1,0:T(8,128)(2,1)}, u32[]{:S(2)}) copy-start(bf16[256,512]{1,0:T(8,128)(2,1)} %get-tuple-element.125) | copy-start | bytes 786436
  51.1 1.0 %copy-start.11 = (bf16[256,512]{1,0:T(8,128)(2,1)S(1)}, bf16[256,512]{1,0:T(8,128)(2,1)}, u32[]{:S(2)}) copy-start(bf16[256,512]{1,0:T(8,128)(2,1)} %get-tuple-element.126) | copy-start | bytes 786436
  52.7 1.0 %copy-start.3 = (bf16[512,512]{1,0:T(8,128)(2,1)S(1)}, bf16[512,512]{1,0:T(8,128)(2,1)}, u32[]{:S(2)}) copy-start(bf16[512,512]{1,0:T(8,128)(2,1)} %get-tuple-element.59) | copy-start | bytes 1572868
  53.8 0.9 %copy-start.8 = (bf16[256,512]{1,0:T(8,128)(2,1)S(1)}, bf16[256,512]{1,0:T(8,128)(2,1)}, u32[]{:S(2)}) copy-start(bf16[256,512]{1,0:T(8,128)(2,1)} %get-tuple-element.113) | copy-start | bytes 786436
  53.8 1.0 %copy-start.9 = (bf16[256,512]{1,0:T(8,128)(2,1)S(1)}, bf16[256,512]{1,0:T(8,128)(2,1)}, u32[]{:S(2)}) copy-start(bf16[256,512]{1,0:T(8,128)(2,1)} %get-tuple-element.114) | copy-start | bytes 786436
  54.8 1.6 %copy-start = (f32[4,2,256,256]{3,2,1,0:T(8,128)S(1)}, f32[4,2,256,256]{3,2,1,0:T(8,128)}, u32[]{:S(2)}) copy-start(f32[4,2,256,256]{3,2,1,0:T(8,128)} %shard_map.64) | copy-start | bytes 6291460
  62.9 1.0 %copy-start.7 = (f32[1,256,256]{2,1,0:T(8,128)S(1)}, f32[1,256,256]{2,1,0:T(8,128)}, u32[]{:S(2)}) copy-start(f32[1,256,256]{2,1,0:T(8,128)} %param.11) | copy-start | bytes 786436
  74.6 13.8 %collective-permute-start.2 = (f32[2,256,256]{2,1,0:T(8,128)S(1)}, f32[2,256,256]{2,1,0:T(8,128)S(1)}, u32[]{:S(2)}, u32[]{:S(2)}) collective-permute-start(f32[2,256,256]{2,1,0:T(8,128)S(1)} %pad_dynamic-slice_fusion.7), channel_id=1, source_target_pairs={{0,4},{4,8},{8,12},{12,16},{16,20},{20,24},{24,28},{28,32},{32,36}... | collective-permute-start | bytes 1572872 | tf_op jit(solution)/shard_map/ppermute | solution.py:12

commit v11 on v9

--- a/solution.py
+++ b/solution.py
@@ -147,7 +147,7 @@
     lent = lax.dynamic_slice(strip, (zero, zero, column_above), (2, width, width))
     lent = jnp.pad(lent, ((0, 0), (width, 0), (0, 0)))
     lent = lax.dynamic_slice(lent, (zero, row_above, zero), (2, width, width))
-    borrowed = shifted(lent, "tile", -1)
+    borrowed = jnp.stack([shifted(lent[0], "tile", -1), shifted(lent[1], "tile", -1)], axis=0)
     kept = jnp.pad(strip, ((0, 0), (0, width), (0, 0)))
     kept = lax.dynamic_slice(kept, (zero, row, column), (2, width, width))
     window = kept + borrowed
@@ -201,7 +201,7 @@
 
     padded = jnp.concatenate([piece, jnp.zeros_like(piece)], axis=1)
     spill = lax.dynamic_slice(padded, (zero, rows - row, zero), (2, width, width))
-    arrived = shifted(spill, "tile", 1)
+    arrived = jnp.stack([shifted(spill[0], "tile", 1), shifted(spill[1], "tile", 1)], axis=0)
 
     own = jnp.pad(piece, ((0, 0), (rows, rows), (columns, columns)))
     own = lax.dynamic_slice(own, (zero, rows - row, columns - column), (2, rows, columns))

time: 91.4 us -> 94.4 us (1.033)
  starting transfers between devices: 8.4 us -> 16.1 us
  waiting for transfers between devices: 15.2 us -> 10.3 us
    ppermute x3 -> x5, starting transfers between devices: 8.4 us -> 16.1 us  [shifted(): return lax.ppermute(value, axis, pairs)]
    ppermute x3 -> x5, waiting for transfers between devices: 15.2 us -> 10.3 us  [shifted(): return lax.ppermute(value, axis, pairs)]
    add x1, other arithmetic: 1.01 us -> 2.03 us  [per_device(): window = kept + borrowed]
    convert_element_type x16, other arithmetic: 5.01 us -> 4.05 us  [halves(): return (high.astype(jnp.bfloat16), low.astype(jnp.bfloat16))]
    squeeze x0 -> x2, local copies, waits for them, and re-layouts: none -> 0.95 us  [the longest x1 0.87 us: per_device(): lent[0]]
  transfers between devices with their start and end apart: 3 -> 5, of which waited for: 3 -> 5; matrix products, arithmetic and copies ran while one was open for 9% -> 7% of each run, Pallas kernels for 0% -> 0%
where the time goes in v11:
time: 94.4 us; the launch traced here: 93.8 us
  Pallas kernels  23 us (24%)
  starting transfers between devices  16.1 us (17%)
  matrix products  16.1 us (17%)
  other arithmetic  15.3 us (16%)
  waiting for transfers between devices  10.3 us (11%)
  between operations  6.95 us (7%)
  local copies, waits for them, and re-layouts  6.12 us (6%)
    pallas_call x1, Pallas kernels, exchange(): pl.pallas_call(exchange_kernel, out_shape=shape, in_specs=[vmem], out_spe...  23 us
    ppermute x5, starting transfers between devices, shifted(): return lax.ppermute(value, axis, pairs)  16.1 us
    ppermute x5, waiting for transfers between devices, shifted(): return lax.ppermute(value, axis, pairs)  10.3 us
    dot_general x14, matrix products, split_dot(): return jnp.dot(split_table, operand, preferred_element_type=jnp.float32)  8.12 us
    dot_general x14, matrix products, split_dot(): return jnp.dot(operand, split_table, preferred_element_type=jnp.float32)  7.97 us
    convert_element_type x16, other arithmetic, halves(): return (high.astype(jnp.bfloat16), low.astype(jnp.bfloat16))  4.05 us
    unnamed x24, local copies, waits for them, and re-layouts  3.24 us
    broadcast_in_dim x1, other arithmetic, per_device(): return result[None]  2.57 us
  transfers between devices with their start and end apart: 5, of which 5 were waited for; matrix products, arithmetic and copies ran while one was open for 7% of the time, Pallas kernels for 0%

profile of v11, /device:TPU:128, one launch (start us, length us, event | category | flops | bytes accessed | tf_op | source)
XLA Modules:
  0.0 93.8 jit_solution(15638294752144471241)
XLA Ops:
  1.4 1.9 %collective-permute-start = (s32[2]{0:T(128)S(1)}, s32[2]{0:T(128)S(1)}, u32[]{:S(2)}, u32[]{:S(2)}) collective-permute-start(s32[2]{0:T(128)S(1)} %pad_add_fusion), channel_id=1, source_target_pairs={{0,4},{4,8},{8,12},{12,16},{16,20},{20,24},{24,28},{28,32},{32,36}... | collective-permute-start | bytes 32 | tf_op jit(solution)/shard_map/ppermute | solution.py:12
  3.3 1.1 %cosine_multiply_fusion = (f32[256,256]{1,0:T(8,128)S(1)}, f32[256,256]{1,0:T(8,128)S(1)}) fusion(), kind=kLoop, calls=%fused_computation.471 | loop fusion | flops 1048576 | bytes 524288 | tf_op jit(solution)/shard_map/mul | solution.py:26
  4.3 1.0 %broadcast_multiply_fusion.1 = (f32[256,256]{1,0:T(8,128)S(1)}, f32[256,256]{1,0:T(8,128)S(1)}) fusion(), kind=kLoop, calls=%fused_computation.476 | loop fusion | flops 1048576 | bytes 524288 | tf_op jit(solution)/shard_map/mul | solution.py:26
  5.3 1.0 %fusion.315 = f32[256,256]{1,0:T(8,128)S(1)} fusion(), kind=kLoop, calls=%fused_computation.479 | loop fusion | flops 1048576 | bytes 262144 | tf_op jit(solution)/shard_map/neg | solution.py:39
  6.3 1.6 %fusion.12 = (bf16[512,512]{1,0:T(8,128)(2,1)}, bf16[512,512]{1,0:T(8,128)(2,1)}, bf16[512,512]{1,0:T(8,128)(2,1)}, bf16[512,512]{1,0:T(8,128)(2,1)}) fusion(f32[256,256]{1,0:T(8,128)S(1)} %get-tuple-element.137, f32[256,256]{1,0:T(8,128)S(1)} %get-tuple-element.139, f32[256,256]{1,0:T(8,128)S(1)} %get-tuple-element.140, ...), kind=kLoop, calls=%fused_computation.26 | loop fusion | flops 4718592 | bytes 3407872 | tf_op jit(solution)/shard_map/convert_element_type | solution.py:33
  7.9 1.6 %collective-permute-done = s32[2]{0:T(128)S(1)} collective-permute-done((s32[2]{0:T(128)S(1)}, s32[2]{0:T(128)S(1)}, u32[]{:S(2)}, u32[]{:S(2)}) %collective-permute-start) | collective-permute-done | bytes 40 | tf_op jit(solution)/shard_map/ppermute | solution.py:12
  9.5 0.6 fusion.345
  13.3 0.2 dynamic-slice_bitcast_fusion
  14.2 0.9 fusion.287
  15.1 5.4 %collective-permute-start.2 = (f32[256,256]{1,0:T(8,128)}, f32[256,256]{1,0:T(8,128)}, u32[]{:S(2)}, u32[]{:S(2)}) collective-permute-start(f32[256,256]{1,0:T(8,128)} %get-tuple-element.128), channel_id=1, source_target_pairs={{4,0},{8,4},{12,8},{16,12},{20,16},{24,20},{28,24},{32,28},{36,32}... | collective-permute-start | bytes 786440 | tf_op jit(solution)/shard_map/ppermute | solution.py:12
  20.5 1.9 %collective-permute-start.1 = (f32[256,256]{1,0:T(8,128)}, f32[256,256]{1,0:T(8,128)}, u32[]{:S(2)}, u32[]{:S(2)}) collective-permute-start(f32[256,256]{1,0:T(8,128)} %get-tuple-element.127), channel_id=1, source_target_pairs={{4,0},{8,4},{12,8},{16,12},{20,16},{24,20},{28,24},{32,28},{36,32}... | collective-permute-start | bytes 786440 | tf_op jit(solution)/shard_map/ppermute | solution.py:12
  22.4 1.0 %fusion.271 = (bf16[256,512]{1,0:T(8,128)(2,1)S(1)}, bf16[256,512]{1,0:T(8,128)(2,1)}, bf16[256,512]{1,0:T(8,128)(2,1)}, bf16[256,512]{1,0:T(8,128)(2,1)}) fusion(f32[256,256]{1,0:T(8,128)S(1)} %get-tuple-element.139, f32[256,256]{1,0:T(8,128)S(1)} %get-tuple-element.137, f32[256,256]{1,0:T(8,128)S(1)} %get-tuple-element.138), kind=kLoop, calls=%fused_computation.327 | loop fusion | flops 1835008 | bytes 1835008 | tf_op jit(solution)/shard_map/convert_element_type | solution.py:33
  23.4 1.1 %fusion.344 = (f32[256,256]{1,0:T(8,128)S(1)}, f32[256,256]{1,0:T(8,128)S(1)}) fusion(f32[256,256]{1,0:T(8,128)S(1)} %copy-done.7), kind=kLoop, calls=%fused_computation.509 | loop fusion | bytes 786432 | tf_op jit(solution)/shard_map/cos | solution.py:137
  24.5 0.2 collective-permute-done.2
  24.7 2.8 %collective-permute-done.1 = f32[256,256]{1,0:T(8,128)} collective-permute-done((f32[256,256]{1,0:T(8,128)}, f32[256,256]{1,0:T(8,128)}, u32[]{:S(2)}, u32[]{:S(2)}) %collective-permute-start.1) | collective-permute-done | bytes 262176 | tf_op jit(solution)/shard_map/ppermute | solution.py:12
  27.5 2.0 %fusion.282.window_ref = f32[2,256,256]{2,1,0:T(8,128)} fusion(s32[]{:T(128)S(6)} %select_n.63, s32[]{:T(128)S(6)} %select_n.64, f32[2,256,1024]{2,1,0:T(8,128)S(1)} %bitcast.186, f32[1,256,256]{2,1,0:T(8,128)} %bitcast.10, f32[1,256,256]{2,1,0:T(8,128)} %bitcast.8), kind=kLoop, calls=%fused_computation.338 | loop fusion | flops 262144 | bytes 3145736 | tf_op jit(solution)/shard_map/add | solution.py:153
  29.5 23.0 %shard_map.64 = f32[4,2,256,256]{3,2,1,0:T(8,128)} custom-call(f32[2,256,256]{2,1,0:T(8,128)} %fusion.282.window_ref), custom_call_target="tpu_custom_call" | custom-call | tf_op jit(solution)/shard_map/pallas_call | solution.py:118
  52.5 1.2 %fusion.302 = (f32[256,256]{1,0:T(8,128)S(1)}, f32[256,256]{1,0:T(8,128)S(1)}) fusion(f32[4,2,256,256]{3,2,1,0:T(8,128)} %shard_map.64, f32[2,256,256]{2,1,0:T(8,128)S(1)} %copy-done.2), kind=kLoop, calls=%fused_computation.423 | loop fusion | flops 393216 | bytes 1572864 | tf_op jit(solution)/shard_map/sub | solution.py:171
  53.9 0.6 fusion.190
  54.4 0.4 copy-done.10
  54.9 0.6 fusion.25
  55.7 0.8 copy-done.3
  56.5 0.2 copy-done.4
  56.7 0.6 fusion.196
  57.2 0.4 copy-done.9
  57.6 0.6 fusion.37
  58.2 1.0 %copy-done = f32[4,2,256,256]{3,2,1,0:T(8,128)S(1)} copy-done((f32[4,2,256,256]{3,2,1,0:T(8,128)S(1)}, f32[4,2,256,256]{3,2,1,0:T(8,128)}, u32[]{:S(2)}) %copy-start) | copy-done | bytes 2097176
  59.5 0.6 fusion.202
  60.1 0.6 fusion.49
  60.9 0.6 fusion.206
  61.4 0.6 fusion.61
  62.0 0.1 fusion.294
  62.3 0.6 fusion.210
  62.9 0.6 fusion.73
  63.7 0.6 fusion.214
  64.3 0.6 fusion.85
  65.1 0.6 fusion.218
  65.7 0.6 fusion.97
  66.3 0.4 copy-done.8
  66.7 0.2 multiply_add_fusion.3
  66.9 0.6 fusion.222
  67.5 0.6 fusion.109
  68.2 0.1 fusion.292
  68.4 0.6 fusion.226
  69.0 0.6 fusion.121
  69.8 0.6 fusion.230
  70.4 0.6 fusion.133
  71.1 0.1 fusion.296
  71.3 0.6 fusion.234
  71.9 0.6 fusion.145
  72.7 0.6 fusion.238
  73.2 0.6 fusion.157
  73.9 0.1 fusion.300
  74.0 0.3 fusion.250
  74.4 0.6 fusion.242
  75.0 0.6 fusion.169
  75.7 0.6 fusion.246
  76.3 0.6 fusion.181
  77.2 0.2 fusion.281
  77.5 1.9 %collective-permute-start.3 = (f32[256,256]{1,0:T(8,128)S(1)}, f32[256,256]{1,0:T(8,128)S(1)}, u32[]{:S(2)}, u32[]{:S(2)}) collective-permute-start(f32[256,256]{1,0:T(8,128)S(1)} %get-tuple-element.63), channel_id=1, source_target_pairs={{0,4},{4,8},{8,12},{12,16},{16,20},{20,24},{24,28},{28,32},{32,36}... | collective-permute-start | bytes 786440 | tf_op jit(solution)/shard_map/ppermute | solution.py:12
  79.4 4.9 %collective-permute-start.4 = (f32[256,256]{1,0:T(8,128)S(1)}, f32[256,256]{1,0:T(8,128)S(1)}, u32[]{:S(2)}, u32[]{:S(2)}) collective-permute-start(f32[256,256]{1,0:T(8,128)S(1)} %get-tuple-element.62), channel_id=1, source_target_pairs={{0,4},{4,8},{8,12},{12,16},{16,20},{20,24},{24,28},{28,32},{32,36}... | collective-permute-start | bytes 786440 | tf_op jit(solution)/shard_map/ppermute | solution.py:12
  85.6 2.9 %collective-permute-done.3 = f32[256,256]{1,0:T(8,128)S(1)} collective-permute-done((f32[256,256]{1,0:T(8,128)S(1)}, f32[256,256]{1,0:T(8,128)S(1)}, u32[]{:S(2)}, u32[]{:S(2)}) %collective-permute-start.3) | collective-permute-done | bytes 262176 | tf_op jit(solution)/shard_map/ppermute | solution.py:12
  88.5 2.8 %collective-permute-done.4 = f32[256,256]{1,0:T(8,128)S(1)} collective-permute-done((f32[256,256]{1,0:T(8,128)S(1)}, f32[256,256]{1,0:T(8,128)S(1)}, u32[]{:S(2)}, u32[]{:S(2)}) %collective-permute-start.4) | collective-permute-done | bytes 262176 | tf_op jit(solution)/shard_map/ppermute | solution.py:12
  91.3 2.6 %fusion.4 = f32[1,2,256,1024]{3,2,1,0:T(8,128)} fusion(s32[]{:T(128)S(6)} %select_n.71, f32[1,256,256]{2,1,0:T(8,128)S(1)} %bitcast.187, f32[1,256,256]{2,1,0:T(8,128)S(1)} %bitcast.188, s32[]{:T(128)S(6)} %select_n.68, s32[]{:T(128)S(6)} %select_n.69, f32[2,256,256]{2,1,0:T(8,128)S(1)} %fusion.281), kind=kLoop, calls=%fused_computation.8 | loop fusion | flops 6815744 | bytes 3147776 | tf_op jit(solution)/shard_map/broadcast_in_dim | solution.py:211
  (52 shorter events, 3.1 us)
Async XLA Ops:
  1.4 8.2 %collective-permute-start = (s32[2]{0:T(128)S(1)}, s32[2]{0:T(128)S(1)}, u32[]{:S(2)}, u32[]{:S(2)}) collective-permute-start(s32[2]{0:T(128)S(1)} %pad_add_fusion), channel_id=1, source_target_pairs={{0,4},{4,8},{8,12},{12,16},{16,20},{20,24},{24,28},{28,32},{32,36}... | collective-permute-start | bytes 32 | tf_op jit(solution)/shard_map/ppermute | solution.py:12
  6.3 7.0 %copy-start.1 = (f32[1,2,256,1024]{3,2,1,0:T(8,128)S(1)}, f32[1,2,256,1024]{3,2,1,0:T(8,128)}, u32[]{:S(2)}) copy-start(f32[1,2,256,1024]{3,2,1,0:T(8,128)} %param.6) | copy-start | bytes 6291460
  15.1 8.3 %copy-start.7 = (f32[256,256]{1,0:T(8,128)S(1)}, f32[256,256]{1,0:T(8,128)}, u32[]{:S(2)}) copy-start(f32[256,256]{1,0:T(8,128)} %param.8) | copy-start | bytes 786436
  15.1 9.6 %collective-permute-start.2 = (f32[256,256]{1,0:T(8,128)}, f32[256,256]{1,0:T(8,128)}, u32[]{:S(2)}, u32[]{:S(2)}) collective-permute-start(f32[256,256]{1,0:T(8,128)} %get-tuple-element.128), channel_id=1, source_target_pairs={{4,0},{8,4},{12,8},{16,12},{20,16},{24,20},{28,24},{32,28},{36,32}... | collective-permute-start | bytes 786440 | tf_op jit(solution)/shard_map/ppermute | solution.py:12
  20.5 7.0 %collective-permute-start.1 = (f32[256,256]{1,0:T(8,128)}, f32[256,256]{1,0:T(8,128)}, u32[]{:S(2)}, u32[]{:S(2)}) collective-permute-start(f32[256,256]{1,0:T(8,128)} %get-tuple-element.127), channel_id=1, source_target_pairs={{4,0},{8,4},{12,8},{16,12},{20,16},{24,20},{28,24},{32,28},{36,32}... | collective-permute-start | bytes 786440 | tf_op jit(solution)/shard_map/ppermute | solution.py:12
  29.5 23.0 %copy-start.2 = (f32[2,256,256]{2,1,0:T(8,128)S(1)}, f32[2,256,256]{2,1,0:T(8,128)}, u32[]{:S(2)}) copy-start(f32[2,256,256]{2,1,0:T(8,128)} %param.7) | copy-start | bytes 1572868
  52.5 1.3 %copy-start.5 = (bf16[512,512]{1,0:T(8,128)(2,1)S(1)}, bf16[512,512]{1,0:T(8,128)(2,1)}, u32[]{:S(2)}) copy-start(bf16[512,512]{1,0:T(8,128)(2,1)} %get-tuple-element.131) | copy-start | bytes 1572868
  52.5 1.3 %copy-start.6 = (bf16[512,512]{1,0:T(8,128)(2,1)S(1)}, bf16[512,512]{1,0:T(8,128)(2,1)}, u32[]{:S(2)}) copy-start(bf16[512,512]{1,0:T(8,128)(2,1)} %get-tuple-element.132) | copy-start | bytes 1572868
  53.9 0.9 %copy-start.10 = (bf16[256,512]{1,0:T(8,128)(2,1)S(1)}, bf16[256,512]{1,0:T(8,128)(2,1)}, u32[]{:S(2)}) copy-start(bf16[256,512]{1,0:T(8,128)(2,1)} %get-tuple-element.129) | copy-start | bytes 786436
  53.9 1.0 %copy-start.11 = (bf16[256,512]{1,0:T(8,128)(2,1)S(1)}, bf16[256,512]{1,0:T(8,128)(2,1)}, u32[]{:S(2)}) copy-start(bf16[256,512]{1,0:T(8,128)(2,1)} %get-tuple-element.130) | copy-start | bytes 786436
  55.5 1.0 %copy-start.3 = (bf16[512,512]{1,0:T(8,128)(2,1)S(1)}, bf16[512,512]{1,0:T(8,128)(2,1)}, u32[]{:S(2)}) copy-start(bf16[512,512]{1,0:T(8,128)(2,1)} %get-tuple-element.58) | copy-start | bytes 1572868
  55.5 1.2 %copy-start.4 = (bf16[512,512]{1,0:T(8,128)(2,1)S(1)}, bf16[512,512]{1,0:T(8,128)(2,1)}, u32[]{:S(2)}) copy-start(bf16[512,512]{1,0:T(8,128)(2,1)} %get-tuple-element.59) | copy-start | bytes 1572868
  56.7 0.9 %copy-start.9 = (bf16[256,512]{1,0:T(8,128)(2,1)S(1)}, bf16[256,512]{1,0:T(8,128)(2,1)}, u32[]{:S(2)}) copy-start(bf16[256,512]{1,0:T(8,128)(2,1)} %get-tuple-element.116) | copy-start | bytes 786436
  57.6 1.6 %copy-start = (f32[4,2,256,256]{3,2,1,0:T(8,128)S(1)}, f32[4,2,256,256]{3,2,1,0:T(8,128)}, u32[]{:S(2)}) copy-start(f32[4,2,256,256]{3,2,1,0:T(8,128)} %shard_map.64) | copy-start | bytes 6291460
  65.7 1.0 %copy-start.8 = (f32[1,256,256]{2,1,0:T(8,128)S(1)}, f32[1,256,256]{2,1,0:T(8,128)}, u32[]{:S(2)}) copy-start(f32[1,256,256]{2,1,0:T(8,128)} %param.11) | copy-start | bytes 786436
  77.5 11.0 %collective-permute-start.3 = (f32[256,256]{1,0:T(8,128)S(1)}, f32[256,256]{1,0:T(8,128)S(1)}, u32[]{:S(2)}, u32[]{:S(2)}) collective-permute-start(f32[256,256]{1,0:T(8,128)S(1)} %get-tuple-element.63), channel_id=1, source_target_pairs={{0,4},{4,8},{8,12},{12,16},{16,20},{20,24},{24,28},{28,32},{32,36}... | collective-permute-start | bytes 786440 | tf_op jit(solution)/shard_map/ppermute | solution.py:12
  79.4 11.9 %collective-permute-start.4 = (f32[256,256]{1,0:T(8,128)S(1)}, f32[256,256]{1,0:T(8,128)S(1)}, u32[]{:S(2)}, u32[]{:S(2)}) collective-permute-start(f32[256,256]{1,0:T(8,128)S(1)} %get-tuple-element.62), channel_id=1, source_target_pairs={{0,4},{4,8},{8,12},{12,16},{16,20},{20,24},{24,28},{28,32},{32,36}... | collective-permute-start | bytes 786440 | tf_op jit(solution)/shard_map/ppermute | solution.py:12

commit v12 on v9

--- a/solution.py
+++ b/solution.py
@@ -35,39 +35,29 @@
 
 def stacked_tables(cosines, sines, direction):
     signed = sines * direction
-    left = jnp.concatenate(
-        [jnp.concatenate([cosines, -signed], axis=1), jnp.concatenate([signed, cosines], axis=1)],
-        axis=0,
-    )
-    right = jnp.concatenate([cosines, signed], axis=1)
-    left_high, left_low = halves(left)
-    right_high, right_low = halves(right)
-    left_split = jnp.concatenate([left_high, left_high, left_low], axis=1)
-    right_split = jnp.concatenate([right_high, right_low, right_high], axis=0)
-    return left_split, right_split
-
-
-def split_dot(split_table, value, table_first):
-    high, low = halves(value)
-    if table_first:
-        operand = jnp.concatenate([high, low, high], axis=0)
-        return jnp.dot(split_table, operand, preferred_element_type=jnp.float32)
-    operand = jnp.concatenate([high, high, low], axis=1)
-    return jnp.dot(operand, split_table, preferred_element_type=jnp.float32)
+    parts = jnp.stack([cosines, cosines + signed, signed - cosines])
+    high, low = halves(parts)
+    left = jnp.concatenate([high, high, low], axis=2)
+    right = jnp.concatenate([high, low, high], axis=1)
+    return left, right
 
 
 def transform(stacked, tables):
     left, right = tables
-    width = right.shape[1] // 2
-    middle = split_dot(left, stacked, True)
-    products = split_dot(right, middle, False)
-    out_real = products[:width, :width] - products[width:, width:]
-    out_imag = products[:width, width:] + products[width:, :width]
-    return out_real, out_imag
+    real, imag = stacked
+    high, low = halves(jnp.stack([real + imag, imag, real]))
+    operand = jnp.concatenate([high, low, high], axis=1)
+    terms = jnp.einsum("bij,bjk->bik", left, operand, preferred_element_type=jnp.float32)
+    middle_real = terms[0] - terms[1]
+    middle_imag = terms[0] + terms[2]
+    high, low = halves(jnp.stack([middle_real + middle_imag, middle_imag, middle_real]))
+    operand = jnp.concatenate([high, high, low], axis=2)
+    terms = jnp.einsum("bij,bjk->bik", operand, right, preferred_element_type=jnp.float32)
+    return terms[0] - terms[1], terms[0] + terms[2]
 
 
 def stack(real_part, imag_part):
-    return jnp.concatenate([real_part, imag_part], axis=0)
+    return (real_part, imag_part)
 
 
 def exchange_kernel(window_ref, layers_ref, send_sem, recv_sem):

time: 91.4 us -> 89.5 us (0.979)
  waiting for transfers between devices: 15.2 us -> 18.3 us
  matrix products: 16.1 us -> 13.5 us
  starting transfers between devices: 8.4 us -> 5.88 us
    ppermute x3, waiting for transfers between devices: 15.2 us -> 18.3 us  [shifted(): return lax.ppermute(value, axis, pairs)]
    dot_general x28, matrix products: 16.1 us -> 13.5 us  [the longest x14 6.75 us: transform(): jnp.einsum('bij,bjk->bik', operand, right, preferred_element_type=jnp.flo...]
    ppermute x3, starting transfers between devices: 8.4 us -> 5.88 us  [shifted(): return lax.ppermute(value, axis, pairs)]
    add x10 -> x25, other arithmetic: 1.02 us -> 3.39 us  [the longest x7 2.13 us: transform(): high, low = halves(jnp.stack([real + imag, imag, real]))]
    mul x2 -> x1, other arithmetic: 2.74 us -> 0.97 us  [dft_tables(): return (jnp.cos(angle) * factor, jnp.sin(angle) * factor)]
    unnamed x24 -> x12, local copies, waits for them, and re-layouts: 3.17 us -> 1.57 us
    dynamic_slice x1, local copies, waits for them, and re-layouts: 0.21 us -> 1.34 us  [per_device(): lax.dynamic_slice(strip, (zero, zero, column_above), (2, width, width))]
    neg x1 -> x0, other arithmetic: 0.98 us -> none  [stacked_tables(): -signed]
  transfers between devices with their start and end apart: 3 -> 3, of which waited for: 3 -> 3; matrix products, arithmetic and copies ran while one was open for 9% -> 6% of each run, Pallas kernels for 0% -> 0%
where the time goes in v12:
time: 89.5 us; the launch traced here: 89 us
  Pallas kernels  22.9 us (26%)
  waiting for transfers between devices  18.3 us (20%)
  other arithmetic  16.4 us (18%)
  matrix products  13.5 us (15%)
  between operations  7.16 us (8%)
  starting transfers between devices  5.88 us (7%)
  local copies, waits for them, and re-layouts  4.83 us (5%)
    pallas_call x1, Pallas kernels, exchange(): pl.pallas_call(exchange_kernel, out_shape=shape, in_specs=[vmem], out_spe...  22.9 us
    ppermute x3, waiting for transfers between devices, shifted(): return lax.ppermute(value, axis, pairs)  18.3 us
    dot_general x14, matrix products, transform(): jnp.einsum('bij,bjk->bik', operand, right, preferred_element_type=jnp.flo...  6.75 us
    dot_general x14, matrix products, transform(): jnp.einsum('bij,bjk->bik', left, operand, preferred_element_type=jnp.floa...  6.75 us
    ppermute x3, starting transfers between devices, shifted(): return lax.ppermute(value, axis, pairs)  5.88 us
    convert_element_type x29, other arithmetic, halves(): return (high.astype(jnp.bfloat16), low.astype(jnp.bfloat16))  4.97 us
    broadcast_in_dim x1, other arithmetic, per_device(): return result[None]  2.56 us
    sub x2, other arithmetic, stacked_tables(): parts = jnp.stack([cosines, cosines + signed, signed - cosines])  2.15 us
  transfers between devices with their start and end apart: 3, of which 3 were waited for; matrix products, arithmetic and copies ran while one was open for 6% of the time, Pallas kernels for 0%

profile of v12, /device:TPU:128, one launch (start us, length us, event | category | flops | bytes accessed | tf_op | source)
XLA Modules:
  0.0 89.0 jit_solution(9314578597288715316)
XLA Ops:
  1.4 1.9 %collective-permute-start = (s32[2]{0:T(128)S(1)}, s32[2]{0:T(128)S(1)}, u32[]{:S(2)}, u32[]{:S(2)}) collective-permute-start(s32[2]{0:T(128)S(1)} %pad_add_fusion), channel_id=1, source_target_pairs={{0,4},{4,8},{8,12},{12,16},{16,20},{20,24},{24,28},{28,32},{32,36}... | collective-permute-start | bytes 32 | tf_op jit(solution)/shard_map/ppermute | solution.py:12
  3.3 1.1 %multiply_subtract_fusion.12 = (f32[1,256,256]{2,1,0:T(8,128)S(1)}, f32[1,256,256]{2,1,0:T(8,128)S(1)}) fusion(), kind=kLoop, calls=%fused_computation.502 | loop fusion | flops 1179648 | bytes 524288 | tf_op jit(solution)/shard_map/sub | solution.py:38
  4.4 5.2 %collective-permute-done = s32[2]{0:T(128)S(1)} collective-permute-done((s32[2]{0:T(128)S(1)}, s32[2]{0:T(128)S(1)}, u32[]{:S(2)}, u32[]{:S(2)}) %collective-permute-start) | collective-permute-done | bytes 40 | tf_op jit(solution)/shard_map/ppermute | solution.py:12
  9.5 0.6 fusion.369
  13.4 1.3 %dynamic-slice_bitcast_fusion = f32[2,256,256]{2,1,0:T(8,128)S(1)} fusion(f32[1,2,256,1024]{3,2,1,0:T(8,128)} %param.6, s32[]{:T(128)S(6)} %select_n.76), kind=kLoop, calls=%fused_computation.345 | loop fusion | bytes 1048580 | tf_op jit(solution)/shard_map/dynamic_slice | solution.py:137
  15.4 2.1 %collective-permute-start.1 = (f32[2,256,256]{2,1,0:T(8,128)S(1)}, f32[2,256,256]{2,1,0:T(8,128)S(1)}, u32[]{:S(2)}, u32[]{:S(2)}) collective-permute-start(f32[2,256,256]{2,1,0:T(8,128)S(1)} %pad_dynamic-slice_fusion.8), channel_id=1, source_target_pairs={{4,0},{8,4},{12,8},{16,12},{20,16},{24,20},{28,24},{32,28},{36,32}... | collective-permute-start | bytes 1572872 | tf_op jit(solution)/shard_map/ppermute | solution.py:12
  17.5 1.0 %cosine_multiply_fusion = f32[1,256,256]{2,1,0:T(8,128)S(1)} fusion(), kind=kLoop, calls=%fused_computation.498 | loop fusion | flops 983040 | bytes 262144 | tf_op jit(solution)/shard_map/mul | solution.py:26
  18.5 1.1 %multiply_subtract_fusion.13 = (f32[1,256,256]{2,1,0:T(8,128)S(1)}, f32[1,256,256]{2,1,0:T(8,128)S(1)}) fusion(), kind=kLoop, calls=%fused_computation.504 | loop fusion | flops 1179648 | bytes 524288 | tf_op jit(solution)/shard_map/sub | solution.py:38
  19.6 1.0 %fusion.171 = (bf16[3,256,256]{2,1,0:T(8,128)(2,1)S(1)}, bf16[3,256,256]{2,1,0:T(8,128)(2,1)S(1)}, bf16[3,256,256]{2,1,0:T(8,128)(2,1)S(1)}, bf16[3,256,256]{2,1,0:T(8,128)(2,1)}) fusion(f32[1,256,256]{2,1,0:T(8,128)S(1)} %get-tuple-element.188, f32[1,256,256]{2,1,0:T(8,128)S(1)} %get-tuple-element.189, f32[1,256,256]{2,1,0:T(8,128)S(1)} %cosine_multiply_fusion, ...), kind=kLoop, calls=%fused_computation.214 | loop fusion | flops 3145728 | bytes 2883584 | tf_op jit(solution)/shard_map/convert_element_type | solution.py:33
  20.6 1.1 %fusion.368 = (f32[256,256]{1,0:T(8,128)S(1)}, f32[256,256]{1,0:T(8,128)S(1)}) fusion(f32[256,256]{1,0:T(8,128)S(1)} %copy-done.4), kind=kLoop, calls=%fused_computation.557 | loop fusion | bytes 786432 | tf_op jit(solution)/shard_map/cos | solution.py:127
  21.7 2.5 %collective-permute-done.1 = f32[2,256,256]{2,1,0:T(8,128)S(1)} collective-permute-done((f32[2,256,256]{2,1,0:T(8,128)S(1)}, f32[2,256,256]{2,1,0:T(8,128)S(1)}, u32[]{:S(2)}, u32[]{:S(2)}) %collective-permute-start.1) | collective-permute-done | bytes 524320 | tf_op jit(solution)/shard_map/ppermute | solution.py:12
  24.2 1.0 %fusion.267.window_ref = f32[2,256,256]{2,1,0:T(8,128)} fusion(f32[2,256,256]{2,1,0:T(8,128)S(1)} %collective-permute-done.1, s32[]{:T(128)S(6)} %select_n.74, s32[]{:T(128)S(6)} %select_n.75, f32[2,256,1024]{2,1,0:T(8,128)S(1)} %bitcast.322), kind=kLoop, calls=%fused_computation.340 | loop fusion | flops 131072 | bytes 3145736 | tf_op jit(solution)/shard_map/add | solution.py:143
  25.2 22.9 %shard_map.64 = f32[4,2,256,256]{3,2,1,0:T(8,128)} custom-call(f32[2,256,256]{2,1,0:T(8,128)} %fusion.267.window_ref), custom_call_target="tpu_custom_call" | custom-call | tf_op jit(solution)/shard_map/pallas_call | solution.py:108
  48.2 1.2 %fusion.365 = (f32[1,256,256]{2,1,0:T(8,128)S(1)}, f32[1,256,256]{2,1,0:T(8,128)S(1)}, f32[1,256,256]{2,1,0:T(8,128)S(1)}) fusion(f32[4,2,256,256]{3,2,1,0:T(8,128)} %shard_map.64, f32[2,256,256]{2,1,0:T(8,128)S(1)} %copy-done.2), kind=kLoop, calls=%fused_computation.556 | loop fusion | flops 458752 | bytes 1835008 | tf_op jit(solution)/shard_map/add | solution.py:48
  49.3 0.1 fusion.259
  49.5 0.5 fusion.2
  50.0 0.1 fusion.177
  50.2 0.5 fusion.8
  50.9 0.5 fusion.14
  51.5 0.1 fusion.181
  51.7 0.5 fusion.20
  52.1 1.1 %copy-done = f32[4,2,256,256]{3,2,1,0:T(8,128)S(1)} copy-done((f32[4,2,256,256]{3,2,1,0:T(8,128)S(1)}, f32[4,2,256,256]{3,2,1,0:T(8,128)}, u32[]{:S(2)}) %copy-start) | copy-done | bytes 2097176
  53.4 0.1 fusion.255
  53.5 0.5 fusion.26
  54.1 0.1 fusion.185
  54.2 0.5 fusion.32
  55.0 0.5 fusion.38
  55.5 0.1 fusion.189
  55.7 0.5 fusion.44
  56.5 0.5 fusion.50
  57.2 0.5 fusion.56
  57.9 0.5 fusion.62
  58.6 0.5 fusion.68
  59.4 0.5 fusion.74
  60.1 0.5 fusion.80
  60.6 0.4 copy-done.5
  61.1 0.2 add_bitcast_fusion.3
  61.4 0.5 fusion.86
  62.1 0.5 fusion.92
  63.0 0.5 fusion.98
  63.5 0.2 fusion.209
  63.7 0.5 fusion.104
  64.3 0.2 fusion.241
  64.5 0.5 fusion.110
  65.0 0.2 fusion.213
  65.2 0.5 fusion.116
  65.8 0.3 fusion.340
  66.1 0.2 fusion.239
  66.3 0.5 fusion.122
  66.9 0.2 fusion.217
  67.0 0.5 fusion.128
  67.6 0.1 fusion.237
  67.8 0.5 fusion.134
  68.3 0.2 fusion.221
  68.5 0.5 fusion.140
  69.2 0.2 fusion.235
  69.4 0.5 fusion.146
  70.1 0.5 fusion.152
  70.8 0.5 fusion.158
  71.5 0.5 fusion.164
  72.3 0.2 fusion.266
  72.6 1.9 %collective-permute-start.2 = (f32[2,256,256]{2,1,0:T(8,128)S(1)}, f32[2,256,256]{2,1,0:T(8,128)S(1)}, u32[]{:S(2)}, u32[]{:S(2)}) collective-permute-start(f32[2,256,256]{2,1,0:T(8,128)S(1)} %pad_dynamic-slice_fusion.7), channel_id=1, source_target_pairs={{0,4},{4,8},{8,12},{12,16},{16,20},{20,24},{24,28},{28,32},{32,36}... | collective-permute-start | bytes 1572872 | tf_op jit(solution)/shard_map/ppermute | solution.py:12
  75.8 10.6 %collective-permute-done.2 = f32[2,256,256]{2,1,0:T(8,128)S(1)} collective-permute-done((f32[2,256,256]{2,1,0:T(8,128)S(1)}, f32[2,256,256]{2,1,0:T(8,128)S(1)}, u32[]{:S(2)}, u32[]{:S(2)}) %collective-permute-start.2) | collective-permute-done | bytes 524320 | tf_op jit(solution)/shard_map/ppermute | solution.py:12
  86.4 2.6 %fusion.1 = f32[1,2,256,1024]{3,2,1,0:T(8,128)} fusion(s32[]{:T(128)S(6)} %select_n.82, f32[2,256,256]{2,1,0:T(8,128)S(1)} %collective-permute-done.2, s32[]{:T(128)S(6)} %select_n.79, s32[]{:T(128)S(6)} %select_n.80, f32[2,256,256]{2,1,0:T(8,128)S(1)} %fusion.266), kind=kLoop, calls=%fused_computation.4 | loop fusion | flops 524288 | bytes 3145740 | tf_op jit(solution)/shard_map/broadcast_in_dim | solution.py:201
  (60 shorter events, 5.0 us)
Async XLA Ops:
  1.4 8.2 %collective-permute-start = (s32[2]{0:T(128)S(1)}, s32[2]{0:T(128)S(1)}, u32[]{:S(2)}, u32[]{:S(2)}) collective-permute-start(s32[2]{0:T(128)S(1)} %pad_add_fusion), channel_id=1, source_target_pairs={{0,4},{4,8},{8,12},{12,16},{16,20},{20,24},{24,28},{28,32},{32,36}... | collective-permute-start | bytes 32 | tf_op jit(solution)/shard_map/ppermute | solution.py:12
  15.4 5.2 %copy-start.4 = (f32[256,256]{1,0:T(8,128)S(1)}, f32[256,256]{1,0:T(8,128)}, u32[]{:S(2)}) copy-start(f32[256,256]{1,0:T(8,128)} %param.8) | copy-start | bytes 786436
  15.4 8.7 %collective-permute-start.1 = (f32[2,256,256]{2,1,0:T(8,128)S(1)}, f32[2,256,256]{2,1,0:T(8,128)S(1)}, u32[]{:S(2)}, u32[]{:S(2)}) collective-permute-start(f32[2,256,256]{2,1,0:T(8,128)S(1)} %pad_dynamic-slice_fusion.8), channel_id=1, source_target_pairs={{4,0},{8,4},{12,8},{16,12},{20,16},{24,20},{28,24},{32,28},{36,32}... | collective-permute-start | bytes 1572872 | tf_op jit(solution)/shard_map/ppermute | solution.py:12
  18.5 5.7 %copy-start.1 = (f32[1,2,256,1024]{3,2,1,0:T(8,128)S(1)}, f32[1,2,256,1024]{3,2,1,0:T(8,128)}, u32[]{:S(2)}) copy-start(f32[1,2,256,1024]{3,2,1,0:T(8,128)} %param.6) | copy-start | bytes 6291460
  25.2 23.0 %copy-start.2 = (f32[2,256,256]{2,1,0:T(8,128)S(1)}, f32[2,256,256]{2,1,0:T(8,128)}, u32[]{:S(2)}) copy-start(f32[2,256,256]{2,1,0:T(8,128)} %param.7) | copy-start | bytes 1572868
  48.2 1.3 %copy-start.3 = (bf16[3,256,256]{2,1,0:T(8,128)(2,1)S(1)}, bf16[3,256,256]{2,1,0:T(8,128)(2,1)}, u32[]{:S(2)}) copy-start(bf16[3,256,256]{2,1,0:T(8,128)(2,1)} %get-tuple-element.181) | copy-start | bytes 1179652
  51.6 1.6 %copy-start = (f32[4,2,256,256]{3,2,1,0:T(8,128)S(1)}, f32[4,2,256,256]{3,2,1,0:T(8,128)}, u32[]{:S(2)}) copy-start(f32[4,2,256,256]{3,2,1,0:T(8,128)} %shard_map.64) | copy-start | bytes 6291460
  60.1 1.0 %copy-start.5 = (f32[1,256,256]{2,1,0:T(8,128)S(1)}, f32[1,256,256]{2,1,0:T(8,128)}, u32[]{:S(2)}) copy-start(f32[1,256,256]{2,1,0:T(8,128)} %param.11) | copy-start | bytes 786436
  72.6 13.8 %collective-permute-start.2 = (f32[2,256,256]{2,1,0:T(8,128)S(1)}, f32[2,256,256]{2,1,0:T(8,128)S(1)}, u32[]{:S(2)}, u32[]{:S(2)}) collective-permute-start(f32[2,256,256]{2,1,0:T(8,128)S(1)} %pad_dynamic-slice_fusion.7), channel_id=1, source_target_pairs={{0,4},{4,8},{8,12},{12,16},{16,20},{20,24},{24,28},{28,32},{32,36}... | collective-permute-start | bytes 1572872 | tf_op jit(solution)/shard_map/ppermute | solution.py:12

commit v13 on v12

--- a/solution.py
+++ b/solution.py
@@ -134,9 +134,8 @@
     column_above = offsets_above[1]
 
     strip = transmission[0]
-    lent = lax.dynamic_slice(strip, (zero, zero, column_above), (2, width, width))
-    lent = jnp.pad(lent, ((0, 0), (width, 0), (0, 0)))
-    lent = lax.dynamic_slice(lent, (zero, row_above, zero), (2, width, width))
+    lent = jnp.pad(strip, ((0, 0), (width, 0), (0, 0)))
+    lent = lax.dynamic_slice(lent, (zero, row_above, column_above), (2, width, width))
     borrowed = shifted(lent, "tile", -1)
     kept = jnp.pad(strip, ((0, 0), (0, width), (0, 0)))
     kept = lax.dynamic_slice(kept, (zero, row, column), (2, width, width))

time: 89.5 us -> 89.2 us (level)
    cos x1, local copies, waits for them, and re-layouts: 1.13 us -> 2.04 us  [per_device(): kernel_real = jnp.cos(prop_phase)]
where the time goes in v13:
time: 89.2 us; the launch traced here: 88.6 us
  Pallas kernels  23 us (26%)
  waiting for transfers between devices  18.1 us (20%)
  other arithmetic  15.6 us (17%)
  matrix products  13.5 us (15%)
  between operations  7.15 us (8%)
  starting transfers between devices  5.78 us (6%)
  local copies, waits for them, and re-layouts  5.47 us (6%)
    pallas_call x1, Pallas kernels, exchange(): pl.pallas_call(exchange_kernel, out_shape=shape, in_specs=[vmem], out_spe...  23 us
    ppermute x3, waiting for transfers between devices, shifted(): return lax.ppermute(value, axis, pairs)  18.1 us
    dot_general x14, matrix products, transform(): jnp.einsum('bij,bjk->bik', left, operand, preferred_element_type=jnp.floa...  6.75 us
    dot_general x14, matrix products, transform(): jnp.einsum('bij,bjk->bik', operand, right, preferred_element_type=jnp.flo...  6.74 us
    ppermute x3, starting transfers between devices, shifted(): return lax.ppermute(value, axis, pairs)  5.78 us
    convert_element_type x29, other arithmetic, halves(): return (high.astype(jnp.bfloat16), low.astype(jnp.bfloat16))  4.23 us
    broadcast_in_dim x1, other arithmetic, per_device(): return result[None]  2.57 us
    sub x2, other arithmetic, stacked_tables(): parts = jnp.stack([cosines, cosines + signed, signed - cosines])  2.15 us
  transfers between devices with their start and end apart: 3, of which 3 were waited for; matrix products, arithmetic and copies ran while one was open for 6% of the time, Pallas kernels for 0%

profile of v13, /device:TPU:128, one launch (start us, length us, event | category | flops | bytes accessed | tf_op | source)
XLA Modules:
  0.0 88.6 jit_solution(330935899399163413)
XLA Ops:
  1.4 1.9 %collective-permute-start = (s32[2]{0:T(128)S(1)}, s32[2]{0:T(128)S(1)}, u32[]{:S(2)}, u32[]{:S(2)}) collective-permute-start(s32[2]{0:T(128)S(1)} %pad_add_fusion), channel_id=1, source_target_pairs={{0,4},{4,8},{8,12},{12,16},{16,20},{20,24},{24,28},{28,32},{32,36}... | collective-permute-start | bytes 32 | tf_op jit(solution)/shard_map/ppermute | solution.py:12
  3.3 1.1 %multiply_subtract_fusion.12 = (f32[1,256,256]{2,1,0:T(8,128)S(1)}, f32[1,256,256]{2,1,0:T(8,128)S(1)}) fusion(), kind=kLoop, calls=%fused_computation.501 | loop fusion | flops 1179648 | bytes 524288 | tf_op jit(solution)/shard_map/sub | solution.py:38
  4.4 5.2 %collective-permute-done = s32[2]{0:T(128)S(1)} collective-permute-done((s32[2]{0:T(128)S(1)}, s32[2]{0:T(128)S(1)}, u32[]{:S(2)}, u32[]{:S(2)}) %collective-permute-start) | collective-permute-done | bytes 40 | tf_op jit(solution)/shard_map/ppermute | solution.py:12
  9.5 0.6 fusion.369
  14.0 1.2 %pad_dynamic-slice_fusion.2 = f32[2,256,256]{2,1,0:T(8,128)S(1)} fusion(s32[]{:T(128)S(6)} %select_n.76, s32[]{:T(128)S(6)} %select_n.77, f32[2,256,1024]{2,1,0:T(8,128)} %bitcast.320), kind=kLoop, calls=%fused_computation.2 | loop fusion | bytes 2621448 | tf_op jit(solution)/shard_map/dynamic_slice | solution.py:138
  15.2 1.9 %collective-permute-start.1 = (f32[2,256,256]{2,1,0:T(8,128)S(1)}, f32[2,256,256]{2,1,0:T(8,128)S(1)}, u32[]{:S(2)}, u32[]{:S(2)}) collective-permute-start(f32[2,256,256]{2,1,0:T(8,128)S(1)} %pad_dynamic-slice_fusion.2), channel_id=1, source_target_pairs={{4,0},{8,4},{12,8},{16,12},{20,16},{24,20},{28,24},{32,28},{36,32}... | collective-permute-start | bytes 1572872 | tf_op jit(solution)/shard_map/ppermute | solution.py:12
  17.1 1.0 %cosine_multiply_fusion = f32[1,256,256]{2,1,0:T(8,128)S(1)} fusion(), kind=kLoop, calls=%fused_computation.497 | loop fusion | flops 983040 | bytes 262144 | tf_op jit(solution)/shard_map/mul | solution.py:26
  18.1 1.1 %multiply_subtract_fusion.13 = (f32[1,256,256]{2,1,0:T(8,128)S(1)}, f32[1,256,256]{2,1,0:T(8,128)S(1)}) fusion(), kind=kLoop, calls=%fused_computation.503 | loop fusion | flops 1179648 | bytes 524288 | tf_op jit(solution)/shard_map/sub | solution.py:38
  19.2 0.3 fusion.171
  19.5 2.0 %fusion.368 = (f32[256,256]{1,0:T(8,128)S(1)}, f32[256,256]{1,0:T(8,128)S(1)}) fusion(f32[256,256]{1,0:T(8,128)} %param.8), kind=kLoop, calls=%fused_computation.556 | loop fusion | bytes 786432 | tf_op jit(solution)/shard_map/cos | solution.py:127
  21.5 2.3 %collective-permute-done.1 = f32[2,256,256]{2,1,0:T(8,128)S(1)} collective-permute-done((f32[2,256,256]{2,1,0:T(8,128)S(1)}, f32[2,256,256]{2,1,0:T(8,128)S(1)}, u32[]{:S(2)}, u32[]{:S(2)}) %collective-permute-start.1) | collective-permute-done | bytes 524320 | tf_op jit(solution)/shard_map/ppermute | solution.py:12
  23.8 1.0 %fusion.267.window_ref = f32[2,256,256]{2,1,0:T(8,128)} fusion(f32[2,256,256]{2,1,0:T(8,128)S(1)} %collective-permute-done.1, s32[]{:T(128)S(6)} %select_n.74, s32[]{:T(128)S(6)} %select_n.75, f32[2,256,1024]{2,1,0:T(8,128)S(1)} %bitcast.321), kind=kLoop, calls=%fused_computation.340 | loop fusion | flops 131072 | bytes 3145736 | tf_op jit(solution)/shard_map/add | solution.py:142
  24.8 23.0 %shard_map.64 = f32[4,2,256,256]{3,2,1,0:T(8,128)} custom-call(f32[2,256,256]{2,1,0:T(8,128)} %fusion.267.window_ref), custom_call_target="tpu_custom_call" | custom-call | tf_op jit(solution)/shard_map/pallas_call | solution.py:108
  47.8 1.1 %fusion.365 = (f32[1,256,256]{2,1,0:T(8,128)S(1)}, f32[1,256,256]{2,1,0:T(8,128)S(1)}, f32[1,256,256]{2,1,0:T(8,128)S(1)}) fusion(f32[4,2,256,256]{3,2,1,0:T(8,128)} %shard_map.64, f32[2,256,256]{2,1,0:T(8,128)S(1)} %copy-done.2), kind=kLoop, calls=%fused_computation.555 | loop fusion | flops 458752 | bytes 1835008 | tf_op jit(solution)/shard_map/add | solution.py:48
  48.9 0.1 fusion.259
  49.1 0.5 fusion.2
  49.8 0.5 fusion.8
  50.6 0.5 fusion.14
  51.3 0.5 fusion.20
  51.8 1.1 %copy-done = f32[4,2,256,256]{3,2,1,0:T(8,128)S(1)} copy-done((f32[4,2,256,256]{3,2,1,0:T(8,128)S(1)}, f32[4,2,256,256]{3,2,1,0:T(8,128)}, u32[]{:S(2)}) %copy-start) | copy-done | bytes 2097176
  53.0 0.1 fusion.255
  53.1 0.5 fusion.26
  53.7 0.1 fusion.185
  53.8 0.5 fusion.32
  54.4 0.1 fusion.253
  54.6 0.5 fusion.38
  55.3 0.5 fusion.44
  56.1 0.5 fusion.50
  56.8 0.5 fusion.56
  57.4 0.1 fusion.249
  57.5 0.5 fusion.62
  58.2 0.5 fusion.68
  58.9 0.1 fusion.247
  59.0 0.5 fusion.74
  59.7 0.5 fusion.80
  60.2 0.5 copy-done.3
  60.7 0.2 add_bitcast_fusion.3
  61.0 0.5 fusion.86
  61.7 0.5 fusion.92
  62.6 0.5 fusion.98
  63.1 0.2 fusion.209
  63.3 0.5 fusion.104
  63.9 0.2 fusion.241
  64.1 0.5 fusion.110
  64.6 0.2 fusion.213
  64.8 0.5 fusion.116
  65.4 0.3 fusion.340
  65.7 0.2 fusion.239
  65.9 0.5 fusion.122
  66.5 0.2 fusion.217
  66.6 0.5 fusion.128
  67.2 0.1 fusion.237
  67.4 0.5 fusion.134
  67.9 0.2 fusion.221
  68.1 0.5 fusion.140
  68.8 0.2 fusion.235
  69.0 0.5 fusion.146
  69.7 0.5 fusion.152
  70.4 0.5 fusion.158
  71.1 0.5 fusion.164
  71.9 0.2 fusion.266
  72.2 1.9 %collective-permute-start.2 = (f32[2,256,256]{2,1,0:T(8,128)S(1)}, f32[2,256,256]{2,1,0:T(8,128)S(1)}, u32[]{:S(2)}, u32[]{:S(2)}) collective-permute-start(f32[2,256,256]{2,1,0:T(8,128)S(1)} %pad_dynamic-slice_fusion.8), channel_id=1, source_target_pairs={{0,4},{4,8},{8,12},{12,16},{16,20},{20,24},{24,28},{28,32},{32,36}... | collective-permute-start | bytes 1572872 | tf_op jit(solution)/shard_map/ppermute | solution.py:12
  75.4 10.6 %collective-permute-done.2 = f32[2,256,256]{2,1,0:T(8,128)S(1)} collective-permute-done((f32[2,256,256]{2,1,0:T(8,128)S(1)}, f32[2,256,256]{2,1,0:T(8,128)S(1)}, u32[]{:S(2)}, u32[]{:S(2)}) %collective-permute-start.2) | collective-permute-done | bytes 524320 | tf_op jit(solution)/shard_map/ppermute | solution.py:12
  86.0 2.6 %fusion.1 = f32[1,2,256,1024]{3,2,1,0:T(8,128)} fusion(s32[]{:T(128)S(6)} %select_n.82, f32[2,256,256]{2,1,0:T(8,128)S(1)} %collective-permute-done.2, s32[]{:T(128)S(6)} %select_n.79, s32[]{:T(128)S(6)} %select_n.80, f32[2,256,256]{2,1,0:T(8,128)S(1)} %fusion.266), kind=kLoop, calls=%fused_computation.5 | loop fusion | flops 524288 | bytes 3145740 | tf_op jit(solution)/shard_map/broadcast_in_dim | solution.py:200
  (55 shorter events, 4.9 us)
Async XLA Ops:
  1.4 8.2 %collective-permute-start = (s32[2]{0:T(128)S(1)}, s32[2]{0:T(128)S(1)}, u32[]{:S(2)}, u32[]{:S(2)}) collective-permute-start(s32[2]{0:T(128)S(1)} %pad_add_fusion), channel_id=1, source_target_pairs={{0,4},{4,8},{8,12},{12,16},{16,20},{20,24},{24,28},{28,32},{32,36}... | collective-permute-start | bytes 32 | tf_op jit(solution)/shard_map/ppermute | solution.py:12
  15.2 8.6 %collective-permute-start.1 = (f32[2,256,256]{2,1,0:T(8,128)S(1)}, f32[2,256,256]{2,1,0:T(8,128)S(1)}, u32[]{:S(2)}, u32[]{:S(2)}) collective-permute-start(f32[2,256,256]{2,1,0:T(8,128)S(1)} %pad_dynamic-slice_fusion.2), channel_id=1, source_target_pairs={{4,0},{8,4},{12,8},{16,12},{20,16},{24,20},{28,24},{32,28},{36,32}... | collective-permute-start | bytes 1572872 | tf_op jit(solution)/shard_map/ppermute | solution.py:12
  18.1 5.7 %copy-start.1 = (f32[1,2,256,1024]{3,2,1,0:T(8,128)S(1)}, f32[1,2,256,1024]{3,2,1,0:T(8,128)}, u32[]{:S(2)}) copy-start(f32[1,2,256,1024]{3,2,1,0:T(8,128)} %param.6) | copy-start | bytes 6291460
  24.8 23.0 %copy-start.2 = (f32[2,256,256]{2,1,0:T(8,128)S(1)}, f32[2,256,256]{2,1,0:T(8,128)}, u32[]{:S(2)}) copy-start(f32[2,256,256]{2,1,0:T(8,128)} %param.7) | copy-start | bytes 1572868
  51.3 1.6 %copy-start = (f32[4,2,256,256]{3,2,1,0:T(8,128)S(1)}, f32[4,2,256,256]{3,2,1,0:T(8,128)}, u32[]{:S(2)}) copy-start(f32[4,2,256,256]{3,2,1,0:T(8,128)} %shard_map.64) | copy-start | bytes 6291460
  59.7 1.0 %copy-start.3 = (f32[1,256,256]{2,1,0:T(8,128)S(1)}, f32[1,256,256]{2,1,0:T(8,128)}, u32[]{:S(2)}) copy-start(f32[1,256,256]{2,1,0:T(8,128)} %param.11) | copy-start | bytes 786436
  72.2 13.8 %collective-permute-start.2 = (f32[2,256,256]{2,1,0:T(8,128)S(1)}, f32[2,256,256]{2,1,0:T(8,128)S(1)}, u32[]{:S(2)}, u32[]{:S(2)}) collective-permute-start(f32[2,256,256]{2,1,0:T(8,128)S(1)} %pad_dynamic-slice_fusion.8), channel_id=1, source_target_pairs={{0,4},{4,8},{8,12},{12,16},{16,20},{20,24},{24,28},{28,32},{32,36}... | collective-permute-start | bytes 1572872 | tf_op jit(solution)/shard_map/ppermute | solution.py:12

commit v14 on v13

--- a/solution.py
+++ b/solution.py
@@ -134,8 +134,16 @@
     column_above = offsets_above[1]
 
     strip = transmission[0]
-    lent = jnp.pad(strip, ((0, 0), (width, 0), (0, 0)))
-    lent = lax.dynamic_slice(lent, (zero, row_above, column_above), (2, width, width))
+    pick_rows = (
+        lax.broadcasted_iota(jnp.int32, (width, rows), 1)
+        == lax.broadcasted_iota(jnp.int32, (width, rows), 0) + (row_above - width)
+    ).astype(jnp.float32)
+    pick_columns = (
+        lax.broadcasted_iota(jnp.int32, (columns, width), 0)
+        == lax.broadcasted_iota(jnp.int32, (columns, width), 1) + column_above
+    ).astype(jnp.float32)
+    lent = jnp.einsum("rn,cnk->crk", pick_rows, strip, precision=lax.Precision.HIGHEST)
+    lent = jnp.einsum("crn,nk->crk", lent, pick_columns, precision=lax.Precision.HIGHEST)
     borrowed = shifted(lent, "tile", -1)
     kept = jnp.pad(strip, ((0, 0), (0, width), (0, 0)))
     kept = lax.dynamic_slice(kept, (zero, row, column), (2, width, width))

time: 89.2 us -> 89.3 us (level)
  matrix products: 13.5 us -> 17.6 us
  between operations: 7.15 us -> 3.99 us
  local copies, waits for them, and re-layouts: 5.47 us -> 4.31 us
    dot_general x0 -> x2, matrix products: none -> 4.11 us  [the longest x1 2.91 us: per_device(): jnp.einsum('rn,cnk->crk', pick_rows, strip, precision=lax.Precision.HIGHEST)]
    dynamic_slice x1 -> x0, local copies, waits for them, and re-layouts: 1.16 us -> none  [per_device(): lax.dynamic_slice(lent, (zero, row_above, column_above), (2, width, width))]
where the time goes in v14:
time: 89.3 us; the launch traced here: 88.9 us
  Pallas kernels  22.9 us (26%)
  waiting for transfers between devices  18.1 us (20%)
  matrix products  17.6 us (20%)
  other arithmetic  16.2 us (18%)
  starting transfers between devices  5.75 us (6%)
  local copies, waits for them, and re-layouts  4.31 us (5%)
  between operations  3.99 us (4%)
    pallas_call x1, Pallas kernels, exchange(): pl.pallas_call(exchange_kernel, out_shape=shape, in_specs=[vmem], out_spe...  22.9 us
    ppermute x3, waiting for transfers between devices, shifted(): return lax.ppermute(value, axis, pairs)  18.1 us
    dot_general x14, matrix products, transform(): jnp.einsum('bij,bjk->bik', left, operand, preferred_element_type=jnp.floa...  6.75 us
    dot_general x14, matrix products, transform(): jnp.einsum('bij,bjk->bik', operand, right, preferred_element_type=jnp.flo...  6.74 us
    ppermute x3, starting transfers between devices, shifted(): return lax.ppermute(value, axis, pairs)  5.75 us
    convert_element_type x29, other arithmetic, halves(): return (high.astype(jnp.bfloat16), low.astype(jnp.bfloat16))  4.23 us
    dot_general x1, matrix products, per_device(): jnp.einsum('rn,cnk->crk', pick_rows, strip, precision=lax.Precision.HIGHEST)  2.91 us
    broadcast_in_dim x1, other arithmetic, per_device(): return result[None]  2.57 us
  transfers between devices with their start and end apart: 3, of which 3 were waited for; matrix products, arithmetic and copies ran while one was open for 6% of the time, Pallas kernels for 0%

profile of v14, /device:TPU:128, one launch (start us, length us, event | category | flops | bytes accessed | tf_op | source)
XLA Modules:
  0.0 88.9 jit_solution(1294925329216030322)
XLA Ops:
  1.4 1.9 %collective-permute-start = (s32[2]{0:T(128)S(1)}, s32[2]{0:T(128)S(1)}, u32[]{:S(2)}, u32[]{:S(2)}) collective-permute-start(s32[2]{0:T(128)S(1)} %pad_add_fusion), channel_id=1, source_target_pairs={{0,4},{4,8},{8,12},{12,16},{16,20},{20,24},{24,28},{28,32},{32,36}... | collective-permute-start | bytes 32 | tf_op jit(solution)/shard_map/ppermute | solution.py:12
  3.3 1.1 %multiply_subtract_fusion.12 = (f32[1,256,256]{2,1,0:T(8,128)S(1)}, f32[1,256,256]{2,1,0:T(8,128)S(1)}) fusion(), kind=kLoop, calls=%fused_computation.508 | loop fusion | flops 1179648 | bytes 524288 | tf_op jit(solution)/shard_map/sub | solution.py:38
  4.4 5.2 %collective-permute-done = s32[2]{0:T(128)S(1)} collective-permute-done((s32[2]{0:T(128)S(1)}, s32[2]{0:T(128)S(1)}, u32[]{:S(2)}, u32[]{:S(2)}) %collective-permute-start) | collective-permute-done | bytes 40 | tf_op jit(solution)/shard_map/ppermute | solution.py:12
  9.5 0.6 fusion.379
  10.2 0.6 iota_add_fusion
  11.5 2.9 %fusion.310 = f32[256,2,1024]{2,0,1:T(8,128)S(1)} fusion(s32[256]{0:T(256)S(1)} %iota_add_fusion.1, f32[1,2,256,1024]{3,2,1,0:T(8,128)} %param.6), kind=kOutput, calls=%fused_computation.507 | convolution fusion | flops 1610678272 | bytes 4195328 | tf_op jit(solution)/shard_map/rn,cnk->crk/dot_general | solution.py:145
  14.4 1.2 %fusion.2 = f32[2,256,256]{2,1,0:T(8,128)S(1)} fusion(f32[256,2,1024]{2,0,1:T(8,128)S(1)} %fusion.310, s32[256]{0:T(256)S(1)} %iota_add_fusion), kind=kOutput, calls=%fused_computation.9 | convolution fusion | flops 1610874880 | bytes 2622464 | tf_op jit(solution)/shard_map/crn,nk->crk/dot_general | solution.py:146
  15.6 1.9 %collective-permute-start.1 = (f32[2,256,256]{2,1,0:T(8,128)S(1)}, f32[2,256,256]{2,1,0:T(8,128)S(1)}, u32[]{:S(2)}, u32[]{:S(2)}) collective-permute-start(f32[2,256,256]{2,1,0:T(8,128)S(1)} %fusion.2), channel_id=1, source_target_pairs={{4,0},{8,4},{12,8},{16,12},{20,16},{24,20},{28,24},{32,28},{36,32}... | collective-permute-start | bytes 1572872 | tf_op jit(solution)/shard_map/ppermute | solution.py:12
  17.5 1.0 %cosine_multiply_fusion = f32[1,256,256]{2,1,0:T(8,128)S(1)} fusion(), kind=kLoop, calls=%fused_computation.502 | loop fusion | flops 983040 | bytes 262144 | tf_op jit(solution)/shard_map/mul | solution.py:26
  18.5 1.1 %multiply_subtract_fusion.13 = (f32[1,256,256]{2,1,0:T(8,128)S(1)}, f32[1,256,256]{2,1,0:T(8,128)S(1)}) fusion(), kind=kLoop, calls=%fused_computation.510 | loop fusion | flops 1179648 | bytes 524288 | tf_op jit(solution)/shard_map/sub | solution.py:38
  19.6 0.3 fusion.175
  19.9 2.0 %fusion.378 = (f32[256,256]{1,0:T(8,128)S(1)}, f32[256,256]{1,0:T(8,128)S(1)}) fusion(f32[256,256]{1,0:T(8,128)} %param.8), kind=kLoop, calls=%fused_computation.567 | loop fusion | bytes 786432 | tf_op jit(solution)/shard_map/cos | solution.py:127
  21.9 2.3 %collective-permute-done.1 = f32[2,256,256]{2,1,0:T(8,128)S(1)} collective-permute-done((f32[2,256,256]{2,1,0:T(8,128)S(1)}, f32[2,256,256]{2,1,0:T(8,128)S(1)}, u32[]{:S(2)}, u32[]{:S(2)}) %collective-permute-start.1) | collective-permute-done | bytes 524320 | tf_op jit(solution)/shard_map/ppermute | solution.py:12
  24.2 1.0 %fusion.271.window_ref = f32[2,256,256]{2,1,0:T(8,128)} fusion(f32[2,256,256]{2,1,0:T(8,128)S(1)} %collective-permute-done.1, s32[]{:T(128)S(6)} %select_n.68, s32[]{:T(128)S(6)} %select_n.69, f32[2,256,1024]{2,1,0:T(8,128)S(1)} %bitcast.331), kind=kLoop, calls=%fused_computation.343 | loop fusion | flops 131072 | bytes 3145736 | tf_op jit(solution)/shard_map/add | solution.py:150
  25.2 22.9 %shard_map.64 = f32[4,2,256,256]{3,2,1,0:T(8,128)} custom-call(f32[2,256,256]{2,1,0:T(8,128)} %fusion.271.window_ref), custom_call_target="tpu_custom_call" | custom-call | tf_op jit(solution)/shard_map/pallas_call | solution.py:108
  48.2 1.1 %fusion.375 = (f32[1,256,256]{2,1,0:T(8,128)S(1)}, f32[1,256,256]{2,1,0:T(8,128)S(1)}, f32[1,256,256]{2,1,0:T(8,128)S(1)}) fusion(f32[4,2,256,256]{3,2,1,0:T(8,128)} %shard_map.64, f32[2,256,256]{2,1,0:T(8,128)S(1)} %copy-done.2), kind=kLoop, calls=%fused_computation.566 | loop fusion | flops 458752 | bytes 1835008 | tf_op jit(solution)/shard_map/add | solution.py:48
  49.3 0.1 fusion.263
  49.4 0.5 fusion.4
  50.0 0.1 fusion.181
  50.1 0.5 fusion.10
  50.7 0.1 fusion.261
  50.9 0.5 fusion.16
  51.4 0.1 fusion.185
  51.6 0.5 fusion.22
  52.1 1.1 %copy-done = f32[4,2,256,256]{3,2,1,0:T(8,128)S(1)} copy-done((f32[4,2,256,256]{3,2,1,0:T(8,128)S(1)}, f32[4,2,256,256]{3,2,1,0:T(8,128)}, u32[]{:S(2)}) %copy-start) | copy-done | bytes 2097176
  53.5 0.5 fusion.28
  54.2 0.5 fusion.34
  54.9 0.5 fusion.40
  55.6 0.5 fusion.46
  56.4 0.5 fusion.52
  57.1 0.5 fusion.58
  57.9 0.5 fusion.64
  58.6 0.5 fusion.70
  59.3 0.5 fusion.76
  60.1 0.5 fusion.82
  60.5 0.5 copy-done.3
  61.0 0.2 add_bitcast_fusion.3
  61.4 0.5 fusion.88
  62.1 0.5 fusion.94
  62.9 0.5 fusion.100
  63.5 0.2 fusion.213
  63.6 0.5 fusion.106
  64.3 0.2 fusion.245
  64.4 0.5 fusion.112
  65.0 0.2 fusion.217
  65.1 0.5 fusion.118
  65.7 0.3 fusion.350
  66.1 0.2 fusion.243
  66.2 0.5 fusion.124
  66.8 0.2 fusion.221
  66.9 0.5 fusion.130
  67.6 0.1 fusion.241
  67.7 0.5 fusion.136
  68.3 0.2 fusion.225
  68.4 0.5 fusion.142
  69.2 0.2 fusion.239
  69.3 0.5 fusion.148
  70.0 0.5 fusion.154
  70.8 0.5 fusion.160
  71.5 0.5 fusion.166
  72.3 0.2 fusion.270
  72.5 1.9 %collective-permute-start.2 = (f32[2,256,256]{2,1,0:T(8,128)S(1)}, f32[2,256,256]{2,1,0:T(8,128)S(1)}, u32[]{:S(2)}, u32[]{:S(2)}) collective-permute-start(f32[2,256,256]{2,1,0:T(8,128)S(1)} %pad_dynamic-slice_fusion.7), channel_id=1, source_target_pairs={{0,4},{4,8},{8,12},{12,16},{16,20},{20,24},{24,28},{28,32},{32,36}... | collective-permute-start | bytes 1572872 | tf_op jit(solution)/shard_map/ppermute | solution.py:12
  75.7 10.6 %collective-permute-done.2 = f32[2,256,256]{2,1,0:T(8,128)S(1)} collective-permute-done((f32[2,256,256]{2,1,0:T(8,128)S(1)}, f32[2,256,256]{2,1,0:T(8,128)S(1)}, u32[]{:S(2)}, u32[]{:S(2)}) %collective-permute-start.2) | collective-permute-done | bytes 524320 | tf_op jit(solution)/shard_map/ppermute | solution.py:12
  86.3 2.6 %fusion.1 = f32[1,2,256,1024]{3,2,1,0:T(8,128)} fusion(s32[]{:T(128)S(6)} %select_n.74, f32[2,256,256]{2,1,0:T(8,128)S(1)} %collective-permute-done.2, s32[]{:T(128)S(6)} %select_n.71, s32[]{:T(128)S(6)} %select_n.72, f32[2,256,256]{2,1,0:T(8,128)S(1)} %fusion.270), kind=kLoop, calls=%fused_computation.4 | loop fusion | flops 524288 | bytes 3145740 | tf_op jit(solution)/shard_map/broadcast_in_dim | solution.py:208
  (58 shorter events, 5.1 us)
Async XLA Ops:
  1.4 8.2 %collective-permute-start = (s32[2]{0:T(128)S(1)}, s32[2]{0:T(128)S(1)}, u32[]{:S(2)}, u32[]{:S(2)}) collective-permute-start(s32[2]{0:T(128)S(1)} %pad_add_fusion), channel_id=1, source_target_pairs={{0,4},{4,8},{8,12},{12,16},{16,20},{20,24},{24,28},{28,32},{32,36}... | collective-permute-start | bytes 32 | tf_op jit(solution)/shard_map/ppermute | solution.py:12
  15.6 8.6 %collective-permute-start.1 = (f32[2,256,256]{2,1,0:T(8,128)S(1)}, f32[2,256,256]{2,1,0:T(8,128)S(1)}, u32[]{:S(2)}, u32[]{:S(2)}) collective-permute-start(f32[2,256,256]{2,1,0:T(8,128)S(1)} %fusion.2), channel_id=1, source_target_pairs={{4,0},{8,4},{12,8},{16,12},{20,16},{24,20},{28,24},{32,28},{36,32}... | collective-permute-start | bytes 1572872 | tf_op jit(solution)/shard_map/ppermute | solution.py:12
  18.5 5.7 %copy-start.1 = (f32[1,2,256,1024]{3,2,1,0:T(8,128)S(1)}, f32[1,2,256,1024]{3,2,1,0:T(8,128)}, u32[]{:S(2)}) copy-start(f32[1,2,256,1024]{3,2,1,0:T(8,128)} %param.6) | copy-start | bytes 6291460
  25.2 23.0 %copy-start.2 = (f32[2,256,256]{2,1,0:T(8,128)S(1)}, f32[2,256,256]{2,1,0:T(8,128)}, u32[]{:S(2)}) copy-start(f32[2,256,256]{2,1,0:T(8,128)} %param.7) | copy-start | bytes 1572868
  51.6 1.6 %copy-start = (f32[4,2,256,256]{3,2,1,0:T(8,128)S(1)}, f32[4,2,256,256]{3,2,1,0:T(8,128)}, u32[]{:S(2)}) copy-start(f32[4,2,256,256]{3,2,1,0:T(8,128)} %shard_map.64) | copy-start | bytes 6291460
  60.0 1.0 %copy-start.3 = (f32[1,256,256]{2,1,0:T(8,128)S(1)}, f32[1,256,256]{2,1,0:T(8,128)}, u32[]{:S(2)}) copy-start(f32[1,256,256]{2,1,0:T(8,128)} %param.11) | copy-start | bytes 786436
  72.5 13.8 %collective-permute-start.2 = (f32[2,256,256]{2,1,0:T(8,128)S(1)}, f32[2,256,256]{2,1,0:T(8,128)S(1)}, u32[]{:S(2)}, u32[]{:S(2)}) collective-permute-start(f32[2,256,256]{2,1,0:T(8,128)S(1)} %pad_dynamic-slice_fusion.7), channel_id=1, source_target_pairs={{0,4},{4,8},{8,12},{12,16},{16,20},{20,24},{24,28},{28,32},{32,36}... | collective-permute-start | bytes 1572872 | tf_op jit(solution)/shard_map/ppermute | solution.py:12
